TPU v7x, 512 devices: a whole 4x8x8 slice. The times are simulated.
512 devices in a mesh: section: 8 (over x, core), replica: 64 (over z, y).
Axes of the slice: x: 4, y: 8, z: 8, core: 2. Of those that a mesh axis runs over, the one named last changes fastest.
Arguments:
- pending_section_entries: bfloat16 [8, 128, 14, 14, 512], P('section', 'replica'), may hold values from -40 to 40
- arriving_microsets: bfloat16 [1, 128, 14, 14, 512], P(None, 'replica'), may hold values from -40 to 40
- opening_filter_kernel: bfloat16 [8, 3, 3, 512, 512], P('section'), may hold values from -0.09375 to 0.09375
- closing_filter_kernel: bfloat16 [8, 3, 3, 512, 512], P('section'), may hold values from -0.09375 to 0.09375
- stretch_factors: float32 [8, 2, 512], P('section'), may hold values from 0.5 to 1.5
- shift_terms: float32 [8, 2, 512], P('section'), may hold values from -3 to 3
Outputs:
- produced: bfloat16 [8, 2, 128, 14, 14, 512], P('section', None, 'replica')
All inputs are finite; a program needn't handle non-finite values.
Results may differ from a plain program's by a relative error of at most 0.0084.
Values may be sent and summed in bfloat16 or wider, within the bound.
No kernel may reach another device: no remote copies, remote signals or barrier semaphores. Data moves between devices by JAX's collectives and lax.ppermute only.
A program may use at most 64 MiB of HBM per device.

v0:
```python
import jax
import jax.numpy as jnp
from jax import lax
from jax.sharding import PartitionSpec as P

TICKS = 2


def from_behind(shard, axis, by):
    length = lax.axis_size(axis)
    pairs = [(i, i + by) for i in range(length) if 0 <= i + by < length]
    return lax.ppermute(shard, axis, pairs)


def convolve(maps, kernel):
    return lax.conv_general_dilated(
        maps,
        kernel,
        (1, 1),
        "SAME",
        dimension_numbers=("NHWC", "HWIO", "NHWC"),
        preferred_element_type=jnp.float32,
    )


def batch_statistics(conv_out, replica_total):
    summed = lax.psum(jnp.sum(conv_out, axis=(0, 1, 2)), "replica")
    mean = summed / replica_total
    centred = conv_out - mean
    spread = lax.psum(jnp.sum(centred * centred, axis=(0, 1, 2)), "replica")
    var = spread / replica_total
    return (mean, var)


def coefficients(conv_out, gain, bias, replica_total):
    mean, var = batch_statistics(conv_out, replica_total)
    scale = gain * lax.rsqrt(var + 1e-05)
    return (scale, bias - mean * scale)


def store(conv_out):
    return lax.optimization_barrier(conv_out.astype(jnp.bfloat16))


def normalize(stored, scale, offset):
    return jnp.maximum(stored.astype(jnp.float32) * scale + offset, 0.0).astype(jnp.bfloat16)


def body(
    pending_section_entries,
    arriving_microsets,
    opening_filter_kernel,
    closing_filter_kernel,
    stretch_factors,
    shift_terms,
):
    replica_total = (
        lax.axis_size("replica")
        * pending_section_entries.shape[1]
        * pending_section_entries.shape[2]
        * pending_section_entries.shape[3]
    )
    is_first = lax.axis_index("section") == 0
    first_kernel = opening_filter_kernel[0]
    second_kernel = closing_filter_kernel[0]
    current_feature_map = pending_section_entries[0]
    results = []
    for tick in range(TICKS):
        conv_one = convolve(current_feature_map, first_kernel)
        scale_one, offset_one = coefficients(
            conv_one, stretch_factors[0, 0], shift_terms[0, 0], replica_total
        )
        hidden = normalize(store(conv_one), scale_one, offset_one)
        conv_two = convolve(hidden, second_kernel)
        stored_two = store(conv_two)
        last = tick + 1 == TICKS
        scale_two, offset_two = coefficients(
            conv_two, stretch_factors[0, 1], shift_terms[0, 1], replica_total
        )
        output = normalize(stored_two, scale_two, offset_two)
        if not last:
            moved = from_behind(output, "section", 1)
        results.append(output)
        if not last:
            current_feature_map = jnp.where(is_first, arriving_microsets[tick], moved)
    return jnp.stack(results, axis=0)[None]


def solution(mesh):
    in_specs = (
        P("section", "replica", None, None, None),
        P(None, "replica", None, None, None),
        P("section", None, None, None, None),
        P("section", None, None, None, None),
        P("section", None, None),
        P("section", None, None),
    )
    out_specs = P("section", None, "replica", None, None, None)
    return jax.shard_map(body, mesh=mesh, in_specs=in_specs, out_specs=out_specs, check_vma=False)
```

profile of v0, /device:TPU:10, one launch (start us, length us, event | category | flops | bytes accessed | tf_op | source)
XLA Modules:
  0.0 1161.6 jit_solution(2862424807309763926)
XLA Ops:
  0.0 0.8 fusion.68
  0.8 0.8 fusion.69
  1.5 1.4 pad
  3.2 4.6 select_reduce_fusion.7
  7.8 146.3 %psum.56 = f32[512]{0:T(512)S(1)} all-reduce(f32[512]{0:T(512)S(1)} %get-tuple-element.25), channel_id=1, replica_groups=mesh['section'=8,'replica'=64] {'replica'}, use_global_device_ids=true, to_apply=%region_1.0 | all-reduce | flops 512 | bytes 4096 | tf_op jit(solution)/shard_map/psum | solution.py:27
  154.2 0.2 select_reduce_fusion.6
  154.4 141.9 %psum.57 = f32[512]{0:T(512)S(1)} all-reduce(f32[512]{0:T(512)S(1)} %get-tuple-element.19), channel_id=1, replica_groups=mesh['section'=8,'replica'=64] {'replica'}, use_global_device_ids=true, to_apply=%region_3.0 | all-reduce | flops 512 | bytes 4096 | tf_op jit(solution)/shard_map/psum | solution.py:30
  296.4 0.5 copy.17
  297.8 4.6 select_reduce_fusion.5
  302.4 138.0 %psum.58 = f32[512]{0:T(512)S(1)} all-reduce(f32[512]{0:T(512)S(1)} %get-tuple-element.27), channel_id=1, replica_groups=mesh['section'=8,'replica'=64] {'replica'}, use_global_device_ids=true, to_apply=%region_5.0 | all-reduce | flops 512 | bytes 4096 | tf_op jit(solution)/shard_map/psum | solution.py:27
  440.4 0.2 select_reduce_fusion.4
  440.6 140.0 %psum.59 = f32[512]{0:T(512)S(1)} all-reduce(f32[512]{0:T(512)S(1)} %get-tuple-element.17), channel_id=1, replica_groups=mesh['section'=8,'replica'=64] {'replica'}, use_global_device_ids=true, to_apply=%region_7.0 | all-reduce | flops 512 | bytes 4096 | tf_op jit(solution)/shard_map/psum | solution.py:30
  580.6 0.5 copy.20
  581.5 1.9 collective-permute-start
  583.6 7.7 collective-permute-done
  591.9 4.6 select_reduce_fusion.3
  596.5 138.0 %psum.60 = f32[512]{0:T(512)S(1)} all-reduce(f32[512]{0:T(512)S(1)} %get-tuple-element.29), channel_id=1, replica_groups=mesh['section'=8,'replica'=64] {'replica'}, use_global_device_ids=true, to_apply=%region_9.10 | all-reduce | flops 512 | bytes 4096 | tf_op jit(solution)/shard_map/psum | solution.py:27
  734.7 140.0 %psum.61 = f32[512]{0:T(512)S(1)} all-reduce(f32[512]{0:T(512)S(1)} %get-tuple-element.15), channel_id=1, replica_groups=mesh['section'=8,'replica'=64] {'replica'}, use_global_device_ids=true, to_apply=%region_11.12 | all-reduce | flops 512 | bytes 4096 | tf_op jit(solution)/shard_map/psum | solution.py:30
  874.7 0.5 copy.24
  876.1 4.6 select_reduce_fusion.1
  880.7 138.0 %psum.62 = f32[512]{0:T(512)S(1)} all-reduce(f32[512]{0:T(512)S(1)} %get-tuple-element.31), channel_id=1, replica_groups=mesh['section'=8,'replica'=64] {'replica'}, use_global_device_ids=true, to_apply=%region_13.14 | all-reduce | flops 512 | bytes 4096 | tf_op jit(solution)/shard_map/psum | solution.py:27
  1018.9 140.0 %psum.63 = f32[512]{0:T(512)S(1)} all-reduce(f32[512]{0:T(512)S(1)} %get-tuple-element.13), channel_id=1, replica_groups=mesh['section'=8,'replica'=64] {'replica'}, use_global_device_ids=true, to_apply=%region_15.16 | all-reduce | flops 512 | bytes 4096 | tf_op jit(solution)/shard_map/psum | solution.py:30
  1158.9 0.5 copy.27
  1159.9 1.7 copy.28
  (43 shorter events, 3.9 us)
Async XLA Ops:
  0.0 3.2 copy-start.1
  581.1 10.2 copy-start
  581.5 9.8 collective-permute-start
where the time goes:
time: 1160 us
  blocking collectives  1120 us (97%)
  matrix products  18.6 us (2%)
    psum x4, blocking collectives, batch_statistics(): spread = lax.psum(jnp.sum(centred * centred, axis=(0, 1, 2)), 'replica')  562 us
    psum x4, blocking collectives, batch_statistics(): summed = lax.psum(jnp.sum(conv_out, axis=(0, 1, 2)), 'replica')  560 us
  transfers between devices with their start and end apart: 1, of which 1 were waited for; matrix products, arithmetic and copies ran while one was open for 0% of the time, Pallas kernels for 0%

commit v1 on v0

--- a/solution.py
+++ b/solution.py
@@ -24,12 +24,19 @@
 
 
 def batch_statistics(conv_out, replica_total):
-    summed = lax.psum(jnp.sum(conv_out, axis=(0, 1, 2)), "replica")
-    mean = summed / replica_total
+    members = lax.axis_size("replica")
+    count = replica_total // members
+    mean = jnp.sum(conv_out, axis=(0, 1, 2)) / count
     centred = conv_out - mean
-    spread = lax.psum(jnp.sum(centred * centred, axis=(0, 1, 2)), "replica")
-    var = spread / replica_total
-    return (mean, var)
+    squares = jnp.sum(centred * centred, axis=(0, 1, 2))
+    packed = jnp.concatenate([mean.reshape(4, 128), squares.reshape(4, 128)], axis=0)
+    copies = jnp.broadcast_to(packed, (members, 8, 128))
+    gathered = lax.all_to_all(copies, "replica", 0, 0)
+    means = gathered[:, :4].reshape(members, 512)
+    mean = jnp.sum(means, axis=0) / members
+    apart = means - mean
+    spread = jnp.sum(gathered[:, 4:], axis=0).reshape(512) + count * jnp.sum(apart * apart, axis=0)
+    return (mean, spread / replica_total)
 
 
 def coefficients(conv_out, gain, bias, replica_total):

time: 1160 us -> 127 us (0.11)
  the two profiles are of different devices: /device:TPU:10 before, /device:TPU:2 now
where the time goes in v1:
time: 127 us; the launch traced here: 126 us
  waiting for transfers between devices  61.8 us (49%)
  starting transfers between devices  32.6 us (26%)
  matrix products  18.6 us (15%)
  local copies, waits for them, and re-layouts  10.5 us (8%)
  other arithmetic  2.52 us (2%)
    all_to_all x4, waiting for transfers between devices, batch_statistics(): gathered = lax.all_to_all(copies, 'replica', 0, 0)  53.9 us
    all_to_all x4, starting transfers between devices, batch_statistics(): gathered = lax.all_to_all(copies, 'replica', 0, 0)  30.6 us
    conv_general_dilated x4, matrix products, convolve(): lax.conv_general_dilated(maps, kernel, (1, 1), 'SAME', dimension_numbers=...  18.6 us
    ppermute x1, waiting for transfers between devices, from_behind(): return lax.ppermute(shard, axis, pairs)  7.86 us
    broadcast_in_dim x4, local copies, waits for them, and re-layouts, batch_statistics(): copies = jnp.broadcast_to(packed, (members, 8, 128))  2.9 us
    convert_element_type x12, local copies, waits for them, and re-layouts, store(): return lax.optimization_barrier(conv_out.astype(jnp.bfloat16))  2.73 us
  transfers between devices with their start and end apart: 5, of which 5 were waited for; matrix products, arithmetic and copies ran while one was open for 2% of the time, Pallas kernels for 0%

profile of v1, /device:TPU:2, one launch (start us, length us, event | category | flops | bytes accessed | tf_op | source)
XLA Modules:
  0.0 126.4 jit_solution(5103421289084374399)
XLA Ops:
  0.0 1.4 %pad = bf16[14,2,16,512]{3,1,2,0:T(2,128)(2,1)S(1)} pad(bf16[14,2,14,512]{3,1,2,0:T(2,128)(2,1)} %bitcast.125, bf16[]{:T(256)} %constant.38), padding=0_0x0_0x1_1x0_0 | pad | bytes 860162 | tf_op jit(solution)/shard_map/squeeze | solution.py:73
  1.7 4.6 %select_reduce_fusion.7 = (f32[512]{0:T(512)S(1)}, f32[14,16,2,512]{3,1,2,0:T(8,128)S(1)}) fusion(pred[16,2]{0,1:T(4,128)(4,1)S(1)} %copy-done.1, bf16[1,3,3,512,512]{4,3,2,1,0:T(8,128)(2,1)} %param.8, bf16[14,2,7,2,512]{4,2,1,3,0:T(8,128)(2,1)S(1)} %slice.60, bf16[14,2,8,2,512]{4,2,1,3,0:T(8,128)(2,1)S(1)} %copy.44), kind=kOutput, calls=%fused_computation.45 | convolution fusion | flops 2016706048 | bytes 6498336 | tf_op jit(solution)/shard_map/conv_general_dilated | solution.py:16
  6.6 0.7 broadcast_in_dim.10
  7.3 16.6 %all-to-all-start = ((f32[64,8,128]{2,1,0:T(8,128)}), f32[64,8,128]{2,1,0:T(8,128)S(1)}, u32[]{:S(2)}, u32[]{:S(2)}) async-start(f32[64,8,128]{2,1,0:T(8,128)} %broadcast_in_dim.10), calls=%async_computation | async-start | bytes 524288 | tf_op jit(solution)/shard_map/all_to_all | solution.py:34
  23.9 0.5 copy.45
  24.6 14.2 %all-to-all-done = f32[64,8,128]{2,1,0:T(8,128)S(1)} async-done(((f32[64,8,128]{2,1,0:T(8,128)}), f32[64,8,128]{2,1,0:T(8,128)S(1)}, u32[]{:S(2)}, u32[]{:S(2)}) %all-to-all-start) | async-done | bytes 262176 | tf_op jit(solution)/shard_map/all_to_all | solution.py:34
  39.7 4.6 %select_reduce_fusion.5 = (f32[512]{0:T(512)S(1)}, f32[14,16,2,512]{3,1,2,0:T(8,128)S(1)}) fusion(pred[16,2]{0,1:T(4,128)(4,1)S(1)} %copy-done.1, bf16[1,3,3,512,512]{4,3,2,1,0:T(8,128)(2,1)} %param.9, bf16[14,2,7,2,512]{4,2,1,3,0:T(8,128)(2,1)S(1)} %slice.64, bf16[14,2,8,2,512]{4,2,1,3,0:T(8,128)(2,1)S(1)} %copy.50), kind=kOutput, calls=%fused_computation.43 | convolution fusion | flops 2016706048 | bytes 6498336 | tf_op jit(solution)/shard_map/conv_general_dilated | solution.py:16
  44.6 0.7 broadcast_in_dim.11
  45.3 4.6 %all-to-all-start.1 = ((f32[64,8,128]{2,1,0:T(8,128)}), f32[64,8,128]{2,1,0:T(8,128)S(1)}, u32[]{:S(2)}, u32[]{:S(2)}) async-start(f32[64,8,128]{2,1,0:T(8,128)} %broadcast_in_dim.11), calls=%async_computation.1 | async-start | bytes 524288 | tf_op jit(solution)/shard_map/all_to_all | solution.py:34
  49.9 0.5 copy.51
  50.6 13.2 %all-to-all-done.1 = f32[64,8,128]{2,1,0:T(8,128)S(1)} async-done(((f32[64,8,128]{2,1,0:T(8,128)}), f32[64,8,128]{2,1,0:T(8,128)S(1)}, u32[]{:S(2)}, u32[]{:S(2)}) %all-to-all-start.1) | async-done | bytes 262176 | tf_op jit(solution)/shard_map/all_to_all | solution.py:34
  64.2 1.9 %collective-permute-start = (bf16[2,14,14,512]{3,2,0,1:T(8,128)(2,1)S(1)}, bf16[2,14,14,512]{3,2,0,1:T(8,128)(2,1)S(1)}, u32[]{:S(2)}, u32[]{:S(2)}) collective-permute-start(bf16[2,14,14,512]{3,2,0,1:T(8,128)(2,1)S(1)} %maximum_convert_fusion.2), channel_id=1, source_target_pairs={{0,64},{64,128},{128,192},{192,256},{256,320},{320,384},{384,448},... | collective-permute-start | bytes 1204232 | tf_op jit(solution)/shard_map/ppermute | solution.py:12
  66.1 7.9 %collective-permute-done = bf16[2,14,14,512]{3,2,0,1:T(8,128)(2,1)S(1)} collective-permute-done((bf16[2,14,14,512]{3,2,0,1:T(8,128)(2,1)S(1)}, bf16[2,14,14,512]{3,2,0,1:T(8,128)(2,1)S(1)}, u32[]{:S(2)}, u32[]{:S(2)}) %collective-permute-start) | collective-permute-done | bytes 401440 | tf_op jit(solution)/shard_map/ppermute | solution.py:12
  74.6 4.6 %select_reduce_fusion.3 = (f32[512]{0:T(512)S(1)}, f32[14,16,2,512]{3,1,2,0:T(8,128)S(1)}) fusion(pred[16,2]{0,1:T(4,128)(4,1)S(1)} %copy-done.1, bf16[1,3,3,512,512]{4,3,2,1,0:T(8,128)(2,1)} %param.8, bf16[14,2,7,2,512]{4,2,1,3,0:T(8,128)(2,1)S(1)} %slice.68, bf16[14,2,8,2,512]{4,2,1,3,0:T(8,128)(2,1)S(1)} %copy.57), kind=kOutput, calls=%fused_computation.41 | convolution fusion | flops 2016706048 | bytes 6498336 | tf_op jit(solution)/shard_map/conv_general_dilated | solution.py:16
  79.5 0.7 broadcast_in_dim.12
  80.2 4.8 %all-to-all-start.2 = ((f32[64,8,128]{2,1,0:T(8,128)}), f32[64,8,128]{2,1,0:T(8,128)S(1)}, u32[]{:S(2)}, u32[]{:S(2)}) async-start(f32[64,8,128]{2,1,0:T(8,128)} %broadcast_in_dim.12), calls=%async_computation.2 | async-start | bytes 524288 | tf_op jit(solution)/shard_map/all_to_all | solution.py:34
  85.0 0.5 copy.58
  85.7 13.6 %all-to-all-done.2 = f32[64,8,128]{2,1,0:T(8,128)S(1)} async-done(((f32[64,8,128]{2,1,0:T(8,128)}), f32[64,8,128]{2,1,0:T(8,128)S(1)}, u32[]{:S(2)}, u32[]{:S(2)}) %all-to-all-start.2) | async-done | bytes 262176 | tf_op jit(solution)/shard_map/all_to_all | solution.py:34
  100.2 4.6 %select_reduce_fusion.1 = (f32[512]{0:T(512)S(1)}, f32[14,16,2,512]{3,1,2,0:T(8,128)S(1)}) fusion(pred[16,2]{0,1:T(4,128)(4,1)S(1)} %copy-done.1, bf16[1,3,3,512,512]{4,3,2,1,0:T(8,128)(2,1)} %param.9, bf16[14,2,7,2,512]{4,2,1,3,0:T(8,128)(2,1)S(1)} %slice.72, bf16[14,2,8,2,512]{4,2,1,3,0:T(8,128)(2,1)S(1)} %copy.63), kind=kOutput, calls=%fused_computation.39 | convolution fusion | flops 2016706048 | bytes 6498336 | tf_op jit(solution)/shard_map/conv_general_dilated | solution.py:16
  105.1 0.7 broadcast_in_dim.13
  105.8 4.6 %all-to-all-start.3 = ((f32[64,8,128]{2,1,0:T(8,128)}), f32[64,8,128]{2,1,0:T(8,128)S(1)}, u32[]{:S(2)}, u32[]{:S(2)}) async-start(f32[64,8,128]{2,1,0:T(8,128)} %broadcast_in_dim.13), calls=%async_computation.3 | async-start | bytes 524288 | tf_op jit(solution)/shard_map/all_to_all | solution.py:34
  110.6 0.5 copy.64
  111.3 12.9 %all-to-all-done.3 = f32[64,8,128]{2,1,0:T(8,128)S(1)} async-done(((f32[64,8,128]{2,1,0:T(8,128)}), f32[64,8,128]{2,1,0:T(8,128)S(1)}, u32[]{:S(2)}, u32[]{:S(2)}) %all-to-all-start.3) | async-done | bytes 262176 | tf_op jit(solution)/shard_map/all_to_all | solution.py:34
  124.7 1.7 %copy.68 = bf16[1,2,2,14,14,512]{5,2,4,3,1,0:T(2,128)(2,1)} copy(bf16[1,2,2,14,14,512]{5,4,2,3,1,0:T(8,128)(2,1)S(1)} %maximum_bitcast_fusion) | data formatting | bytes 1605632 | tf_op jit(solution)/shard_map/broadcast_in_dim | solution.py:93
  (67 shorter events, 5.1 us)
Async XLA Ops:
  0.0 1.7 %copy-start.1 = (pred[16,2]{0,1:T(4,128)(4,1)S(1)}, pred[16,2]{0,1:T(4,128)(4,1)}, u32[]{:S(2)}) copy-start(pred[16,2]{0,1:T(4,128)(4,1)} %constant.62) | copy-start | bytes 100
  6.5 18.1 %copy-start.2 = (f32[1,2,512]{2,1,0:T(2,128)S(1)}, f32[1,2,512]{2,1,0:T(2,128)}, u32[]{:S(2)}) copy-start(f32[1,2,512]{2,1,0:T(2,128)} %param.10) | copy-start | bytes 12292
  6.6 18.1 %copy-start.3 = (f32[1,2,512]{2,1,0:T(2,128)S(1)}, f32[1,2,512]{2,1,0:T(2,128)}, u32[]{:S(2)}) copy-start(f32[1,2,512]{2,1,0:T(2,128)} %param.11) | copy-start | bytes 12292
  7.3 31.5 %all-to-all-start = ((f32[64,8,128]{2,1,0:T(8,128)}), f32[64,8,128]{2,1,0:T(8,128)S(1)}, u32[]{:S(2)}, u32[]{:S(2)}) async-start(f32[64,8,128]{2,1,0:T(8,128)} %broadcast_in_dim.10), calls=%async_computation | async-start | bytes 524288 | tf_op jit(solution)/shard_map/all_to_all | solution.py:34
  45.3 18.6 %all-to-all-start.1 = ((f32[64,8,128]{2,1,0:T(8,128)}), f32[64,8,128]{2,1,0:T(8,128)S(1)}, u32[]{:S(2)}, u32[]{:S(2)}) async-start(f32[64,8,128]{2,1,0:T(8,128)} %broadcast_in_dim.11), calls=%async_computation.1 | async-start | bytes 524288 | tf_op jit(solution)/shard_map/all_to_all | solution.py:34
  49.9 24.1 %copy-start = (bf16[1,2,14,14,512]{4,1,3,2,0:T(2,128)(2,1)S(1)}, bf16[1,2,14,14,512]{4,1,3,2,0:T(2,128)(2,1)}, u32[]{:S(2)}) copy-start(bf16[1,2,14,14,512]{4,1,3,2,0:T(2,128)(2,1)} %param.7) | copy-start | bytes 1204228
  64.2 9.8 %collective-permute-start = (bf16[2,14,14,512]{3,2,0,1:T(8,128)(2,1)S(1)}, bf16[2,14,14,512]{3,2,0,1:T(8,128)(2,1)S(1)}, u32[]{:S(2)}, u32[]{:S(2)}) collective-permute-start(bf16[2,14,14,512]{3,2,0,1:T(8,128)(2,1)S(1)} %maximum_convert_fusion.2), channel_id=1, source_target_pairs={{0,64},{64,128},{128,192},{192,256},{256,320},{320,384},{384,448},... | collective-permute-start | bytes 1204232 | tf_op jit(solution)/shard_map/ppermute | solution.py:12
  80.2 19.1 %all-to-all-start.2 = ((f32[64,8,128]{2,1,0:T(8,128)}), f32[64,8,128]{2,1,0:T(8,128)S(1)}, u32[]{:S(2)}, u32[]{:S(2)}) async-start(f32[64,8,128]{2,1,0:T(8,128)} %broadcast_in_dim.12), calls=%async_computation.2 | async-start | bytes 524288 | tf_op jit(solution)/shard_map/all_to_all | solution.py:34
  105.8 18.4 %all-to-all-start.3 = ((f32[64,8,128]{2,1,0:T(8,128)}), f32[64,8,128]{2,1,0:T(8,128)S(1)}, u32[]{:S(2)}, u32[]{:S(2)}) async-start(f32[64,8,128]{2,1,0:T(8,128)} %broadcast_in_dim.13), calls=%async_computation.3 | async-start | bytes 524288 | tf_op jit(solution)/shard_map/all_to_all | solution.py:34

commit v2 on v0

v2 whole, which is shorter than its diff:
```python
import jax
import jax.numpy as jnp
from jax import lax
from jax.experimental import pallas as pl
from jax.experimental.pallas import tpu as pltpu
from jax.sharding import PartitionSpec as P

TICKS = 2
LANES = 128
EPS = 1e-05


class Plan:
    def __init__(self, images, height, width, channels, members):
        self.images, self.height, self.width, self.channels = images, height, width, channels
        self.members = members
        self.wide = 16
        self.line = self.wide * images
        self.rows = height * self.line
        self.groups = channels // LANES
        self.count = images * height * width

    def real_rows(self):
        row = lax.broadcasted_iota(jnp.int32, (self.rows, LANES), 0)
        return row % self.line < self.width * self.images


def fill_shifted(plan, padded):
    line, rows, step = plan.line, plan.rows, plan.images
    padded[0, pl.ds(line, rows), :] = padded[1, pl.ds(line - step, rows), :]
    padded[2, pl.ds(line, rows), :] = padded[1, pl.ds(line + step, rows), :]


def zero_borders(plan, padded):
    border = jnp.zeros((plan.line, plan.channels), jnp.bfloat16)
    for shift in range(3):
        padded[shift, pl.ds(0, plan.line), :] = border
        padded[shift, pl.ds(plan.line + plan.rows, plan.line), :] = border


def convolve_and_measure(plan, padded, tap, stored_ref, packed_ref):
    pieces, filters = [], []
    for kh in range(3):
        for kw in range(3):
            pieces.append(padded[kw, pl.ds(kh * plan.line, plan.rows), :])
            filters.append(tap(kh, kw))
    conv_out = jnp.dot(
        jnp.concatenate(pieces, axis=1),
        jnp.concatenate(filters, axis=0),
        preferred_element_type=jnp.float32,
    )
    stored_ref[...] = conv_out.astype(jnp.bfloat16)
    real = plan.real_rows()
    means, squares = [], []
    for group in range(plan.groups):
        values = jnp.where(real, conv_out[:, group * LANES : (group + 1) * LANES], 0.0)
        mean = jnp.sum(values, axis=0, keepdims=True) / plan.count
        centred = jnp.where(real, values - mean, 0.0)
        means.append(mean)
        squares.append(jnp.sum(centred * centred, axis=0, keepdims=True))
    packed = jnp.concatenate(means + squares, axis=0)
    packed_ref[...] = jnp.broadcast_to(packed[None], packed_ref.shape)


def join(plan, gathered, gain, bias):
    groups = plan.groups
    means = gathered[:, :groups, :]
    mean = jnp.sum(means, axis=0) / plan.members
    apart = means - mean[None]
    spread = jnp.sum(gathered[:, groups:, :], axis=0) + plan.count * jnp.sum(apart * apart, axis=0)
    scale = gain * lax.rsqrt(spread / (plan.count * plan.members) + EPS)
    return scale, bias - mean * scale


def normalize_into(plan, stored_ref, scale, offset, write):
    real = plan.real_rows()
    for group in range(plan.groups):
        lanes = slice(group * LANES, (group + 1) * LANES)
        values = stored_ref[:, lanes].astype(jnp.float32) * scale[group : group + 1] + offset[group : group + 1]
        write(lanes, jnp.where(real, jnp.maximum(values, 0.0), 0.0).astype(jnp.bfloat16))


def start_filters(kernel_hbm, kernel_vmem, sems):
    copies = {}
    for kh in range(3):
        for kw in range(3):
            copy = pltpu.make_async_copy(kernel_hbm.at[kh, kw], kernel_vmem.at[kh, kw], sems.at[kh, kw])
            copy.start()
            copies[kh, kw] = copy

    def tap(kh, kw):
        copies[kh, kw].wait()
        return kernel_vmem[kh, kw]

    return tap


def conv_layer(plan, body, operands, kernel):
    whole = pl.BlockSpec(memory_space=pltpu.VMEM)

    def run(*refs):
        ins = refs[: len(operands)]
        kernel_hbm, stored_ref, packed_ref, padded, kernel_vmem, sems = refs[len(operands) :]
        tap = start_filters(kernel_hbm, kernel_vmem, sems)
        zero_borders(plan, padded)
        body(padded, *ins)
        fill_shifted(plan, padded)
        convolve_and_measure(plan, padded, tap, stored_ref, packed_ref)

    channels = plan.channels
    return pl.pallas_call(
        run,
        in_specs=[whole] * len(operands) + [pl.BlockSpec(memory_space=pltpu.HBM)],
        out_specs=[whole, whole],
        out_shape=[
            jax.ShapeDtypeStruct((plan.rows, channels), jnp.bfloat16),
            jax.ShapeDtypeStruct((plan.members, 2 * plan.groups, LANES), jnp.float32),
        ],
        scratch_shapes=[
            pltpu.VMEM((3, plan.rows + 2 * plan.line, channels), jnp.bfloat16),
            pltpu.VMEM((3, 3, channels, channels), jnp.bfloat16),
            pltpu.SemaphoreType.DMA((3, 3)),
        ],
        compiler_params=pltpu.CompilerParams(vmem_limit_bytes=32 << 20),
    )(*operands, kernel)


def inner(plan):
    return pl.ds(plan.line, plan.rows)


def layer_of_map(plan, rows, kernel):
    def body(padded, rows_ref):
        padded[1, inner(plan), :] = rows_ref[...]

    return conv_layer(plan, body, [rows], kernel)


def layer_of_stored(plan, stored, gathered, gain, bias, kernel):
    def body(padded, stored_ref, gathered_ref, gain_ref, bias_ref):
        scale, offset = join(plan, gathered_ref[...], gain_ref[...], bias_ref[...])

        def write(lanes, values):
            padded[1, inner(plan), lanes] = values

        normalize_into(plan, stored_ref, scale, offset, write)

    return conv_layer(plan, body, [stored, gathered, gain, bias], kernel)


def layer_of_moved(plan, stored, coefficients, rows, is_first, kernel):
    def body(padded, stored_ref, coefficients_ref, rows_ref, first_ref):
        first = jnp.broadcast_to(first_ref[...], (plan.rows, LANES)) > 0.5

        def write(lanes, values):
            padded[1, inner(plan), lanes] = jnp.where(first, rows_ref[:, lanes], values)

        both = coefficients_ref[...]
        normalize_into(plan, stored_ref, both[: plan.groups], both[plan.groups :], write)

    return conv_layer(plan, body, [stored, coefficients, rows, is_first], kernel)


def finish(plan, stored, scale, offset):
    whole = pl.BlockSpec(memory_space=pltpu.VMEM)

    def run(stored_ref, scale_ref, offset_ref, out_ref):
        def write(lanes, values):
            out_ref[:, lanes] = values

        normalize_into(plan, stored_ref, scale_ref[...], offset_ref[...], write)

    return pl.pallas_call(
        run,
        in_specs=[whole] * 3,
        out_specs=whole,
        out_shape=jax.ShapeDtypeStruct(stored.shape, stored.dtype),
    )(stored, scale, offset)


def to_rows(plan, maps):
    rows = jnp.transpose(maps, (1, 2, 0, 3))
    rows = jnp.pad(rows, ((0, 0), (0, plan.wide - plan.width), (0, 0), (0, 0)))
    return rows.reshape(plan.rows, plan.channels)


def to_maps(plan, rows):
    maps = rows.reshape(plan.height, plan.wide, plan.images, plan.channels)[:, : plan.width]
    return jnp.transpose(maps, (2, 0, 1, 3))


def from_behind(value, axis):
    pairs = [(i, i + 1) for i in range(lax.axis_size(axis) - 1)]
    return lax.ppermute(value, axis, pairs)


def exchange(copies):
    return lax.all_to_all(copies, "replica", 0, 0)


def body(
    pending_section_entries,
    arriving_microsets,
    opening_filter_kernel,
    closing_filter_kernel,
    stretch_factors,
    shift_terms,
):
    _, images, height, width, channels = pending_section_entries.shape
    plan = Plan(images, height, width, channels, lax.axis_size("replica"))
    first_kernel = opening_filter_kernel[0]
    second_kernel = closing_filter_kernel[0]
    gain = stretch_factors[0].reshape(2, plan.groups, LANES)
    bias = shift_terms[0].reshape(2, plan.groups, LANES)
    is_first = jnp.broadcast_to((lax.axis_index("section") == 0).astype(jnp.float32), (1, LANES))
    stored, packed = layer_of_map(plan, to_rows(plan, pending_section_entries[0]), first_kernel)
    results = []
    for tick in range(TICKS):
        stored, packed = layer_of_stored(plan, stored, exchange(packed), gain[0], bias[0], second_kernel)
        last = tick + 1 == TICKS
        if not last:
            moved = from_behind(stored, "section")
        scale, offset = join(plan, exchange(packed), gain[1], bias[1])
        if not last:
            coefficients = from_behind(jnp.concatenate([scale, offset], axis=0), "section")
        results.append(to_maps(plan, finish(plan, stored, scale, offset)))
        if not last:
            rows = to_rows(plan, arriving_microsets[tick])
            stored, packed = layer_of_moved(plan, moved, coefficients, rows, is_first, first_kernel)
    return jnp.stack(results, axis=0)[None]


def solution(mesh):
    in_specs = (
        P("section", "replica", None, None, None),
        P(None, "replica", None, None, None),
        P("section", None, None, None, None),
        P("section", None, None, None, None),
        P("section", None, None),
        P("section", None, None),
    )
    out_specs = P("section", None, "replica", None, None, None)
    return jax.shard_map(body, mesh=mesh, in_specs=in_specs, out_specs=out_specs, check_vma=False)
```

time: 1160 us -> 129 us (0.11)
  the two profiles are of different devices: /device:TPU:10 before, /device:TPU:1 now
where the time goes in v2:
time: 129 us; the launch traced here: 128 us
  starting transfers between devices  39.2 us (30%)
  waiting for transfers between devices  31.7 us (25%)
  Pallas kernels  21 us (16%)
  blocking collectives  17.8 us (14%)
  local copies, waits for them, and re-layouts  15.3 us (12%)
  other arithmetic  2.99 us (2%)
    all_to_all x3, waiting for transfers between devices, exchange(): return lax.all_to_all(copies, 'replica', 0, 0)  31.6 us
    all_to_all x3, starting transfers between devices, exchange(): return lax.all_to_all(copies, 'replica', 0, 0)  27.8 us
    all_to_all x1, blocking collectives, exchange(): return lax.all_to_all(copies, 'replica', 0, 0)  17.8 us
    pallas_call x4, Pallas kernels, conv_layer(): pl.pallas_call(run, in_specs=[whole] * len(operands) + [pl.BlockSpec(memo...  17.1 us
    ppermute x2, starting transfers between devices, from_behind(): return lax.ppermute(value, axis, pairs)  11.4 us
    unnamed x22, local copies, waits for them, and re-layouts  10.1 us
    pallas_call x2, Pallas kernels, finish(): pl.pallas_call(run, in_specs=[whole] * 3, out_specs=whole, out_shape=jax....  3.95 us
  transfers between devices with their start and end apart: 5, of which 4 were waited for; matrix products, arithmetic and copies ran while one was open for 2% of the time, Pallas kernels for 2%

profile of v2, /device:TPU:1, one launch (start us, length us, event | category | flops | bytes accessed | tf_op | source)
XLA Modules:
  0.0 128.3 jit_solution(9122837812266809251)
XLA Ops:
  0.0 1.4 %pad.7 = bf16[14,16,2,512]{3,2,1,0:T(2,128)(2,1)S(1)} pad(bf16[14,14,2,512]{3,2,1,0:T(2,128)(2,1)} %bitcast.30, bf16[]{:T(256)} %constant.7.clone.1), padding=0_0x0_2x0_0x0_0 | pad | bytes 860162 | tf_op jit(solution)/shard_map/jit(_pad)/pad | solution.py:183
  1.6 2.3 %copy-done = bf16[1,3,3,512,512]{4,3,2,1,0:T(8,128)(2,1)S(1)} copy-done((bf16[1,3,3,512,512]{4,3,2,1,0:T(8,128)(2,1)S(1)}, bf16[1,3,3,512,512]{4,3,2,1,0:T(8,128)(2,1)}, u32[]{:S(2)}) %copy-start) | copy-done | bytes 4718616
  4.0 4.2 %shard_map.64 = (bf16[448,512]{1,0:T(8,128)(2,1)S(1)}, f32[64,8,128]{2,1,0:T(8,128)}) custom-call(bf16[448,512]{1,0:T(8,128)(2,1)S(1)} %reshape.26.refs_0_, bf16[3,3,512,512]{3,2,1,0:T(8,128)(2,1)S(1)} %bitcast.22), custom_call_target="tpu_custom_call" | custom-call | tf_op jit(solution)/shard_map/pallas_call | solution.py:111
  8.2 17.3 %all-to-all-start = ((f32[64,8,128]{2,1,0:T(8,128)}), f32[64,8,128]{2,1,0:T(8,128)S(1)}, u32[]{:S(2)}, u32[]{:S(2)}) async-start(f32[64,8,128]{2,1,0:T(8,128)} %get-tuple-element.14), calls=%async_computation | async-start | bytes 524288 | tf_op jit(solution)/shard_map/all_to_all | solution.py:198
  25.6 12.6 %all-to-all-done.refs_1_ = f32[64,8,128]{2,1,0:T(8,128)S(1)} async-done(((f32[64,8,128]{2,1,0:T(8,128)}), f32[64,8,128]{2,1,0:T(8,128)S(1)}, u32[]{:S(2)}, u32[]{:S(2)}) %all-to-all-start) | async-done | bytes 262176 | tf_op jit(solution)/shard_map/all_to_all | solution.py:198
  38.2 2.3 %copy-done.2 = bf16[1,3,3,512,512]{4,3,2,1,0:T(8,128)(2,1)S(1)} copy-done((bf16[1,3,3,512,512]{4,3,2,1,0:T(8,128)(2,1)S(1)}, bf16[1,3,3,512,512]{4,3,2,1,0:T(8,128)(2,1)}, u32[]{:S(2)}) %copy-start.2) | copy-done | bytes 4718616
  40.5 4.5 %shard_map.65 = (bf16[448,512]{1,0:T(8,128)(2,1)S(1)}, f32[64,8,128]{2,1,0:T(8,128)}) custom-call(bf16[448,512]{1,0:T(8,128)(2,1)S(1)} %get-tuple-element.13.refs_0_, f32[64,8,128]{2,1,0:T(8,128)S(1)} %all-to-all-done.refs_1_, f32[4,128]{1,0:T(4,128)S(1)} %bitcast.26, f32[4,128]{1,0:T(4,128)S(1)} %bitcast.28, bf16[3,3,512,512]{3,2,1,0:T(8,128)(2,1)S(1)} %bitcast.24), custom_call_target="tpu_custom_call" | custom-call | tf_op jit(solution)/shard_map/pallas_call | solution.py:111
  45.1 5.9 %all-to-all-start.1 = ((f32[64,8,128]{2,1,0:T(8,128)}), f32[64,8,128]{2,1,0:T(8,128)S(1)}, u32[]{:S(2)}, u32[]{:S(2)}) async-start(f32[64,8,128]{2,1,0:T(8,128)} %get-tuple-element.16), calls=%async_computation.1 | async-start | bytes 524288 | tf_op jit(solution)/shard_map/all_to_all | solution.py:198
  50.9 5.0 %collective-permute-start = (bf16[448,512]{1,0:T(8,128)(2,1)S(1)}, bf16[448,512]{1,0:T(8,128)(2,1)S(1)}, u32[]{:S(2)}, u32[]{:S(2)}) collective-permute-start(bf16[448,512]{1,0:T(8,128)(2,1)S(1)} %get-tuple-element.15.stored_ref), channel_id=1, source_target_pairs={{0,64},{64,128},{128,192},{192,256},{256,320},{320,384},{384,448},... | collective-permute-start | bytes 1376264 | tf_op jit(solution)/shard_map/ppermute | solution.py:194
  55.9 7.5 %all-to-all-done.1 = f32[64,8,128]{2,1,0:T(8,128)S(1)} async-done(((f32[64,8,128]{2,1,0:T(8,128)}), f32[64,8,128]{2,1,0:T(8,128)S(1)}, u32[]{:S(2)}, u32[]{:S(2)}) %all-to-all-start.1) | async-done | bytes 262176 | tf_op jit(solution)/shard_map/all_to_all | solution.py:198
  63.7 6.4 %collective-permute-start.1 = (f32[8,128]{1,0:T(8,128)S(1)}, f32[8,128]{1,0:T(8,128)S(1)}, u32[]{:S(2)}, u32[]{:S(2)}) collective-permute-start(f32[8,128]{1,0:T(8,128)S(1)} %pad_maximum_fusion), channel_id=1, source_target_pairs={{0,64},{64,128},{128,192},{192,256},{256,320},{320,384},{384,448},... | collective-permute-start | bytes 12296 | tf_op jit(solution)/shard_map/ppermute | solution.py:194
  70.8 2.3 %copy-done.1 = bf16[1,3,3,512,512]{4,3,2,1,0:T(8,128)(2,1)S(1)} copy-done((bf16[1,3,3,512,512]{4,3,2,1,0:T(8,128)(2,1)S(1)}, bf16[1,3,3,512,512]{4,3,2,1,0:T(8,128)(2,1)}, u32[]{:S(2)}) %copy-start.1) | copy-done | bytes 4718616
  73.2 3.8 %shard_map.67 = (bf16[448,512]{1,0:T(8,128)(2,1)S(1)}, f32[64,8,128]{2,1,0:T(8,128)S(1)}) custom-call(bf16[448,512]{1,0:T(8,128)(2,1)S(1)} %collective-permute-done.refs_0_, f32[8,128]{1,0:T(8,128)S(1)} %collective-permute-done.1.refs_1_, bf16[448,512]{1,0:T(8,128)(2,1)S(1)} %reshape.28.refs_2_, f32[1,128]{1,0:T(1,128)S(1)} %broadcast_in_dim.8.refs_3_, ...), custom_call_target="tpu_custom_call" | custom-call | tf_op jit(solution)/shard_map/pallas_call | solution.py:111
  77.0 17.8 %all_to_all.20.refs_1_ = f32[64,8,128]{2,1,0:T(8,128)S(1)} all-to-all(f32[64,8,128]{2,1,0:T(8,128)S(1)} %get-tuple-element.18), channel_id=1, replica_groups=mesh['section'=8,'replica'=64] {'replica'}, dimensions={0} | all-to-all | bytes 524288 | tf_op jit(solution)/shard_map/all_to_all | solution.py:198
  94.8 2.3 %copy-done.3 = bf16[1,3,3,512,512]{4,3,2,1,0:T(8,128)(2,1)S(1)} copy-done((bf16[1,3,3,512,512]{4,3,2,1,0:T(8,128)(2,1)S(1)}, bf16[1,3,3,512,512]{4,3,2,1,0:T(8,128)(2,1)}, u32[]{:S(2)}) %copy-start.3) | copy-done | bytes 4718616
  97.1 4.5 %shard_map.68 = (bf16[448,512]{1,0:T(8,128)(2,1)S(1)}, f32[64,8,128]{2,1,0:T(8,128)}) custom-call(bf16[448,512]{1,0:T(8,128)(2,1)S(1)} %get-tuple-element.17.refs_0_, f32[64,8,128]{2,1,0:T(8,128)S(1)} %all_to_all.20.refs_1_, f32[4,128]{1,0:T(4,128)S(1)} %bitcast.27, f32[4,128]{1,0:T(4,128)S(1)} %bitcast.29, bf16[3,3,512,512]{3,2,1,0:T(8,128)(2,1)S(1)} %bitcast.25), custom_call_target="tpu_custom_call" | custom-call | tf_op jit(solution)/shard_map/pallas_call | solution.py:111
  101.7 0.8 copy-done.5
  102.5 4.6 %all-to-all-start.3 = ((f32[64,8,128]{2,1,0:T(8,128)}), f32[64,8,128]{2,1,0:T(8,128)S(1)}, u32[]{:S(2)}, u32[]{:S(2)}) async-start(f32[64,8,128]{2,1,0:T(8,128)} %get-tuple-element.20), calls=%async_computation.3 | async-start | bytes 524288 | tf_op jit(solution)/shard_map/all_to_all | solution.py:198
  107.1 2.0 %shard_map.66 = bf16[448,512]{1,0:T(8,128)(2,1)} custom-call(bf16[448,512]{1,0:T(8,128)(2,1)} %copy-done.4, f32[4,128]{1,0:T(4,128)} %copy-done.8, f32[4,128]{1,0:T(4,128)} %copy-done.7), custom_call_target="tpu_custom_call" | custom-call | tf_op jit(solution)/shard_map/pallas_call | solution.py:173
  109.1 1.2 reshape.27
  110.3 11.4 %all-to-all-done.3 = f32[64,8,128]{2,1,0:T(8,128)S(1)} async-done(((f32[64,8,128]{2,1,0:T(8,128)}), f32[64,8,128]{2,1,0:T(8,128)S(1)}, u32[]{:S(2)}, u32[]{:S(2)}) %all-to-all-start.3) | async-done | bytes 262176 | tf_op jit(solution)/shard_map/all_to_all | solution.py:198
  122.5 2.0 %shard_map.69 = bf16[448,512]{1,0:T(8,128)(2,1)} custom-call(bf16[448,512]{1,0:T(8,128)(2,1)} %copy-done.5, f32[4,128]{1,0:T(4,128)} %get-tuple-element.26.scale_ref, f32[4,128]{1,0:T(4,128)} %get-tuple-element.25.offset_ref), custom_call_target="tpu_custom_call" | custom-call | tf_op jit(solution)/shard_map/pallas_call | solution.py:173
  124.5 1.2 reshape.29
  126.2 2.0 %maximum_bitcast_fusion = bf16[1,2,2,14,14,512]{5,2,4,3,1,0:T(2,128)(2,1)} fusion(bf16[1,2,14,14,512]{4,1,3,2,0:T(2,128)(2,1)S(1)} %get-tuple-element.33, bf16[1,2,14,14,512]{4,1,3,2,0:T(2,128)(2,1)S(1)} %get-tuple-element.34), kind=kLoop, calls=%fused_computation | loop fusion | flops 401408 | bytes 1605632 | tf_op jit(solution)/shard_map/broadcast_in_dim | solution.py:230
  (35 shorter events, 2.4 us)
Async XLA Ops:
  0.0 25.5 %copy-start.9 = (f32[1,2,512]{2,1,0:T(2,128)S(1)}, f32[1,2,512]{2,1,0:T(2,128)}, u32[]{:S(2)}) copy-start(f32[1,2,512]{2,1,0:T(2,128)} %param.10) | copy-start | bytes 12292
  0.0 25.5 %copy-start.10 = (f32[1,2,512]{2,1,0:T(2,128)S(1)}, f32[1,2,512]{2,1,0:T(2,128)}, u32[]{:S(2)}) copy-start(f32[1,2,512]{2,1,0:T(2,128)} %param.11) | copy-start | bytes 12292
  1.6 2.3 %copy-start = (bf16[1,3,3,512,512]{4,3,2,1,0:T(8,128)(2,1)S(1)}, bf16[1,3,3,512,512]{4,3,2,1,0:T(8,128)(2,1)}, u32[]{:S(2)}) copy-start(bf16[1,3,3,512,512]{4,3,2,1,0:T(8,128)(2,1)} %param.8) | copy-start | bytes 14155780
  8.2 61.9 %copy-start.6 = (bf16[1,2,14,14,512]{4,1,3,2,0:T(2,128)(2,1)S(1)}, bf16[1,2,14,14,512]{4,1,3,2,0:T(2,128)(2,1)}, u32[]{:S(2)}) copy-start(bf16[1,2,14,14,512]{4,1,3,2,0:T(2,128)(2,1)} %param.7) | copy-start | bytes 1204228
  8.2 29.9 %all-to-all-start = ((f32[64,8,128]{2,1,0:T(8,128)}), f32[64,8,128]{2,1,0:T(8,128)S(1)}, u32[]{:S(2)}, u32[]{:S(2)}) async-start(f32[64,8,128]{2,1,0:T(8,128)} %get-tuple-element.14), calls=%async_computation | async-start | bytes 524288 | tf_op jit(solution)/shard_map/all_to_all | solution.py:198
  38.2 2.3 %copy-start.2 = (bf16[1,3,3,512,512]{4,3,2,1,0:T(8,128)(2,1)S(1)}, bf16[1,3,3,512,512]{4,3,2,1,0:T(8,128)(2,1)}, u32[]{:S(2)}) copy-start(bf16[1,3,3,512,512]{4,3,2,1,0:T(8,128)(2,1)} %param.9) | copy-start | bytes 14155780
  45.0 56.6 %copy-start.4 = (bf16[448,512]{1,0:T(8,128)(2,1)}, bf16[448,512]{1,0:T(8,128)(2,1)S(1)}, u32[]{:S(2)}) copy-start(bf16[448,512]{1,0:T(8,128)(2,1)S(1)} %get-tuple-element.15.stored_ref) | copy-start | bytes 1376260
  45.1 18.4 %all-to-all-start.1 = ((f32[64,8,128]{2,1,0:T(8,128)}), f32[64,8,128]{2,1,0:T(8,128)S(1)}, u32[]{:S(2)}, u32[]{:S(2)}) async-start(f32[64,8,128]{2,1,0:T(8,128)} %get-tuple-element.16), calls=%async_computation.1 | async-start | bytes 524288 | tf_op jit(solution)/shard_map/all_to_all | solution.py:198
  50.9 19.8 %collective-permute-start = (bf16[448,512]{1,0:T(8,128)(2,1)S(1)}, bf16[448,512]{1,0:T(8,128)(2,1)S(1)}, u32[]{:S(2)}, u32[]{:S(2)}) collective-permute-start(bf16[448,512]{1,0:T(8,128)(2,1)S(1)} %get-tuple-element.15.stored_ref), channel_id=1, source_target_pairs={{0,64},{64,128},{128,192},{192,256},{256,320},{320,384},{384,448},... | collective-permute-start | bytes 1376264 | tf_op jit(solution)/shard_map/ppermute | solution.py:194
  63.6 38.1 %copy-start.7 = (f32[4,128]{1,0:T(4,128)}, f32[4,128]{1,0:T(4,128)S(1)}, u32[]{:S(2)}) copy-start(f32[4,128]{1,0:T(4,128)S(1)} %get-tuple-element.27.offset_ref) | copy-start | bytes 6148
  63.6 38.1 %copy-start.8 = (f32[4,128]{1,0:T(4,128)}, f32[4,128]{1,0:T(4,128)S(1)}, u32[]{:S(2)}) copy-start(f32[4,128]{1,0:T(4,128)S(1)} %get-tuple-element.28.scale_ref) | copy-start | bytes 6148
  63.7 7.2 %collective-permute-start.1 = (f32[8,128]{1,0:T(8,128)S(1)}, f32[8,128]{1,0:T(8,128)S(1)}, u32[]{:S(2)}, u32[]{:S(2)}) collective-permute-start(f32[8,128]{1,0:T(8,128)S(1)} %pad_maximum_fusion), channel_id=1, source_target_pairs={{0,64},{64,128},{128,192},{192,256},{256,320},{320,384},{384,448},... | collective-permute-start | bytes 12296 | tf_op jit(solution)/shard_map/ppermute | solution.py:194
  70.8 2.3 %copy-start.1 = (bf16[1,3,3,512,512]{4,3,2,1,0:T(8,128)(2,1)S(1)}, bf16[1,3,3,512,512]{4,3,2,1,0:T(8,128)(2,1)}, u32[]{:S(2)}) copy-start(bf16[1,3,3,512,512]{4,3,2,1,0:T(8,128)(2,1)} %param.8) | copy-start | bytes 14155780
  94.8 2.3 %copy-start.3 = (bf16[1,3,3,512,512]{4,3,2,1,0:T(8,128)(2,1)S(1)}, bf16[1,3,3,512,512]{4,3,2,1,0:T(8,128)(2,1)}, u32[]{:S(2)}) copy-start(bf16[1,3,3,512,512]{4,3,2,1,0:T(8,128)(2,1)} %param.9) | copy-start | bytes 14155780
  101.7 0.8 copy-start.5
  102.5 19.2 %all-to-all-start.3 = ((f32[64,8,128]{2,1,0:T(8,128)}), f32[64,8,128]{2,1,0:T(8,128)S(1)}, u32[]{:S(2)}, u32[]{:S(2)}) async-start(f32[64,8,128]{2,1,0:T(8,128)} %get-tuple-element.20), calls=%async_computation.3 | async-start | bytes 524288 | tf_op jit(solution)/shard_map/all_to_all | solution.py:198

commit v3 on v2

--- a/solution.py
+++ b/solution.py
@@ -38,17 +38,20 @@
         padded[shift, pl.ds(plan.line + plan.rows, plan.line), :] = border
 
 
-def convolve_and_measure(plan, padded, tap, stored_ref, packed_ref):
-    pieces, filters = [], []
-    for kh in range(3):
-        for kw in range(3):
-            pieces.append(padded[kw, pl.ds(kh * plan.line, plan.rows), :])
-            filters.append(tap(kh, kw))
-    conv_out = jnp.dot(
-        jnp.concatenate(pieces, axis=1),
-        jnp.concatenate(filters, axis=0),
-        preferred_element_type=jnp.float32,
-    )
+def convolve_and_measure(plan, padded, tap, lines, stored_ref, packed_ref):
+    conv_out = None
+    for start in range(0, 3, lines):
+        pieces, filters = [], []
+        for kh in range(start, start + lines):
+            for kw in range(3):
+                pieces.append(padded[kw, pl.ds(kh * plan.line, plan.rows), :])
+                filters.append(tap(kh, kw))
+        part = jnp.dot(
+            jnp.concatenate(pieces, axis=1),
+            jnp.concatenate(filters, axis=0),
+            preferred_element_type=jnp.float32,
+        )
+        conv_out = part if conv_out is None else conv_out + part
     stored_ref[...] = conv_out.astype(jnp.bfloat16)
     real = plan.real_rows()
     means, squares = [], []
@@ -80,6 +83,14 @@
         write(lanes, jnp.where(real, jnp.maximum(values, 0.0), 0.0).astype(jnp.bfloat16))
 
 
+def in_vmem(value):
+    return pltpu.with_memory_space_constraint(value, pltpu.VMEM)
+
+
+def in_hbm(value):
+    return pltpu.with_memory_space_constraint(value, pltpu.HBM)
+
+
 def start_filters(kernel_hbm, kernel_vmem, sems):
     copies = {}
     for kh in range(3):
@@ -95,9 +106,27 @@
     return tap
 
 
+def filter_scratch(kernel):
+    return [pltpu.VMEM(kernel.shape, kernel.dtype), pltpu.SemaphoreType.DMA((3, 3))]
+
+
+def layer_outputs(plan):
+    return [
+        pltpu.VMEM((plan.rows, plan.channels), jnp.bfloat16),
+        pltpu.VMEM((plan.members, 2 * plan.groups, LANES), jnp.float32),
+    ]
+
+
+def padded_scratch(plan):
+    return pltpu.VMEM((3, plan.rows + 2 * plan.line, plan.channels), jnp.bfloat16)
+
+
+WHOLE = pl.BlockSpec(memory_space=pltpu.VMEM)
+OUTSIDE = pl.BlockSpec(memory_space=pltpu.HBM)
+PARAMS = pltpu.CompilerParams(vmem_limit_bytes=32 << 20)
+
+
 def conv_layer(plan, body, operands, kernel):
-    whole = pl.BlockSpec(memory_space=pltpu.VMEM)
-
     def run(*refs):
         ins = refs[: len(operands)]
         kernel_hbm, stored_ref, packed_ref, padded, kernel_vmem, sems = refs[len(operands) :]
@@ -105,35 +134,74 @@
         zero_borders(plan, padded)
         body(padded, *ins)
         fill_shifted(plan, padded)
-        convolve_and_measure(plan, padded, tap, stored_ref, packed_ref)
-
-    channels = plan.channels
+        convolve_and_measure(plan, padded, tap, 3, stored_ref, packed_ref)
+
     return pl.pallas_call(
         run,
-        in_specs=[whole] * len(operands) + [pl.BlockSpec(memory_space=pltpu.HBM)],
-        out_specs=[whole, whole],
-        out_shape=[
-            jax.ShapeDtypeStruct((plan.rows, channels), jnp.bfloat16),
-            jax.ShapeDtypeStruct((plan.members, 2 * plan.groups, LANES), jnp.float32),
-        ],
-        scratch_shapes=[
-            pltpu.VMEM((3, plan.rows + 2 * plan.line, channels), jnp.bfloat16),
-            pltpu.VMEM((3, 3, channels, channels), jnp.bfloat16),
-            pltpu.SemaphoreType.DMA((3, 3)),
-        ],
-        compiler_params=pltpu.CompilerParams(vmem_limit_bytes=32 << 20),
-    )(*operands, kernel)
+        in_specs=[WHOLE] * len(operands) + [OUTSIDE],
+        out_specs=[WHOLE, WHOLE],
+        out_shape=layer_outputs(plan),
+        scratch_shapes=[padded_scratch(plan)] + filter_scratch(kernel),
+        compiler_params=PARAMS,
+    )(*operands, in_hbm(kernel))
 
 
 def inner(plan):
     return pl.ds(plan.line, plan.rows)
 
 
-def layer_of_map(plan, rows, kernel):
-    def body(padded, rows_ref):
-        padded[1, inner(plan), :] = rows_ref[...]
-
-    return conv_layer(plan, body, [rows], kernel)
+def spread_lines(plan, maps_ref, write):
+    real = plan.width * plan.images
+    blank = jnp.zeros((plan.line - real, plan.channels), jnp.bfloat16)
+    for row in range(plan.height):
+        write(row * plan.line, maps_ref[row].reshape(real, plan.channels))
+        write(row * plan.line + real, blank)
+
+
+def opening_layer(plan, maps, kernel):
+    def run(maps_hbm, kernel_hbm, stored_ref, packed_ref, maps_vmem, map_sem, padded, kernel_vmem, sems):
+        fetch = pltpu.make_async_copy(maps_hbm, maps_vmem, map_sem)
+        fetch.start()
+        tap = start_filters(kernel_hbm, kernel_vmem, sems)
+        zero_borders(plan, padded)
+        fetch.wait()
+
+        def write(start, rows):
+            padded[1, pl.ds(plan.line + start, rows.shape[0]), :] = rows
+
+        spread_lines(plan, maps_vmem, write)
+        fill_shifted(plan, padded)
+        convolve_and_measure(plan, padded, tap, 1, stored_ref, packed_ref)
+
+    return pl.pallas_call(
+        run,
+        in_specs=[OUTSIDE, OUTSIDE],
+        out_specs=[WHOLE, WHOLE],
+        out_shape=layer_outputs(plan),
+        scratch_shapes=[
+            pltpu.VMEM(maps.shape, maps.dtype),
+            pltpu.SemaphoreType.DMA(()),
+            padded_scratch(plan),
+        ]
+        + filter_scratch(kernel),
+        compiler_params=PARAMS,
+    )(in_hbm(maps), in_hbm(kernel))
+
+
+def prepare(plan, maps):
+    def run(maps_ref, rows_ref):
+        def write(start, rows):
+            rows_ref[pl.ds(start, rows.shape[0]), :] = rows
+
+        spread_lines(plan, maps_ref, write)
+
+    return pl.pallas_call(
+        run,
+        in_specs=[WHOLE],
+        out_specs=WHOLE,
+        out_shape=pltpu.VMEM((plan.rows, plan.channels), jnp.bfloat16),
+        compiler_params=PARAMS,
+    )(maps)
 
 
 def layer_of_stored(plan, stored, gathered, gain, bias, kernel):
@@ -145,7 +213,7 @@
 
         normalize_into(plan, stored_ref, scale, offset, write)
 
-    return conv_layer(plan, body, [stored, gathered, gain, bias], kernel)
+    return conv_layer(plan, body, [in_vmem(stored), gathered, gain, bias], kernel)
 
 
 def layer_of_moved(plan, stored, coefficients, rows, is_first, kernel):
@@ -158,35 +226,37 @@
         both = coefficients_ref[...]
         normalize_into(plan, stored_ref, both[: plan.groups], both[plan.groups :], write)
 
-    return conv_layer(plan, body, [stored, coefficients, rows, is_first], kernel)
-
-
-def finish(plan, stored, scale, offset):
-    whole = pl.BlockSpec(memory_space=pltpu.VMEM)
-
-    def run(stored_ref, scale_ref, offset_ref, out_ref):
+    return conv_layer(plan, body, [stored, coefficients, in_vmem(rows), is_first], kernel)
+
+
+def finish(plan, stored, joined, result, tick):
+    shape = (TICKS, plan.height, plan.width, plan.images, plan.channels)
+
+    def run(stored_ref, *refs):
+        out_ref = refs[-1]
+        terms = [ref[...] for ref in refs[: len(joined)]]
+        if len(terms) == 1:
+            scale, offset = terms[0][: plan.groups], terms[0][plan.groups :]
+        else:
+            scale, offset = join(plan, *terms)
+
         def write(lanes, values):
-            out_ref[:, lanes] = values
-
-        normalize_into(plan, stored_ref, scale_ref[...], offset_ref[...], write)
-
+            for row in range(plan.height):
+                line = values[row * plan.line : row * plan.line + plan.width * plan.images]
+                out_ref[0, row, :, :, lanes] = line.reshape(plan.width, plan.images, LANES)
+
+        normalize_into(plan, stored_ref, scale, offset, write)
+
+    before = [] if result is None else [result]
     return pl.pallas_call(
         run,
-        in_specs=[whole] * 3,
-        out_specs=whole,
-        out_shape=jax.ShapeDtypeStruct(stored.shape, stored.dtype),
-    )(stored, scale, offset)
-
-
-def to_rows(plan, maps):
-    rows = jnp.transpose(maps, (1, 2, 0, 3))
-    rows = jnp.pad(rows, ((0, 0), (0, plan.wide - plan.width), (0, 0), (0, 0)))
-    return rows.reshape(plan.rows, plan.channels)
-
-
-def to_maps(plan, rows):
-    maps = rows.reshape(plan.height, plan.wide, plan.images, plan.channels)[:, : plan.width]
-    return jnp.transpose(maps, (2, 0, 1, 3))
+        grid=(1,),
+        in_specs=[WHOLE] * (1 + len(joined)) + [OUTSIDE] * len(before),
+        out_specs=pl.BlockSpec((1,) + shape[1:], lambda i: (tick, 0, 0, 0, 0)),
+        out_shape=pltpu.HBM(shape, jnp.bfloat16),
+        input_output_aliases={1 + len(joined): 0} if before else {},
+        compiler_params=PARAMS,
+    )(in_vmem(stored), *joined, *before)
 
 
 def from_behind(value, axis):
@@ -213,21 +283,29 @@
     gain = stretch_factors[0].reshape(2, plan.groups, LANES)
     bias = shift_terms[0].reshape(2, plan.groups, LANES)
     is_first = jnp.broadcast_to((lax.axis_index("section") == 0).astype(jnp.float32), (1, LANES))
-    stored, packed = layer_of_map(plan, to_rows(plan, pending_section_entries[0]), first_kernel)
-    results = []
+    order = (1, 2, 0, 3)
+    stored, packed = opening_layer(
+        plan, jnp.transpose(pending_section_entries[0], order), first_kernel
+    )
+    result = None
     for tick in range(TICKS):
-        stored, packed = layer_of_stored(plan, stored, exchange(packed), gain[0], bias[0], second_kernel)
         last = tick + 1 == TICKS
         if not last:
+            packed, arriving = lax.optimization_barrier((packed, arriving_microsets[tick]))
+            rows = prepare(plan, jnp.transpose(arriving, order))
+        gathered = exchange(packed)
+        if not last:
+            gathered, rows = lax.optimization_barrier((gathered, rows))
+        stored, packed = layer_of_stored(plan, stored, gathered, gain[0], bias[0], second_kernel)
+        if last:
+            result = finish(plan, stored, [exchange(packed), gain[1], bias[1]], result, tick)
+        else:
             moved = from_behind(stored, "section")
-        scale, offset = join(plan, exchange(packed), gain[1], bias[1])
-        if not last:
-            coefficients = from_behind(jnp.concatenate([scale, offset], axis=0), "section")
-        results.append(to_maps(plan, finish(plan, stored, scale, offset)))
-        if not last:
-            rows = to_rows(plan, arriving_microsets[tick])
+            coefficients = jnp.concatenate(join(plan, exchange(packed), gain[1], bias[1]), axis=0)
+            result = finish(plan, stored, [coefficients], result, tick)
+            coefficients = from_behind(coefficients, "section")
             stored, packed = layer_of_moved(plan, moved, coefficients, rows, is_first, first_kernel)
-    return jnp.stack(results, axis=0)[None]
+    return jnp.transpose(result, (0, 3, 1, 2, 4))[None]
 
 
 def solution(mesh):

time: 129 us -> 117 us (0.907)
  local copies, waits for them, and re-layouts: 15.3 us -> 0.02 us
  Pallas kernels: 21 us -> 24.7 us
  other arithmetic: 2.99 us -> 0.18 us
  waiting for transfers between devices: 31.7 us -> 34.3 us
    unnamed x22 -> x6, local copies, waits for them, and re-layouts: 10.1 us -> 0.01 us
    pallas_call x6 -> x7, Pallas kernels: 21 us -> 24.7 us  [the longest x3 16 us: conv_layer(): pl.pallas_call(run, in_specs=[WHOLE] * len(operands) + [OUTSIDE], out_spe...]
    reshape x4 -> x0, local copies, waits for them, and re-layouts: 2.74 us -> none  [the longest x2 2.39 us: to_maps(): rows.reshape(plan.height, plan.wide, plan.images, plan.channels)]
    broadcast_in_dim x1 -> x0, other arithmetic: 2.05 us -> none  [body(): return jnp.stack(results, axis=0)[None]]
    all_to_all x3, waiting for transfers between devices: 31.6 us -> 33.6 us  [exchange(): return lax.all_to_all(copies, 'replica', 0, 0)]
    pad x2 -> x0, local copies, waits for them, and re-layouts: 1.86 us -> none  [to_rows(): rows = jnp.pad(rows, ((0, 0), (0, plan.wide - plan.width), (0, 0), (0, 0)))]
  transfers between devices with their start and end apart: 5 -> 5, of which waited for: 4 -> 4; matrix products, arithmetic and copies ran while one was open for 2% -> 0% of each run, Pallas kernels for 2% -> 1%
where the time goes in v3:
time: 117 us; the launch traced here: 116 us
  starting transfers between devices  39 us (33%)
  waiting for transfers between devices  34.3 us (29%)
  Pallas kernels  24.7 us (21%)
  blocking collectives  17.8 us (15%)
    all_to_all x3, waiting for transfers between devices, exchange(): return lax.all_to_all(copies, 'replica', 0, 0)  33.6 us
    all_to_all x3, starting transfers between devices, exchange(): return lax.all_to_all(copies, 'replica', 0, 0)  27.6 us
    all_to_all x1, blocking collectives, exchange(): return lax.all_to_all(copies, 'replica', 0, 0)  17.8 us
    pallas_call x3, Pallas kernels, conv_layer(): pl.pallas_call(run, in_specs=[WHOLE] * len(operands) + [OUTSIDE], out_spe...  16 us
    ppermute x2, starting transfers between devices, from_behind(): return lax.ppermute(value, axis, pairs)  11.4 us
    pallas_call x1, Pallas kernels, opening_layer(): pl.pallas_call(run, in_specs=[OUTSIDE, OUTSIDE], out_specs=[WHOLE, WHOLE]...  6.35 us
  transfers between devices with their start and end apart: 5, of which 4 were waited for; matrix products, arithmetic and copies ran while one was open for 0% of the time, Pallas kernels for 1%

profile of v3, /device:TPU:1, one launch (start us, length us, event | category | flops | bytes accessed | tf_op | source)
XLA Modules:
  0.0 116.2 jit_solution(5750948833504695475)
XLA Ops:
  0.0 0.0 copy-start
  0.0 6.3 %shard_map.64 = (bf16[448,512]{1,0:T(8,128)(2,1)S(1)}, f32[64,8,128]{2,1,0:T(8,128)}) custom-call(bf16[14,14,2,512]{3,2,1,0:T(2,128)(2,1)} %bitcast.27, bf16[3,3,512,512]{3,2,1,0:T(8,128)(2,1)} %bitcast.23), custom_call_target="tpu_custom_call" | custom-call | tf_op jit(solution)/shard_map/pallas_call | solution.py:176
  6.4 17.1 %all-to-all-start = ((f32[64,8,128]{2,1,0:T(8,128)}), f32[64,8,128]{2,1,0:T(8,128)S(1)}, u32[]{:S(2)}, u32[]{:S(2)}) async-start(f32[64,8,128]{2,1,0:T(8,128)} %get-tuple-element.19), calls=%async_computation | async-start | bytes 524288 | tf_op jit(solution)/shard_map/all_to_all | solution.py:268
  23.5 0.0 copy-done
  23.5 0.1 shard_map.65.refs_2_
  23.6 0.0 copy-done.1
  23.6 0.0 copy-done.2
  23.7 12.5 %all-to-all-done.refs_1_ = f32[64,8,128]{2,1,0:T(8,128)S(1)} async-done(((f32[64,8,128]{2,1,0:T(8,128)}), f32[64,8,128]{2,1,0:T(8,128)S(1)}, u32[]{:S(2)}, u32[]{:S(2)}) %all-to-all-start) | async-done | bytes 262176 | tf_op jit(solution)/shard_map/all_to_all | solution.py:268
  36.2 5.5 %shard_map.66 = (bf16[448,512]{1,0:T(8,128)(2,1)S(1)}, f32[64,8,128]{2,1,0:T(8,128)}) custom-call(bf16[448,512]{1,0:T(8,128)(2,1)S(1)} %get-tuple-element.17.refs_0_, f32[64,8,128]{2,1,0:T(8,128)S(1)} %all-to-all-done.refs_1_, f32[4,128]{1,0:T(4,128)S(1)} %bitcast.15, f32[4,128]{1,0:T(4,128)S(1)} %bitcast.17, bf16[3,3,512,512]{3,2,1,0:T(8,128)(2,1)} %bitcast.25), custom_call_target="tpu_custom_call" | custom-call | tf_op jit(solution)/shard_map/pallas_call | solution.py:139
  41.7 5.8 %all-to-all-start.1 = ((f32[64,8,128]{2,1,0:T(8,128)}), f32[64,8,128]{2,1,0:T(8,128)S(1)}, u32[]{:S(2)}, u32[]{:S(2)}) async-start(f32[64,8,128]{2,1,0:T(8,128)} %get-tuple-element.23), calls=%async_computation.1 | async-start | bytes 524288 | tf_op jit(solution)/shard_map/all_to_all | solution.py:268
  47.6 5.0 %collective-permute-start = (bf16[448,512]{1,0:T(8,128)(2,1)S(1)}, bf16[448,512]{1,0:T(8,128)(2,1)S(1)}, u32[]{:S(2)}, u32[]{:S(2)}) collective-permute-start(bf16[448,512]{1,0:T(8,128)(2,1)S(1)} %get-tuple-element.22.stored_ref), channel_id=1, source_target_pairs={{0,64},{64,128},{128,192},{192,256},{256,320},{320,384},{384,448},... | collective-permute-start | bytes 1376264 | tf_op jit(solution)/shard_map/ppermute | solution.py:264
  52.6 7.5 %all-to-all-done.1 = f32[64,8,128]{2,1,0:T(8,128)S(1)} async-done(((f32[64,8,128]{2,1,0:T(8,128)}), f32[64,8,128]{2,1,0:T(8,128)S(1)}, u32[]{:S(2)}, u32[]{:S(2)}) %all-to-all-start.1) | async-done | bytes 262176 | tf_op jit(solution)/shard_map/all_to_all | solution.py:268
  60.1 0.1 slice_reduce_fusion.1
  60.2 0.1 multiply_reduce_fusion
  60.3 6.4 %collective-permute-start.1 = (f32[8,128]{1,0:T(8,128)S(1)}, f32[8,128]{1,0:T(8,128)S(1)}, u32[]{:S(2)}, u32[]{:S(2)}) collective-permute-start(f32[8,128]{1,0:T(8,128)S(1)} %pad_maximum_fusion.refs_0_), channel_id=1, source_target_pairs={{0,64},{64,128},{128,192},{192,256},{256,320},{320,384},{384,448},... | collective-permute-start | bytes 12296 | tf_op jit(solution)/shard_map/ppermute | solution.py:264
  66.7 0.0 collective-permute-done.refs_0_
  66.8 0.7 collective-permute-done.1.refs_1_
  67.5 4.8 %shard_map.67 = (bf16[448,512]{1,0:T(8,128)(2,1)S(1)}, f32[64,8,128]{2,1,0:T(8,128)S(1)}) custom-call(bf16[448,512]{1,0:T(8,128)(2,1)S(1)} %collective-permute-done.refs_0_, f32[8,128]{1,0:T(8,128)S(1)} %collective-permute-done.1.refs_1_, bf16[448,512]{1,0:T(8,128)(2,1)S(1)} %shard_map.65.refs_2_, f32[1,128]{1,0:T(1,128)S(1)} %broadcast_in_dim.7.refs_3_, ...), custom_call_target="tpu_custom_call" | custom-call | tf_op jit(solution)/shard_map/pallas_call | solution.py:139
  72.3 17.8 %all_to_all.20.refs_1_ = f32[64,8,128]{2,1,0:T(8,128)S(1)} all-to-all(f32[64,8,128]{2,1,0:T(8,128)S(1)} %get-tuple-element.26), channel_id=1, replica_groups=mesh['section'=8,'replica'=64] {'replica'}, dimensions={0} | all-to-all | bytes 524288 | tf_op jit(solution)/shard_map/all_to_all | solution.py:268
  90.2 5.6 %shard_map.68 = (bf16[448,512]{1,0:T(8,128)(2,1)S(1)}, f32[64,8,128]{2,1,0:T(8,128)}) custom-call(bf16[448,512]{1,0:T(8,128)(2,1)S(1)} %get-tuple-element.25.refs_0_, f32[64,8,128]{2,1,0:T(8,128)S(1)} %all_to_all.20.refs_1_, f32[4,128]{1,0:T(4,128)S(1)} %bitcast.16, f32[4,128]{1,0:T(4,128)S(1)} %bitcast.18, bf16[3,3,512,512]{3,2,1,0:T(8,128)(2,1)} %bitcast.26), custom_call_target="tpu_custom_call" | custom-call | tf_op jit(solution)/shard_map/pallas_call | solution.py:139
  95.7 4.6 %all-to-all-start.3 = ((f32[64,8,128]{2,1,0:T(8,128)}), f32[64,8,128]{2,1,0:T(8,128)S(1)}, u32[]{:S(2)}, u32[]{:S(2)}) async-start(f32[64,8,128]{2,1,0:T(8,128)} %get-tuple-element.28), calls=%async_computation.3 | async-start | bytes 524288 | tf_op jit(solution)/shard_map/all_to_all | solution.py:268
  100.4 1.1 shard_map.69.refs_3_
  101.4 13.5 %all-to-all-done.3.refs_0_ = f32[64,8,128]{2,1,0:T(8,128)S(1)} async-done(((f32[64,8,128]{2,1,0:T(8,128)}), f32[64,8,128]{2,1,0:T(8,128)S(1)}, u32[]{:S(2)}, u32[]{:S(2)}) %all-to-all-start.3) | async-done | bytes 262176 | tf_op jit(solution)/shard_map/all_to_all | solution.py:268
  115.0 1.2 %shard_map.70 = bf16[2,14,14,2,512]{4,3,2,1,0:T(2,128)(2,1)} custom-call(bf16[448,512]{1,0:T(8,128)(2,1)S(1)} %get-tuple-element.27.stored_ref, f32[64,8,128]{2,1,0:T(8,128)S(1)} %all-to-all-done.3.refs_0_, f32[4,128]{1,0:T(4,128)S(1)} %bitcast.20, f32[4,128]{1,0:T(4,128)S(1)} %bitcast.22, ...), custom_call_target="tpu_custom_call", output_to_operand_aliasing={{}: (4, {})} | custom-call | tf_op jit(solution)/shard_map/pallas_call | solution.py:251
  (8 shorter events, 0.0 us)
Async XLA Ops:
  0.0 23.5 %copy-start = (bf16[1,2,14,14,512]{4,1,3,2,0:T(2,128)(2,1)S(1)}, bf16[1,2,14,14,512]{4,1,3,2,0:T(2,128)(2,1)}, u32[]{:S(2)}) copy-start(bf16[1,2,14,14,512]{4,1,3,2,0:T(2,128)(2,1)} %param.7) | copy-start | bytes 1204228
  0.0 23.6 %copy-start.1 = (f32[1,2,512]{2,1,0:T(2,128)S(1)}, f32[1,2,512]{2,1,0:T(2,128)}, u32[]{:S(2)}) copy-start(f32[1,2,512]{2,1,0:T(2,128)} %param.10) | copy-start | bytes 12292
  0.0 23.6 %copy-start.2 = (f32[1,2,512]{2,1,0:T(2,128)S(1)}, f32[1,2,512]{2,1,0:T(2,128)}, u32[]{:S(2)}) copy-start(f32[1,2,512]{2,1,0:T(2,128)} %param.11) | copy-start | bytes 12292
  6.4 29.8 %all-to-all-start = ((f32[64,8,128]{2,1,0:T(8,128)}), f32[64,8,128]{2,1,0:T(8,128)S(1)}, u32[]{:S(2)}, u32[]{:S(2)}) async-start(f32[64,8,128]{2,1,0:T(8,128)} %get-tuple-element.19), calls=%async_computation | async-start | bytes 524288 | tf_op jit(solution)/shard_map/all_to_all | solution.py:268
  41.7 18.4 %all-to-all-start.1 = ((f32[64,8,128]{2,1,0:T(8,128)}), f32[64,8,128]{2,1,0:T(8,128)S(1)}, u32[]{:S(2)}, u32[]{:S(2)}) async-start(f32[64,8,128]{2,1,0:T(8,128)} %get-tuple-element.23), calls=%async_computation.1 | async-start | bytes 524288 | tf_op jit(solution)/shard_map/all_to_all | solution.py:268
  47.6 19.2 %collective-permute-start = (bf16[448,512]{1,0:T(8,128)(2,1)S(1)}, bf16[448,512]{1,0:T(8,128)(2,1)S(1)}, u32[]{:S(2)}, u32[]{:S(2)}) collective-permute-start(bf16[448,512]{1,0:T(8,128)(2,1)S(1)} %get-tuple-element.22.stored_ref), channel_id=1, source_target_pairs={{0,64},{64,128},{128,192},{192,256},{256,320},{320,384},{384,448},... | collective-permute-start | bytes 1376264 | tf_op jit(solution)/shard_map/ppermute | solution.py:264
  60.3 7.1 %collective-permute-start.1 = (f32[8,128]{1,0:T(8,128)S(1)}, f32[8,128]{1,0:T(8,128)S(1)}, u32[]{:S(2)}, u32[]{:S(2)}) collective-permute-start(f32[8,128]{1,0:T(8,128)S(1)} %pad_maximum_fusion.refs_0_), channel_id=1, source_target_pairs={{0,64},{64,128},{128,192},{192,256},{256,320},{320,384},{384,448},... | collective-permute-start | bytes 12296 | tf_op jit(solution)/shard_map/ppermute | solution.py:264
  95.7 19.2 %all-to-all-start.3 = ((f32[64,8,128]{2,1,0:T(8,128)}), f32[64,8,128]{2,1,0:T(8,128)S(1)}, u32[]{:S(2)}, u32[]{:S(2)}) async-start(f32[64,8,128]{2,1,0:T(8,128)} %get-tuple-element.28), calls=%async_computation.3 | async-start | bytes 524288 | tf_op jit(solution)/shard_map/all_to_all | solution.py:268

commit v4 on v3

v4 whole, which is shorter than its diff:
```python
import jax
import jax.numpy as jnp
from jax import lax
from jax.experimental import pallas as pl
from jax.experimental.pallas import tpu as pltpu
from jax.sharding import PartitionSpec as P

TICKS = 2
LANES = 128
EPS = 1e-05


class Plan:
    def __init__(self, images, height, width, channels, members):
        self.images, self.height, self.width, self.channels = images, height, width, channels
        self.members = members
        self.wide = 16
        self.line = self.wide * images
        self.rows = height * self.line
        self.groups = channels // LANES
        self.count = images * height * width

    def real_rows(self):
        row = lax.broadcasted_iota(jnp.int32, (self.rows, LANES), 0)
        return row % self.line < self.width * self.images


def fill_shifted(plan, padded):
    line, rows, step = plan.line, plan.rows, plan.images
    padded[0, pl.ds(line, rows), :] = padded[1, pl.ds(line - step, rows), :]
    padded[2, pl.ds(line, rows), :] = padded[1, pl.ds(line + step, rows), :]


def zero_borders(plan, padded):
    border = jnp.zeros((plan.line, plan.channels), jnp.bfloat16)
    for shift in range(3):
        padded[shift, pl.ds(0, plan.line), :] = border
        padded[shift, pl.ds(plan.line + plan.rows, plan.line), :] = border


def convolve_and_measure(plan, padded, tap, stored_ref, packed_ref):
    conv_out = None
    for kh in range(3):
        for kw in range(3):
            shifted = padded[kw, pl.ds(kh * plan.line, plan.rows), :]
            part = jnp.dot(shifted, tap(kh, kw), preferred_element_type=jnp.float32)
            conv_out = part if conv_out is None else conv_out + part
    stored_ref[...] = conv_out.astype(jnp.bfloat16)
    real = plan.real_rows()
    means, deviations = [], []
    for group in range(plan.groups):
        values = jnp.where(real, conv_out[:, group * LANES : (group + 1) * LANES], 0.0)
        mean = jnp.sum(values, axis=0, keepdims=True) / plan.count
        centred = jnp.where(real, values - mean, 0.0)
        means.append(mean)
        deviations.append(jnp.sqrt(jnp.sum(centred * centred, axis=0, keepdims=True) / plan.count))
    packed_ref[...] = jnp.concatenate(means + deviations, axis=0)


def join(plan, packed, gain, bias):
    groups = plan.groups
    copies = jnp.broadcast_to(packed.astype(jnp.float16), (plan.members,) + packed.shape)
    gathered = lax.all_to_all(copies, "replica", 0, 0)
    gathered, gain, bias = lax.optimization_barrier((gathered, gain, bias))
    gathered = gathered.astype(jnp.float32)
    gain, bias = gain.reshape(groups, LANES), bias.reshape(groups, LANES)
    means, deviations = gathered[:, :groups], gathered[:, groups:]
    mean = jnp.sum(means, axis=0) / plan.members
    apart = means - mean
    var = jnp.sum(deviations * deviations + apart * apart, axis=0) / plan.members
    scale = gain * lax.rsqrt(var + EPS)
    return jnp.concatenate([scale, bias - mean * scale], axis=0)


def normalize_into(plan, stored_ref, terms, write):
    real = plan.real_rows()
    scale, offset = terms[: plan.groups], terms[plan.groups :]
    for group in range(plan.groups):
        lanes = slice(group * LANES, (group + 1) * LANES)
        values = stored_ref[:, lanes].astype(jnp.float32) * scale[group : group + 1] + offset[group : group + 1]
        write(lanes, jnp.where(real, jnp.maximum(values, 0.0), 0.0).astype(jnp.bfloat16))


def in_vmem(value):
    return pltpu.with_memory_space_constraint(value, pltpu.VMEM)


def in_hbm(value):
    return pltpu.with_memory_space_constraint(value, pltpu.HBM)


def start_filters(kernel_hbm, kernel_vmem, sems):
    copies = {}
    for kh in range(3):
        for kw in range(3):
            copy = pltpu.make_async_copy(kernel_hbm.at[kh, kw], kernel_vmem.at[kh, kw], sems.at[kh, kw])
            copy.start()
            copies[kh, kw] = copy

    def tap(kh, kw):
        copies[kh, kw].wait()
        return kernel_vmem[kh, kw]

    return tap


def filter_scratch(kernel):
    return [pltpu.VMEM(kernel.shape, kernel.dtype), pltpu.SemaphoreType.DMA((3, 3))]


def layer_outputs(plan):
    return [
        pltpu.VMEM((plan.rows, plan.channels), jnp.bfloat16),
        pltpu.VMEM((2 * plan.groups, LANES), jnp.float32),
    ]


def padded_scratch(plan):
    return pltpu.VMEM((3, plan.rows + 2 * plan.line, plan.channels), jnp.bfloat16)


WHOLE = pl.BlockSpec(memory_space=pltpu.VMEM)
OUTSIDE = pl.BlockSpec(memory_space=pltpu.HBM)
PARAMS = pltpu.CompilerParams(vmem_limit_bytes=32 << 20)


def conv_layer(plan, body, operands, kernel):
    def run(*refs):
        ins = refs[: len(operands)]
        kernel_hbm, stored_ref, packed_ref, padded, kernel_vmem, sems = refs[len(operands) :]
        tap = start_filters(kernel_hbm, kernel_vmem, sems)
        zero_borders(plan, padded)
        body(padded, *ins)
        fill_shifted(plan, padded)
        convolve_and_measure(plan, padded, tap, stored_ref, packed_ref)

    return pl.pallas_call(
        run,
        in_specs=[WHOLE] * len(operands) + [OUTSIDE],
        out_specs=[WHOLE, WHOLE],
        out_shape=layer_outputs(plan),
        scratch_shapes=[padded_scratch(plan)] + filter_scratch(kernel),
        compiler_params=PARAMS,
    )(*operands, in_hbm(kernel))


def inner(plan):
    return pl.ds(plan.line, plan.rows)


def spread_lines(plan, maps_ref, write):
    real = plan.width * plan.images
    blank = jnp.zeros((plan.line - real, plan.channels), jnp.bfloat16)
    for row in range(plan.height):
        write(row * plan.line, maps_ref[row].reshape(real, plan.channels))
        write(row * plan.line + real, blank)


def opening_layer(plan, maps, kernel):
    def run(maps_hbm, kernel_hbm, stored_ref, packed_ref, maps_vmem, map_sem, padded, kernel_vmem, sems):
        fetch = pltpu.make_async_copy(maps_hbm, maps_vmem, map_sem)
        fetch.start()
        tap = start_filters(kernel_hbm, kernel_vmem, sems)
        zero_borders(plan, padded)
        fetch.wait()

        def write(start, rows):
            padded[1, pl.ds(plan.line + start, rows.shape[0]), :] = rows

        spread_lines(plan, maps_vmem, write)
        fill_shifted(plan, padded)
        convolve_and_measure(plan, padded, tap, stored_ref, packed_ref)

    return pl.pallas_call(
        run,
        in_specs=[OUTSIDE, OUTSIDE],
        out_specs=[WHOLE, WHOLE],
        out_shape=layer_outputs(plan),
        scratch_shapes=[
            pltpu.VMEM(maps.shape, maps.dtype),
            pltpu.SemaphoreType.DMA(()),
            padded_scratch(plan),
        ]
        + filter_scratch(kernel),
        compiler_params=PARAMS,
    )(in_hbm(maps), in_hbm(kernel))


def layer_of_stored(plan, stored, terms, kernel):
    def body(padded, stored_ref, terms_ref):
        def write(lanes, values):
            padded[1, inner(plan), lanes] = values

        normalize_into(plan, stored_ref, terms_ref[...], write)

    return conv_layer(plan, body, [in_vmem(stored), terms], kernel)


def layer_of_moved(plan, stored, terms, maps, is_first, kernel):
    def body(padded, stored_ref, terms_ref, maps_ref, first_ref):
        first = jnp.broadcast_to(first_ref[...], (plan.rows, LANES)) > 0.5

        def write(lanes, values):
            arrived = padded[1, inner(plan), lanes]
            padded[1, inner(plan), lanes] = jnp.where(first, arrived, values)

        def write_line(start, rows):
            padded[1, pl.ds(plan.line + start, rows.shape[0]), :] = rows

        spread_lines(plan, maps_ref, write_line)
        normalize_into(plan, stored_ref, terms_ref[...], write)

    return conv_layer(plan, body, [in_vmem(stored), terms, in_vmem(maps), is_first], kernel)


def finish(plan, stored, terms):
    shape = (TICKS, plan.height, plan.width, plan.images, plan.channels)

    def run(*refs):
        out_ref = refs[-1]
        for tick in range(TICKS):

            def write(lanes, values, tick=tick):
                for row in range(plan.height):
                    line = values[row * plan.line : row * plan.line + plan.width * plan.images]
                    out_ref[tick, row, :, :, lanes] = line.reshape(plan.width, plan.images, LANES)

            normalize_into(plan, refs[tick], refs[TICKS + tick][...], write)

    return pl.pallas_call(
        run,
        in_specs=[WHOLE] * (2 * TICKS),
        out_specs=WHOLE,
        out_shape=pltpu.HBM(shape, jnp.bfloat16),
        compiler_params=PARAMS,
    )(*(in_vmem(value) for value in stored), *terms)


def from_behind(value, axis):
    pairs = [(i, i + 1) for i in range(lax.axis_size(axis) - 1)]
    return lax.ppermute(value, axis, pairs)


def body(
    pending_section_entries,
    arriving_microsets,
    opening_filter_kernel,
    closing_filter_kernel,
    stretch_factors,
    shift_terms,
):
    _, images, height, width, channels = pending_section_entries.shape
    plan = Plan(images, height, width, channels, lax.axis_size("replica"))
    first_kernel = opening_filter_kernel[0]
    second_kernel = closing_filter_kernel[0]
    gain = stretch_factors[0]
    bias = shift_terms[0]
    is_first = jnp.broadcast_to((lax.axis_index("section") == 0).astype(jnp.float32), (1, LANES))
    order = (1, 2, 0, 3)
    stored, packed = opening_layer(
        plan, jnp.transpose(pending_section_entries[0], order), first_kernel
    )
    kept, kept_terms = [], []
    for tick in range(TICKS):
        terms = join(plan, packed, gain[0], bias[0])
        stored, packed = layer_of_stored(plan, stored, terms, second_kernel)
        last = tick + 1 == TICKS
        if not last:
            moved = from_behind(stored, "section")
        terms = join(plan, packed, gain[1], bias[1])
        kept.append(stored)
        kept_terms.append(terms)
        if not last:
            terms = from_behind(terms, "section")
            arriving = jnp.transpose(arriving_microsets[tick], order)
            stored, packed = layer_of_moved(plan, moved, terms, arriving, is_first, first_kernel)
    result = finish(plan, kept, kept_terms)
    return jnp.transpose(result, (0, 3, 1, 2, 4))[None]


def solution(mesh):
    in_specs = (
        P("section", "replica", None, None, None),
        P(None, "replica", None, None, None),
        P("section", None, None, None, None),
        P("section", None, None, None, None),
        P("section", None, None),
        P("section", None, None),
    )
    out_specs = P("section", None, "replica", None, None, None)
    return jax.shard_map(body, mesh=mesh, in_specs=in_specs, out_specs=out_specs, check_vma=False)
```

time: 117 us -> 108 us (0.923)
  the two profiles are of different devices: /device:TPU:1 before, /device:TPU:2 now
where the time goes in v4:
time: 108 us
  blocking collectives  33.7 us (31%)
  waiting for transfers between devices  26.5 us (25%)
  starting transfers between devices  25 us (23%)
  Pallas kernels  20.1 us (19%)
  local copies, waits for them, and re-layouts  1.42 us (1%)
    all_to_all x2, blocking collectives, join(): gathered = lax.all_to_all(copies, 'replica', 0, 0)  33.7 us
    all_to_all x2, waiting for transfers between devices, join(): gathered = lax.all_to_all(copies, 'replica', 0, 0)  23.5 us
    all_to_all x2, starting transfers between devices, join(): gathered = lax.all_to_all(copies, 'replica', 0, 0)  21.2 us
    pallas_call x3, Pallas kernels, conv_layer(): pl.pallas_call(run, in_specs=[WHOLE] * len(operands) + [OUTSIDE], out_spe...  12.9 us
    pallas_call x1, Pallas kernels, opening_layer(): pl.pallas_call(run, in_specs=[OUTSIDE, OUTSIDE], out_specs=[WHOLE, WHOLE]...  5.66 us
    ppermute x2, starting transfers between devices, from_behind(): return lax.ppermute(value, axis, pairs)  3.84 us
    ppermute x2, waiting for transfers between devices, from_behind(): return lax.ppermute(value, axis, pairs)  2.99 us
  transfers between devices with their start and end apart: 4, of which 3 were waited for; matrix products, arithmetic and copies ran while one was open for 0% of the time, Pallas kernels for 0%

profile of v4, /device:TPU:2, one launch (start us, length us, event | category | flops | bytes accessed | tf_op | source)
XLA Modules:
  0.0 107.8 jit_solution(11293783437191299545)
XLA Ops:
  0.0 5.7 %shard_map.64 = (bf16[448,512]{1,0:T(8,128)(2,1)S(1)}, f32[8,128]{1,0:T(8,128)S(1)}) custom-call(bf16[14,14,2,512]{3,2,1,0:T(2,128)(2,1)} %bitcast.40, bf16[3,3,512,512]{3,2,1,0:T(8,128)(2,1)} %bitcast.36), custom_call_target="tpu_custom_call" | custom-call | tf_op jit(solution)/shard_map/pallas_call | solution.py:174
  5.7 0.7 broadcast_in_dim.22
  6.4 16.6 %all-to-all-start = ((f16[64,8,128]{2,1,0:T(8,128)(2,1)}), f16[64,8,128]{2,1,0:T(8,128)(2,1)S(1)}, u32[]{:S(2)}, u32[]{:S(2)}) async-start(f16[64,8,128]{2,1,0:T(8,128)(2,1)} %broadcast_in_dim.22), calls=%async_computation | async-start | bytes 262144 | tf_op jit(solution)/shard_map/all_to_all | solution.py:63
  23.0 12.7 %all-to-all-done = f16[64,8,128]{2,1,0:T(8,128)(2,1)S(1)} async-done(((f16[64,8,128]{2,1,0:T(8,128)(2,1)}), f16[64,8,128]{2,1,0:T(8,128)(2,1)S(1)}, u32[]{:S(2)}, u32[]{:S(2)}) %all-to-all-start) | async-done | bytes 131104 | tf_op jit(solution)/shard_map/all_to_all | solution.py:63
  35.7 0.1 slice_reduce_fusion.3
  35.8 0.1 fusion.7
  35.9 4.3 %shard_map.65 = (bf16[448,512]{1,0:T(8,128)(2,1)S(1)}, f32[8,128]{1,0:T(8,128)S(1)}) custom-call(bf16[448,512]{1,0:T(8,128)(2,1)S(1)} %get-tuple-element.25.refs_0_, f32[8,128]{1,0:T(8,128)S(1)} %pad_maximum_fusion.refs_1_, bf16[3,3,512,512]{3,2,1,0:T(8,128)(2,1)} %bitcast.38), custom_call_target="tpu_custom_call" | custom-call | tf_op jit(solution)/shard_map/pallas_call | solution.py:137
  40.2 0.7 broadcast_in_dim.23
  40.9 4.6 %all-to-all-start.1 = ((f16[64,8,128]{2,1,0:T(8,128)(2,1)}), f16[64,8,128]{2,1,0:T(8,128)(2,1)S(1)}, u32[]{:S(2)}, u32[]{:S(2)}) async-start(f16[64,8,128]{2,1,0:T(8,128)(2,1)} %broadcast_in_dim.23), calls=%async_computation.1 | async-start | bytes 262144 | tf_op jit(solution)/shard_map/all_to_all | solution.py:63
  45.5 1.9 %collective-permute-start = (bf16[448,512]{1,0:T(8,128)(2,1)S(1)}, bf16[448,512]{1,0:T(8,128)(2,1)S(1)}, u32[]{:S(2)}, u32[]{:S(2)}) collective-permute-start(bf16[448,512]{1,0:T(8,128)(2,1)S(1)} %get-tuple-element.30.refs_0_), channel_id=1, source_target_pairs={{0,64},{64,128},{128,192},{192,256},{256,320},{320,384},{384,448},... | collective-permute-start | bytes 1376264 | tf_op jit(solution)/shard_map/ppermute | solution.py:241
  47.5 10.8 %all-to-all-done.1 = f16[64,8,128]{2,1,0:T(8,128)(2,1)S(1)} async-done(((f16[64,8,128]{2,1,0:T(8,128)(2,1)}), f16[64,8,128]{2,1,0:T(8,128)(2,1)S(1)}, u32[]{:S(2)}, u32[]{:S(2)}) %all-to-all-start.1) | async-done | bytes 131104 | tf_op jit(solution)/shard_map/all_to_all | solution.py:63
  58.3 0.1 slice_reduce_fusion.2
  58.4 0.1 fusion.5
  58.5 1.9 %collective-permute-start.1 = (f32[8,128]{1,0:T(8,128)S(1)}, f32[8,128]{1,0:T(8,128)S(1)}, u32[]{:S(2)}, u32[]{:S(2)}) collective-permute-start(f32[8,128]{1,0:T(8,128)S(1)} %pad_maximum_fusion.1.refs_2_), channel_id=1, source_target_pairs={{0,64},{64,128},{128,192},{192,256},{256,320},{320,384},{384,448},... | collective-permute-start | bytes 12296 | tf_op jit(solution)/shard_map/ppermute | solution.py:241
  60.4 3.0 %collective-permute-done.1.refs_1_ = f32[8,128]{1,0:T(8,128)S(1)} collective-permute-done((f32[8,128]{1,0:T(8,128)S(1)}, f32[8,128]{1,0:T(8,128)S(1)}, u32[]{:S(2)}, u32[]{:S(2)}) %collective-permute-start.1) | collective-permute-done | bytes 4128 | tf_op jit(solution)/shard_map/ppermute | solution.py:241
  63.4 4.3 %shard_map.66 = (bf16[448,512]{1,0:T(8,128)(2,1)S(1)}, f32[8,128]{1,0:T(8,128)S(1)}) custom-call(bf16[448,512]{1,0:T(8,128)(2,1)S(1)} %collective-permute-done.refs_0_, f32[8,128]{1,0:T(8,128)S(1)} %collective-permute-done.1.refs_1_, bf16[14,14,2,512]{3,2,1,0:T(2,128)(2,1)S(1)} %bitcast.35, f32[1,128]{1,0:T(1,128)S(1)} %broadcast_in_dim.24.refs_3_, ...), custom_call_target="tpu_custom_call" | custom-call | tf_op jit(solution)/shard_map/pallas_call | solution.py:137
  67.8 17.2 %all_to_all.20 = f16[64,8,128]{2,1,0:T(8,128)(2,1)S(1)} all-to-all(f16[64,8,128]{2,1,0:T(8,128)(2,1)S(1)} %broadcast_in_dim.25), channel_id=1, replica_groups=mesh['section'=8,'replica'=64] {'replica'}, dimensions={0} | all-to-all | bytes 262144 | tf_op jit(solution)/shard_map/all_to_all | solution.py:63
  85.0 0.1 slice_reduce_fusion.1
  85.1 0.1 fusion.3
  85.2 4.3 %shard_map.67 = (bf16[448,512]{1,0:T(8,128)(2,1)S(1)}, f32[8,128]{1,0:T(8,128)S(1)}) custom-call(bf16[448,512]{1,0:T(8,128)(2,1)S(1)} %get-tuple-element.35.refs_0_, f32[8,128]{1,0:T(8,128)S(1)} %pad_maximum_fusion.2.refs_1_, bf16[3,3,512,512]{3,2,1,0:T(8,128)(2,1)} %bitcast.39), custom_call_target="tpu_custom_call" | custom-call | tf_op jit(solution)/shard_map/pallas_call | solution.py:137
  89.5 16.5 %all_to_all.21 = f16[64,8,128]{2,1,0:T(8,128)(2,1)S(1)} all-to-all(f16[64,8,128]{2,1,0:T(8,128)(2,1)S(1)} %broadcast_in_dim.26), channel_id=1, replica_groups=mesh['section'=8,'replica'=64] {'replica'}, dimensions={0} | all-to-all | bytes 262144 | tf_op jit(solution)/shard_map/all_to_all | solution.py:63
  106.1 0.1 slice_reduce_fusion
  106.2 0.1 fusion.1
  106.3 1.5 %shard_map.68 = bf16[2,14,14,2,512]{4,3,2,1,0:T(2,128)(2,1)} custom-call(bf16[448,512]{1,0:T(8,128)(2,1)S(1)} %get-tuple-element.30.refs_0_, bf16[448,512]{1,0:T(8,128)(2,1)S(1)} %get-tuple-element.40.refs_1_, f32[8,128]{1,0:T(8,128)S(1)} %pad_maximum_fusion.1.refs_2_, f32[8,128]{1,0:T(8,128)S(1)} %pad_maximum_fusion.3.refs_3_), custom_call_target="tpu_custom_call" | custom-call | tf_op jit(solution)/shard_map/pallas_call | solution.py:230
  (32 shorter events, 0.3 us)
Async XLA Ops:
  0.0 23.0 %copy-start.1 = (f32[1,2,512]{2,1,0:T(2,128)S(1)}, f32[1,2,512]{2,1,0:T(2,128)}, u32[]{:S(2)}) copy-start(f32[1,2,512]{2,1,0:T(2,128)} %param.10) | copy-start | bytes 12292
  0.0 23.0 %copy-start.2 = (f32[1,2,512]{2,1,0:T(2,128)S(1)}, f32[1,2,512]{2,1,0:T(2,128)}, u32[]{:S(2)}) copy-start(f32[1,2,512]{2,1,0:T(2,128)} %param.11) | copy-start | bytes 12292
  5.7 57.8 %copy-start = (bf16[1,2,14,14,512]{4,1,3,2,0:T(2,128)(2,1)S(1)}, bf16[1,2,14,14,512]{4,1,3,2,0:T(2,128)(2,1)}, u32[]{:S(2)}) copy-start(bf16[1,2,14,14,512]{4,1,3,2,0:T(2,128)(2,1)} %param.7) | copy-start | bytes 1204228
  6.4 29.3 %all-to-all-start = ((f16[64,8,128]{2,1,0:T(8,128)(2,1)}), f16[64,8,128]{2,1,0:T(8,128)(2,1)S(1)}, u32[]{:S(2)}, u32[]{:S(2)}) async-start(f16[64,8,128]{2,1,0:T(8,128)(2,1)} %broadcast_in_dim.22), calls=%async_computation | async-start | bytes 262144 | tf_op jit(solution)/shard_map/all_to_all | solution.py:63
  40.9 17.4 %all-to-all-start.1 = ((f16[64,8,128]{2,1,0:T(8,128)(2,1)}), f16[64,8,128]{2,1,0:T(8,128)(2,1)S(1)}, u32[]{:S(2)}, u32[]{:S(2)}) async-start(f16[64,8,128]{2,1,0:T(8,128)(2,1)} %broadcast_in_dim.23), calls=%async_computation.1 | async-start | bytes 262144 | tf_op jit(solution)/shard_map/all_to_all | solution.py:63
  45.5 17.9 %collective-permute-start = (bf16[448,512]{1,0:T(8,128)(2,1)S(1)}, bf16[448,512]{1,0:T(8,128)(2,1)S(1)}, u32[]{:S(2)}, u32[]{:S(2)}) collective-permute-start(bf16[448,512]{1,0:T(8,128)(2,1)S(1)} %get-tuple-element.30.refs_0_), channel_id=1, source_target_pairs={{0,64},{64,128},{128,192},{192,256},{256,320},{320,384},{384,448},... | collective-permute-start | bytes 1376264 | tf_op jit(solution)/shard_map/ppermute | solution.py:241
  58.5 4.9 %collective-permute-start.1 = (f32[8,128]{1,0:T(8,128)S(1)}, f32[8,128]{1,0:T(8,128)S(1)}, u32[]{:S(2)}, u32[]{:S(2)}) collective-permute-start(f32[8,128]{1,0:T(8,128)S(1)} %pad_maximum_fusion.1.refs_2_), channel_id=1, source_target_pairs={{0,64},{64,128},{128,192},{192,256},{256,320},{320,384},{384,448},... | collective-permute-start | bytes 12296 | tf_op jit(solution)/shard_map/ppermute | solution.py:241

commit v5 on v4

v5 whole, which is shorter than its diff:
```python
import jax
import jax.numpy as jnp
from jax import lax
from jax.experimental import pallas as pl
from jax.experimental.pallas import tpu as pltpu
from jax.sharding import PartitionSpec as P

TICKS = 2
LANES = 128
EPS = 1e-05


class Plan:
    def __init__(self, images, height, width, channels, members):
        self.images, self.height, self.width, self.channels = images, height, width, channels
        self.members = members
        self.wide = 16
        self.line = self.wide * images
        self.rows = height * self.line
        self.groups = channels // LANES
        self.count = images * height * width

    def real_rows(self):
        row = lax.broadcasted_iota(jnp.int32, (self.rows, LANES), 0)
        return row % self.line < self.width * self.images


def fill_shifted(plan, padded):
    line, rows, step = plan.line, plan.rows, plan.images
    padded[0, pl.ds(line, rows), :] = padded[1, pl.ds(line - step, rows), :]
    padded[2, pl.ds(line, rows), :] = padded[1, pl.ds(line + step, rows), :]


def zero_borders(plan, padded):
    border = jnp.zeros((plan.line, plan.channels), jnp.bfloat16)
    for shift in range(3):
        padded[shift, pl.ds(0, plan.line), :] = border
        padded[shift, pl.ds(plan.line + plan.rows, plan.line), :] = border


MIDDLE = [(0, 1), (1, 1), (2, 1)]
SIDES = [(0, 0), (1, 0), (2, 0), (0, 2), (1, 2), (2, 2)]


def convolve_and_measure(plan, padded, tap, stored_ref, packed_ref):
    conv_out = None
    for kh, kw in MIDDLE + SIDES:
        shifted = padded[kw, pl.ds(kh * plan.line, plan.rows), :]
        part = jnp.dot(shifted, tap(kh, kw), preferred_element_type=jnp.float32)
        conv_out = part if conv_out is None else conv_out + part
    stored_ref[...] = conv_out.astype(jnp.bfloat16)
    real = plan.real_rows()
    means, deviations = [], []
    for group in range(plan.groups):
        values = jnp.where(real, conv_out[:, group * LANES : (group + 1) * LANES], 0.0)
        mean = jnp.sum(values, axis=0, keepdims=True) / plan.count
        centred = jnp.where(real, values - mean, 0.0)
        means.append(mean)
        deviations.append(jnp.sqrt(jnp.sum(centred * centred, axis=0, keepdims=True) / plan.count))
    packed_ref[...] = jnp.concatenate(means + deviations, axis=0)


def exchange(plan, packed):
    copies = jnp.broadcast_to(packed.astype(jnp.float16), (plan.members,) + packed.shape)
    return lax.all_to_all(copies, "replica", 0, 0).astype(jnp.float32)


def join(plan, gathered, gain, bias):
    groups = plan.groups
    means, deviations = gathered[:, :groups], gathered[:, groups:]
    mean = jnp.sum(means, axis=0) / plan.members
    apart = means - mean[None]
    var = jnp.sum(deviations * deviations + apart * apart, axis=0) / plan.members
    scale = gain * lax.rsqrt(var + EPS)
    return scale, bias - mean * scale


def normalize_into(plan, stored_ref, scale, offset, write):
    real = plan.real_rows()
    for group in range(plan.groups):
        lanes = slice(group * LANES, (group + 1) * LANES)
        values = stored_ref[:, lanes].astype(jnp.float32) * scale[group : group + 1] + offset[group : group + 1]
        write(lanes, jnp.where(real, jnp.maximum(values, 0.0), 0.0).astype(jnp.bfloat16))


def in_vmem(value):
    return pltpu.with_memory_space_constraint(value, pltpu.VMEM)


def in_hbm(value):
    return pltpu.with_memory_space_constraint(value, pltpu.HBM)


def fetch_taps(kernel_hbm, taps, place, sems):
    return [
        pltpu.make_async_copy(kernel_hbm.at[kh, kw], place(i), sems.at[i]) for i, (kh, kw) in enumerate(taps)
    ]


def layer_outputs(plan):
    return [
        pltpu.VMEM((plan.rows, plan.channels), jnp.bfloat16),
        pltpu.VMEM((2 * plan.groups, LANES), jnp.float32),
    ]


def column(kernel):
    return pltpu.VMEM((3,) + kernel.shape[2:], kernel.dtype)


def padded_scratch(plan):
    return pltpu.VMEM((3, plan.rows + 2 * plan.line, plan.channels), jnp.bfloat16)


WHOLE = pl.BlockSpec(memory_space=pltpu.VMEM)
OUTSIDE = pl.BlockSpec(memory_space=pltpu.HBM)
PARAMS = pltpu.CompilerParams(vmem_limit_bytes=32 << 20)


def conv_layer(plan, body, operands, middle, kernel, following):
    ahead = [] if following is None else [following]

    def run(*refs):
        ins, refs = refs[: len(operands)], refs[len(operands) :]
        middle_ref, kernel_hbm, refs = refs[0], refs[1], refs[2:]
        next_hbm, refs = refs[: len(ahead)], refs[len(ahead) :]
        stored_ref, packed_ref, refs = refs[0], refs[1], refs[2:]
        next_middle, refs = refs[: len(ahead)], refs[len(ahead) :]
        padded, sides, sems, next_sems = refs
        copies = fetch_taps(kernel_hbm, SIDES, lambda i: sides.at[i], sems)
        for source, target in zip(next_hbm, next_middle):
            copies += fetch_taps(source, MIDDLE, lambda i: target.at[i], next_sems)
        for copy in copies:
            copy.start()
        zero_borders(plan, padded)
        body(padded, *ins)
        fill_shifted(plan, padded)

        def tap(kh, kw):
            if kw == 1:
                return middle_ref[kh]
            place = SIDES.index((kh, kw))
            copies[place].wait()
            return sides[place]

        convolve_and_measure(plan, padded, tap, stored_ref, packed_ref)
        for copy in copies[len(SIDES) :]:
            copy.wait()

    return pl.pallas_call(
        run,
        in_specs=[WHOLE] * (len(operands) + 1) + [OUTSIDE] * (1 + len(ahead)),
        out_specs=[WHOLE] * (2 + len(ahead)),
        out_shape=layer_outputs(plan) + [column(kernel) for kernel in ahead],
        scratch_shapes=[
            padded_scratch(plan),
            pltpu.VMEM((len(SIDES),) + kernel.shape[2:], kernel.dtype),
            pltpu.SemaphoreType.DMA((len(SIDES),)),
            pltpu.SemaphoreType.DMA((len(MIDDLE),)),
        ],
        compiler_params=PARAMS,
    )(*operands, in_vmem(middle), in_hbm(kernel), *map(in_hbm, ahead))


def inner(plan):
    return pl.ds(plan.line, plan.rows)


def spread_lines(plan, maps_ref, write):
    real = plan.width * plan.images
    blank = jnp.zeros((plan.line - real, plan.channels), jnp.bfloat16)
    for row in range(plan.height):
        write(row * plan.line, maps_ref[row].reshape(real, plan.channels))
        write(row * plan.line + real, blank)


def opening_layer(plan, maps, kernel, following):
    def run(maps_hbm, kernel_hbm, next_hbm, stored_ref, packed_ref, next_middle, *scratch):
        maps_vmem, map_sem, padded, filters, sems, next_sems = scratch
        fetch = pltpu.make_async_copy(maps_hbm, maps_vmem, map_sem)
        fetch.start()
        copies = fetch_taps(kernel_hbm, MIDDLE + SIDES, lambda i: filters.at[i], sems)
        ahead = fetch_taps(next_hbm, MIDDLE, lambda i: next_middle.at[i], next_sems)
        for copy in copies[: len(MIDDLE)]:
            copy.start()
        zero_borders(plan, padded)
        fetch.wait()
        for copy in copies[len(MIDDLE) :] + ahead:
            copy.start()

        def write(start, rows):
            padded[1, pl.ds(plan.line + start, rows.shape[0]), :] = rows

        spread_lines(plan, maps_vmem, write)
        fill_shifted(plan, padded)

        def tap(kh, kw):
            place = (MIDDLE + SIDES).index((kh, kw))
            copies[place].wait()
            return filters[place]

        convolve_and_measure(plan, padded, tap, stored_ref, packed_ref)
        for copy in ahead:
            copy.wait()

    return pl.pallas_call(
        run,
        in_specs=[OUTSIDE] * 3,
        out_specs=[WHOLE] * 3,
        out_shape=layer_outputs(plan) + [column(following)],
        scratch_shapes=[
            pltpu.VMEM(maps.shape, maps.dtype),
            pltpu.SemaphoreType.DMA(()),
            padded_scratch(plan),
            pltpu.VMEM((9,) + kernel.shape[2:], kernel.dtype),
            pltpu.SemaphoreType.DMA((9,)),
            pltpu.SemaphoreType.DMA((len(MIDDLE),)),
        ],
        compiler_params=PARAMS,
    )(in_hbm(maps), in_hbm(kernel), in_hbm(following))


def layer_of_stored(plan, stored, gathered, gain, bias, middle, kernel, following):
    def body(padded, stored_ref, gathered_ref, gain_ref, bias_ref):
        scale, offset = join(plan, gathered_ref[...], gain_ref[...], bias_ref[...])

        def write(lanes, values):
            padded[1, inner(plan), lanes] = values

        normalize_into(plan, stored_ref, scale, offset, write)

    return conv_layer(plan, body, [in_vmem(stored), gathered, gain, bias], middle, kernel, following)


def layer_of_moved(plan, stored, terms, maps, is_first, middle, kernel, following):
    def body(padded, stored_ref, terms_ref, maps_ref, first_ref):
        first = jnp.broadcast_to(first_ref[...], (plan.rows, LANES)) > 0.5

        def write(lanes, values):
            arrived = padded[1, inner(plan), lanes]
            padded[1, inner(plan), lanes] = jnp.where(first, arrived, values)

        def write_line(start, rows):
            padded[1, pl.ds(plan.line + start, rows.shape[0]), :] = rows

        spread_lines(plan, maps_ref, write_line)
        terms = terms_ref[...]
        normalize_into(plan, stored_ref, terms[: plan.groups], terms[plan.groups :], write)

    operands = [in_vmem(stored), terms, in_vmem(maps), is_first]
    return conv_layer(plan, body, operands, middle, kernel, following)


def finish(plan, stored, terms, gathered, gain, bias):
    shape = (TICKS, plan.height, plan.width, plan.images, plan.channels)

    def run(*refs):
        out_ref = refs[-1]
        for tick in range(TICKS):

            def write(lanes, values, tick=tick):
                for row in range(plan.height):
                    line = values[row * plan.line : row * plan.line + plan.width * plan.images]
                    out_ref[tick, row, :, :, lanes] = line.reshape(plan.width, plan.images, LANES)

            if tick + 1 < TICKS:
                known = refs[TICKS + tick][...]
                scale, offset = known[: plan.groups], known[plan.groups :]
            else:
                scale, offset = join(plan, *(ref[...] for ref in refs[2 * TICKS - 1 : -1]))
            normalize_into(plan, refs[tick], scale, offset, write)

    operands = [in_vmem(value) for value in stored] + terms + [gathered, gain, bias]
    return pl.pallas_call(
        run,
        in_specs=[WHOLE] * len(operands),
        out_specs=WHOLE,
        out_shape=pltpu.HBM(shape, jnp.bfloat16),
        compiler_params=PARAMS,
    )(*operands)


def from_behind(value, axis):
    pairs = [(i, i + 1) for i in range(lax.axis_size(axis) - 1)]
    return lax.ppermute(value, axis, pairs)


def body(
    pending_section_entries,
    arriving_microsets,
    opening_filter_kernel,
    closing_filter_kernel,
    stretch_factors,
    shift_terms,
):
    _, images, height, width, channels = pending_section_entries.shape
    plan = Plan(images, height, width, channels, lax.axis_size("replica"))
    first_kernel = opening_filter_kernel[0]
    second_kernel = closing_filter_kernel[0]
    is_first = jnp.broadcast_to((lax.axis_index("section") == 0).astype(jnp.float32), (1, LANES))
    order = (1, 2, 0, 3)
    maps = jnp.transpose(pending_section_entries[0], order)
    stored, packed, middle = opening_layer(plan, maps, first_kernel, second_kernel)
    kept, kept_terms = [], []
    for tick in range(TICKS):
        gathered = exchange(plan, packed)
        if tick == 0:
            gathered, gains, biases = lax.optimization_barrier((gathered, stretch_factors, shift_terms))
            gain = gains[0].reshape(2, plan.groups, LANES)
            bias = biases[0].reshape(2, plan.groups, LANES)
        last = tick + 1 == TICKS
        stored, packed, *middle = layer_of_stored(
            plan, stored, gathered, gain[0], bias[0], middle, second_kernel, None if last else first_kernel
        )
        kept.append(stored)
        if last:
            break
        moved = from_behind(stored, "section")
        terms = jnp.concatenate(join(plan, exchange(plan, packed), gain[1], bias[1]), axis=0)
        kept_terms.append(terms)
        terms = from_behind(terms, "section")
        arriving = jnp.transpose(arriving_microsets[tick], order)
        stored, packed, middle = layer_of_moved(
            plan, moved, terms, arriving, is_first, middle[0], first_kernel, second_kernel
        )
    result = finish(plan, kept, kept_terms, exchange(plan, packed), gain[1], bias[1])
    return jnp.transpose(result, (0, 3, 1, 2, 4))[None]


def solution(mesh):
    in_specs = (
        P("section", "replica", None, None, None),
        P(None, "replica", None, None, None),
        P("section", None, None, None, None),
        P("section", None, None, None, None),
        P("section", None, None),
        P("section", None, None),
    )
    out_specs = P("section", None, "replica", None, None, None)
    return jax.shard_map(body, mesh=mesh, in_specs=in_specs, out_specs=out_specs, check_vma=False)
```

time: 108 us -> 105 us (0.972)
  blocking collectives: 33.7 us -> 62.8 us
  starting transfers between devices: 25 us -> 8.46 us
  waiting for transfers between devices: 26.5 us -> 13.8 us
  Pallas kernels: 20.1 us -> 18.9 us
    all_to_all x2 -> x3, blocking collectives: 33.7 us -> 62.8 us  [exchange(): return lax.all_to_all(copies, 'replica', 0, 0).astype(jnp.float32)]
    all_to_all x2 -> x1, starting transfers between devices: 21.2 us -> 4.62 us  [exchange(): return lax.all_to_all(copies, 'replica', 0, 0).astype(jnp.float32)]
    all_to_all x2 -> x1, waiting for transfers between devices: 23.5 us -> 10.8 us  [exchange(): return lax.all_to_all(copies, 'replica', 0, 0).astype(jnp.float32)]
    pallas_call x5, Pallas kernels: 20.1 us -> 18.9 us  [the longest x3 12.4 us: conv_layer(): pl.pallas_call(run, in_specs=[WHOLE] * (len(operands) + 1) + [OUTSIDE] *...]
  transfers between devices with their start and end apart: 4 -> 3, of which waited for: 3 -> 2; matrix products, arithmetic and copies ran while one was open for 0% -> 0% of each run, Pallas kernels for 0% -> 0%
where the time goes in v5:
time: 105 us
  blocking collectives  62.8 us (60%)
  Pallas kernels  18.9 us (18%)
  waiting for transfers between devices  13.8 us (13%)
  starting transfers between devices  8.46 us (8%)
    all_to_all x3, blocking collectives, exchange(): return lax.all_to_all(copies, 'replica', 0, 0).astype(jnp.float32)  62.8 us
    pallas_call x3, Pallas kernels, conv_layer(): pl.pallas_call(run, in_specs=[WHOLE] * (len(operands) + 1) + [OUTSIDE] *...  12.4 us
    all_to_all x1, waiting for transfers between devices, exchange(): return lax.all_to_all(copies, 'replica', 0, 0).astype(jnp.float32)  10.8 us
    pallas_call x1, Pallas kernels, opening_layer(): pl.pallas_call(run, in_specs=[OUTSIDE] * 3, out_specs=[WHOLE] * 3, out_sh...  4.75 us
    all_to_all x1, starting transfers between devices, exchange(): return lax.all_to_all(copies, 'replica', 0, 0).astype(jnp.float32)  4.62 us
    ppermute x2, starting transfers between devices, from_behind(): return lax.ppermute(value, axis, pairs)  3.84 us
    ppermute x2, waiting for transfers between devices, from_behind(): return lax.ppermute(value, axis, pairs)  2.99 us
  transfers between devices with their start and end apart: 3, of which 2 were waited for; matrix products, arithmetic and copies ran while one was open for 0% of the time, Pallas kernels for 0%

profile of v5, /device:TPU:2, one launch (start us, length us, event | category | flops | bytes accessed | tf_op | source)
XLA Modules:
  0.0 105.1 jit_solution(14634635707589689135)
XLA Ops:
  0.0 0.0 copy-start.1
  0.0 0.0 copy-start.2
  0.0 4.8 %shard_map.64 = (bf16[448,512]{1,0:T(8,128)(2,1)S(1)}, f32[8,128]{1,0:T(8,128)S(1)}, bf16[3,512,512]{2,1,0:T(8,128)(2,1)S(1)}) custom-call(bf16[14,14,2,512]{3,2,1,0:T(2,128)(2,1)} %bitcast.31, bf16[3,3,512,512]{3,2,1,0:T(8,128)(2,1)} %bitcast.28, bf16[3,3,512,512]{3,2,1,0:T(8,128)(2,1)} %bitcast.24), custom_call_target="tpu_custom_call" | custom-call | tf_op jit(solution)/shard_map/pallas_call | solution.py:206
  4.8 29.1 %all_to_all.20 = f16[64,8,128]{2,1,0:T(8,128)(2,1)S(1)} all-to-all(f16[64,8,128]{2,1,0:T(8,128)(2,1)S(1)} %broadcast_in_dim.19), channel_id=1, replica_groups=mesh['section'=8,'replica'=64] {'replica'}, dimensions={0} | all-to-all | bytes 262144 | tf_op jit(solution)/shard_map/all_to_all | solution.py:65
  33.9 0.0 copy-done.1
  33.9 0.0 copy-done.2
  34.0 0.0 copy-start
  34.0 4.2 %shard_map.65 = (bf16[448,512]{1,0:T(8,128)(2,1)S(1)}, f32[8,128]{1,0:T(8,128)S(1)}, bf16[3,512,512]{2,1,0:T(8,128)(2,1)S(1)}) custom-call(bf16[448,512]{1,0:T(8,128)(2,1)S(1)} %get-tuple-element.19.refs_0_, f32[64,8,128]{2,1,0:T(8,128)S(1)} %convert_element_type.28.refs_1_, f32[4,128]{1,0:T(4,128)S(1)} %bitcast.20, f32[4,128]{1,0:T(4,128)S(1)} %bitcast.22, ...), custom_call_target="tpu_custom_call" | custom-call | tf_op jit(solution)/shard_map/pallas_call | solution.py:150
  38.2 0.7 broadcast_in_dim.20
  38.8 4.6 %all-to-all-start.1 = ((f16[64,8,128]{2,1,0:T(8,128)(2,1)}), f16[64,8,128]{2,1,0:T(8,128)(2,1)S(1)}, u32[]{:S(2)}, u32[]{:S(2)}) async-start(f16[64,8,128]{2,1,0:T(8,128)(2,1)} %broadcast_in_dim.20), calls=%async_computation.1 | async-start | bytes 262144 | tf_op jit(solution)/shard_map/all_to_all | solution.py:65
  43.5 1.9 %collective-permute-start = (bf16[448,512]{1,0:T(8,128)(2,1)S(1)}, bf16[448,512]{1,0:T(8,128)(2,1)S(1)}, u32[]{:S(2)}, u32[]{:S(2)}) collective-permute-start(bf16[448,512]{1,0:T(8,128)(2,1)S(1)} %get-tuple-element.25.refs_0_), channel_id=1, source_target_pairs={{0,64},{64,128},{128,192},{192,256},{256,320},{320,384},{384,448},... | collective-permute-start | bytes 1376264 | tf_op jit(solution)/shard_map/ppermute | solution.py:285
  45.4 10.8 %all-to-all-done.1 = f16[64,8,128]{2,1,0:T(8,128)(2,1)S(1)} async-done(((f16[64,8,128]{2,1,0:T(8,128)(2,1)}), f16[64,8,128]{2,1,0:T(8,128)(2,1)S(1)}, u32[]{:S(2)}, u32[]{:S(2)}) %all-to-all-start.1) | async-done | bytes 131104 | tf_op jit(solution)/shard_map/all_to_all | solution.py:65
  56.2 0.1 slice_reduce_fusion
  56.3 0.1 fusion.1
  56.4 1.9 %collective-permute-start.1 = (f32[8,128]{1,0:T(8,128)S(1)}, f32[8,128]{1,0:T(8,128)S(1)}, u32[]{:S(2)}, u32[]{:S(2)}) collective-permute-start(f32[8,128]{1,0:T(8,128)S(1)} %pad_maximum_fusion.refs_2_), channel_id=1, source_target_pairs={{0,64},{64,128},{128,192},{192,256},{256,320},{320,384},{384,448},... | collective-permute-start | bytes 12296 | tf_op jit(solution)/shard_map/ppermute | solution.py:285
  58.4 3.0 %collective-permute-done.1.refs_1_ = f32[8,128]{1,0:T(8,128)S(1)} collective-permute-done((f32[8,128]{1,0:T(8,128)S(1)}, f32[8,128]{1,0:T(8,128)S(1)}, u32[]{:S(2)}, u32[]{:S(2)}) %collective-permute-start.1) | collective-permute-done | bytes 4128 | tf_op jit(solution)/shard_map/ppermute | solution.py:285
  61.4 0.0 collective-permute-done.refs_0_
  61.4 0.0 copy-done
  61.4 4.1 %shard_map.66 = (bf16[448,512]{1,0:T(8,128)(2,1)S(1)}, f32[8,128]{1,0:T(8,128)S(1)}, bf16[3,512,512]{2,1,0:T(8,128)(2,1)S(1)}) custom-call(bf16[448,512]{1,0:T(8,128)(2,1)S(1)} %collective-permute-done.refs_0_, f32[8,128]{1,0:T(8,128)S(1)} %collective-permute-done.1.refs_1_, bf16[14,14,2,512]{3,2,1,0:T(2,128)(2,1)S(1)} %bitcast.15, ...), custom_call_target="tpu_custom_call" | custom-call | tf_op jit(solution)/shard_map/pallas_call | solution.py:150
  65.5 17.2 %all_to_all.21 = f16[64,8,128]{2,1,0:T(8,128)(2,1)S(1)} all-to-all(f16[64,8,128]{2,1,0:T(8,128)(2,1)S(1)} %broadcast_in_dim.22), channel_id=1, replica_groups=mesh['section'=8,'replica'=64] {'replica'}, dimensions={0} | all-to-all | bytes 262144 | tf_op jit(solution)/shard_map/all_to_all | solution.py:65
  82.7 4.1 %shard_map.67 = (bf16[448,512]{1,0:T(8,128)(2,1)S(1)}, f32[8,128]{1,0:T(8,128)S(1)}) custom-call(bf16[448,512]{1,0:T(8,128)(2,1)S(1)} %get-tuple-element.28.refs_0_, f32[64,8,128]{2,1,0:T(8,128)S(1)} %convert_element_type.33.refs_1_, f32[4,128]{1,0:T(4,128)S(1)} %bitcast.21, f32[4,128]{1,0:T(4,128)S(1)} %bitcast.23, ...), custom_call_target="tpu_custom_call" | custom-call | tf_op jit(solution)/shard_map/pallas_call | solution.py:150
  86.9 16.5 %all_to_all.22 = f16[64,8,128]{2,1,0:T(8,128)(2,1)S(1)} all-to-all(f16[64,8,128]{2,1,0:T(8,128)(2,1)S(1)} %broadcast_in_dim.23), channel_id=1, replica_groups=mesh['section'=8,'replica'=64] {'replica'}, dimensions={0} | all-to-all | bytes 262144 | tf_op jit(solution)/shard_map/all_to_all | solution.py:65
  103.5 1.7 %shard_map.68 = bf16[2,14,14,2,512]{4,3,2,1,0:T(2,128)(2,1)} custom-call(bf16[448,512]{1,0:T(8,128)(2,1)S(1)} %get-tuple-element.25.refs_0_, bf16[448,512]{1,0:T(8,128)(2,1)S(1)} %get-tuple-element.31.refs_1_, f32[8,128]{1,0:T(8,128)S(1)} %pad_maximum_fusion.refs_2_, f32[64,8,128]{2,1,0:T(8,128)S(1)} %convert_element_type.35.refs_3_, f32[4,128]{1,0:T(4,128)S(1)} %bitcast.17, ...), custom_call_target="tpu_custom_call" | custom-call | tf_op jit(solution)/shard_map/pallas_call | solution.py:274
  (16 shorter events, 0.2 us)
Async XLA Ops:
  0.0 33.9 %copy-start.1 = (f32[1,2,512]{2,1,0:T(2,128)S(1)}, f32[1,2,512]{2,1,0:T(2,128)}, u32[]{:S(2)}) copy-start(f32[1,2,512]{2,1,0:T(2,128)} %param.10) | copy-start | bytes 12292
  0.0 33.9 %copy-start.2 = (f32[1,2,512]{2,1,0:T(2,128)S(1)}, f32[1,2,512]{2,1,0:T(2,128)}, u32[]{:S(2)}) copy-start(f32[1,2,512]{2,1,0:T(2,128)} %param.11) | copy-start | bytes 12292
  34.0 27.4 %copy-start = (bf16[1,2,14,14,512]{4,1,3,2,0:T(2,128)(2,1)S(1)}, bf16[1,2,14,14,512]{4,1,3,2,0:T(2,128)(2,1)}, u32[]{:S(2)}) copy-start(bf16[1,2,14,14,512]{4,1,3,2,0:T(2,128)(2,1)} %param.7) | copy-start | bytes 1204228
  38.8 17.4 %all-to-all-start.1 = ((f16[64,8,128]{2,1,0:T(8,128)(2,1)}), f16[64,8,128]{2,1,0:T(8,128)(2,1)S(1)}, u32[]{:S(2)}, u32[]{:S(2)}) async-start(f16[64,8,128]{2,1,0:T(8,128)(2,1)} %broadcast_in_dim.20), calls=%async_computation.1 | async-start | bytes 262144 | tf_op jit(solution)/shard_map/all_to_all | solution.py:65
  43.5 17.9 %collective-permute-start = (bf16[448,512]{1,0:T(8,128)(2,1)S(1)}, bf16[448,512]{1,0:T(8,128)(2,1)S(1)}, u32[]{:S(2)}, u32[]{:S(2)}) collective-permute-start(bf16[448,512]{1,0:T(8,128)(2,1)S(1)} %get-tuple-element.25.refs_0_), channel_id=1, source_target_pairs={{0,64},{64,128},{128,192},{192,256},{256,320},{320,384},{384,448},... | collective-permute-start | bytes 1376264 | tf_op jit(solution)/shard_map/ppermute | solution.py:285
  56.4 4.9 %collective-permute-start.1 = (f32[8,128]{1,0:T(8,128)S(1)}, f32[8,128]{1,0:T(8,128)S(1)}, u32[]{:S(2)}, u32[]{:S(2)}) collective-permute-start(f32[8,128]{1,0:T(8,128)S(1)} %pad_maximum_fusion.refs_2_), channel_id=1, source_target_pairs={{0,64},{64,128},{128,192},{192,256},{256,320},{320,384},{384,448},... | collective-permute-start | bytes 12296 | tf_op jit(solution)/shard_map/ppermute | solution.py:285

commit v6 on v5

--- a/solution.py
+++ b/solution.py
@@ -38,13 +38,14 @@
         padded[shift, pl.ds(plan.line + plan.rows, plan.line), :] = border
 
 
-MIDDLE = [(0, 1), (1, 1), (2, 1)]
-SIDES = [(0, 0), (1, 0), (2, 0), (0, 2), (1, 2), (2, 2)]
+TAPS = [(0, 1), (1, 1), (2, 1), (0, 0), (1, 0), (2, 0), (0, 2), (1, 2), (2, 2)]
+OPENING_AHEAD = 3
+CLOSING_AHEAD = 4
 
 
 def convolve_and_measure(plan, padded, tap, stored_ref, packed_ref):
     conv_out = None
-    for kh, kw in MIDDLE + SIDES:
+    for kh, kw in TAPS:
         shifted = padded[kw, pl.ds(kh * plan.line, plan.rows), :]
         part = jnp.dot(shifted, tap(kh, kw), preferred_element_type=jnp.float32)
         conv_out = part if conv_out is None else conv_out + part
@@ -104,8 +105,8 @@
     ]
 
 
-def column(kernel):
-    return pltpu.VMEM((3,) + kernel.shape[2:], kernel.dtype)
+def filters_in_vmem(taps, kernel):
+    return pltpu.VMEM((len(taps),) + kernel.shape[2:], kernel.dtype)
 
 
 def padded_scratch(plan):
@@ -117,19 +118,20 @@
 PARAMS = pltpu.CompilerParams(vmem_limit_bytes=32 << 20)
 
 
-def conv_layer(plan, body, operands, middle, kernel, following):
+def conv_layer(plan, body, operands, early, kernel, following, count):
     ahead = [] if following is None else [following]
+    first, late, upcoming = TAPS[: early.shape[0]], TAPS[early.shape[0] :], TAPS[:count]
 
     def run(*refs):
         ins, refs = refs[: len(operands)], refs[len(operands) :]
-        middle_ref, kernel_hbm, refs = refs[0], refs[1], refs[2:]
+        early_ref, kernel_hbm, refs = refs[0], refs[1], refs[2:]
         next_hbm, refs = refs[: len(ahead)], refs[len(ahead) :]
         stored_ref, packed_ref, refs = refs[0], refs[1], refs[2:]
-        next_middle, refs = refs[: len(ahead)], refs[len(ahead) :]
+        next_early, refs = refs[: len(ahead)], refs[len(ahead) :]
         padded, sides, sems, next_sems = refs
-        copies = fetch_taps(kernel_hbm, SIDES, lambda i: sides.at[i], sems)
-        for source, target in zip(next_hbm, next_middle):
-            copies += fetch_taps(source, MIDDLE, lambda i: target.at[i], next_sems)
+        copies = fetch_taps(kernel_hbm, late, lambda i: sides.at[i], sems)
+        for source, target in zip(next_hbm, next_early):
+            copies += fetch_taps(source, upcoming, lambda i: target.at[i], next_sems)
         for copy in copies:
             copy.start()
         zero_borders(plan, padded)
@@ -137,29 +139,29 @@
         fill_shifted(plan, padded)
 
         def tap(kh, kw):
-            if kw == 1:
-                return middle_ref[kh]
-            place = SIDES.index((kh, kw))
+            if (kh, kw) in first:
+                return early_ref[first.index((kh, kw))]
+            place = late.index((kh, kw))
             copies[place].wait()
             return sides[place]
 
         convolve_and_measure(plan, padded, tap, stored_ref, packed_ref)
-        for copy in copies[len(SIDES) :]:
+        for copy in copies[len(late) :]:
             copy.wait()
 
     return pl.pallas_call(
         run,
         in_specs=[WHOLE] * (len(operands) + 1) + [OUTSIDE] * (1 + len(ahead)),
         out_specs=[WHOLE] * (2 + len(ahead)),
-        out_shape=layer_outputs(plan) + [column(kernel) for kernel in ahead],
+        out_shape=layer_outputs(plan) + [filters_in_vmem(upcoming, kernel) for kernel in ahead],
         scratch_shapes=[
             padded_scratch(plan),
-            pltpu.VMEM((len(SIDES),) + kernel.shape[2:], kernel.dtype),
-            pltpu.SemaphoreType.DMA((len(SIDES),)),
-            pltpu.SemaphoreType.DMA((len(MIDDLE),)),
+            filters_in_vmem(late, kernel),
+            pltpu.SemaphoreType.DMA((len(late),)),
+            pltpu.SemaphoreType.DMA((max(count, 1),)),
         ],
         compiler_params=PARAMS,
-    )(*operands, in_vmem(middle), in_hbm(kernel), *map(in_hbm, ahead))
+    )(*operands, in_vmem(early), in_hbm(kernel), *map(in_hbm, ahead))
 
 
 def inner(plan):
@@ -174,18 +176,18 @@
         write(row * plan.line + real, blank)
 
 
-def opening_layer(plan, maps, kernel, following):
-    def run(maps_hbm, kernel_hbm, next_hbm, stored_ref, packed_ref, next_middle, *scratch):
+def opening_layer(plan, maps, kernel, following, count):
+    def run(maps_hbm, kernel_hbm, next_hbm, stored_ref, packed_ref, next_early, *scratch):
         maps_vmem, map_sem, padded, filters, sems, next_sems = scratch
         fetch = pltpu.make_async_copy(maps_hbm, maps_vmem, map_sem)
         fetch.start()
-        copies = fetch_taps(kernel_hbm, MIDDLE + SIDES, lambda i: filters.at[i], sems)
-        ahead = fetch_taps(next_hbm, MIDDLE, lambda i: next_middle.at[i], next_sems)
-        for copy in copies[: len(MIDDLE)]:
+        copies = fetch_taps(kernel_hbm, TAPS, lambda i: filters.at[i], sems)
+        ahead = fetch_taps(next_hbm, TAPS[:count], lambda i: next_early.at[i], next_sems)
+        for copy in copies[:3]:
             copy.start()
         zero_borders(plan, padded)
         fetch.wait()
-        for copy in copies[len(MIDDLE) :] + ahead:
+        for copy in copies[3:] + ahead:
             copy.start()
 
         def write(start, rows):
@@ -195,7 +197,7 @@
         fill_shifted(plan, padded)
 
         def tap(kh, kw):
-            place = (MIDDLE + SIDES).index((kh, kw))
+            place = TAPS.index((kh, kw))
             copies[place].wait()
             return filters[place]
 
@@ -207,20 +209,20 @@
         run,
         in_specs=[OUTSIDE] * 3,
         out_specs=[WHOLE] * 3,
-        out_shape=layer_outputs(plan) + [column(following)],
+        out_shape=layer_outputs(plan) + [filters_in_vmem(TAPS[:count], following)],
         scratch_shapes=[
             pltpu.VMEM(maps.shape, maps.dtype),
             pltpu.SemaphoreType.DMA(()),
             padded_scratch(plan),
-            pltpu.VMEM((9,) + kernel.shape[2:], kernel.dtype),
-            pltpu.SemaphoreType.DMA((9,)),
-            pltpu.SemaphoreType.DMA((len(MIDDLE),)),
+            filters_in_vmem(TAPS, kernel),
+            pltpu.SemaphoreType.DMA((len(TAPS),)),
+            pltpu.SemaphoreType.DMA((count,)),
         ],
         compiler_params=PARAMS,
     )(in_hbm(maps), in_hbm(kernel), in_hbm(following))
 
 
-def layer_of_stored(plan, stored, gathered, gain, bias, middle, kernel, following):
+def layer_of_stored(plan, stored, gathered, gain, bias, early, kernel, following, count):
     def body(padded, stored_ref, gathered_ref, gain_ref, bias_ref):
         scale, offset = join(plan, gathered_ref[...], gain_ref[...], bias_ref[...])
 
@@ -229,10 +231,10 @@
 
         normalize_into(plan, stored_ref, scale, offset, write)
 
-    return conv_layer(plan, body, [in_vmem(stored), gathered, gain, bias], middle, kernel, following)
-
-
-def layer_of_moved(plan, stored, terms, maps, is_first, middle, kernel, following):
+    return conv_layer(plan, body, [in_vmem(stored), gathered, gain, bias], early, kernel, following, count)
+
+
+def layer_of_moved(plan, stored, terms, maps, is_first, early, kernel, following, count):
     def body(padded, stored_ref, terms_ref, maps_ref, first_ref):
         first = jnp.broadcast_to(first_ref[...], (plan.rows, LANES)) > 0.5
 
@@ -248,14 +250,15 @@
         normalize_into(plan, stored_ref, terms[: plan.groups], terms[plan.groups :], write)
 
     operands = [in_vmem(stored), terms, in_vmem(maps), is_first]
-    return conv_layer(plan, body, operands, middle, kernel, following)
+    return conv_layer(plan, body, operands, early, kernel, following, count)
 
 
 def finish(plan, stored, terms, gathered, gain, bias):
     shape = (TICKS, plan.height, plan.width, plan.images, plan.channels)
 
     def run(*refs):
-        out_ref = refs[-1]
+        *refs, out_hbm, out_ref, sems = refs
+        copies = []
         for tick in range(TICKS):
 
             def write(lanes, values, tick=tick):
@@ -267,22 +270,27 @@
                 known = refs[TICKS + tick][...]
                 scale, offset = known[: plan.groups], known[plan.groups :]
             else:
-                scale, offset = join(plan, *(ref[...] for ref in refs[2 * TICKS - 1 : -1]))
+                scale, offset = join(plan, *(ref[...] for ref in refs[2 * TICKS - 1 :]))
             normalize_into(plan, refs[tick], scale, offset, write)
+            copies.append(pltpu.make_async_copy(out_ref.at[tick], out_hbm.at[tick], sems.at[tick]))
+            copies[-1].start()
+        for copy in copies:
+            copy.wait()
 
     operands = [in_vmem(value) for value in stored] + terms + [gathered, gain, bias]
     return pl.pallas_call(
         run,
         in_specs=[WHOLE] * len(operands),
-        out_specs=WHOLE,
+        out_specs=OUTSIDE,
         out_shape=pltpu.HBM(shape, jnp.bfloat16),
+        scratch_shapes=[pltpu.VMEM(shape, jnp.bfloat16), pltpu.SemaphoreType.DMA((TICKS,))],
         compiler_params=PARAMS,
     )(*operands)
 
 
 def from_behind(value, axis):
-    pairs = [(i, i + 1) for i in range(lax.axis_size(axis) - 1)]
-    return lax.ppermute(value, axis, pairs)
+    length = lax.axis_size(axis)
+    return lax.ppermute(value, axis, [(i, (i + 1) % length) for i in range(length)])
 
 
 def body(
@@ -300,7 +308,7 @@
     is_first = jnp.broadcast_to((lax.axis_index("section") == 0).astype(jnp.float32), (1, LANES))
     order = (1, 2, 0, 3)
     maps = jnp.transpose(pending_section_entries[0], order)
-    stored, packed, middle = opening_layer(plan, maps, first_kernel, second_kernel)
+    stored, packed, early = opening_layer(plan, maps, first_kernel, second_kernel, CLOSING_AHEAD)
     kept, kept_terms = [], []
     for tick in range(TICKS):
         gathered = exchange(plan, packed)
@@ -309,8 +317,9 @@
             gain = gains[0].reshape(2, plan.groups, LANES)
             bias = biases[0].reshape(2, plan.groups, LANES)
         last = tick + 1 == TICKS
-        stored, packed, *middle = layer_of_stored(
-            plan, stored, gathered, gain[0], bias[0], middle, second_kernel, None if last else first_kernel
+        ahead = (None, 0) if last else (first_kernel, OPENING_AHEAD)
+        stored, packed, *early = layer_of_stored(
+            plan, stored, gathered, gain[0], bias[0], early, second_kernel, *ahead
         )
         kept.append(stored)
         if last:
@@ -320,8 +329,9 @@
         kept_terms.append(terms)
         terms = from_behind(terms, "section")
         arriving = jnp.transpose(arriving_microsets[tick], order)
-        stored, packed, middle = layer_of_moved(
-            plan, moved, terms, arriving, is_first, middle[0], first_kernel, second_kernel
+        ahead = (second_kernel, CLOSING_AHEAD)
+        stored, packed, early = layer_of_moved(
+            plan, moved, terms, arriving, is_first, early[0], first_kernel, *ahead
         )
     result = finish(plan, kept, kept_terms, exchange(plan, packed), gain[1], bias[1])
     return jnp.transpose(result, (0, 3, 1, 2, 4))[None]

time: 105 us -> 102 us (0.971)
  the two profiles are of different devices: /device:TPU:2 before, /device:TPU:8 now
where the time goes in v6:
time: 102 us; the launch traced here: 101 us
  blocking collectives  62 us (61%)
  Pallas kernels  16.7 us (16%)
  waiting for transfers between devices  16.2 us (16%)
  starting transfers between devices  5.36 us (5%)
    all_to_all x3, blocking collectives, exchange(): return lax.all_to_all(copies, 'replica', 0, 0).astype(jnp.float32)  62 us
    all_to_all x1, waiting for transfers between devices, exchange(): return lax.all_to_all(copies, 'replica', 0, 0).astype(jnp.float32)  12 us
    pallas_call x3, Pallas kernels, conv_layer(): pl.pallas_call(run, in_specs=[WHOLE] * (len(operands) + 1) + [OUTSIDE] *...  10.4 us
    all_to_all x1, starting transfers between devices, exchange(): return lax.all_to_all(copies, 'replica', 0, 0).astype(jnp.float32)  5.33 us
    pallas_call x1, Pallas kernels, opening_layer(): pl.pallas_call(run, in_specs=[OUTSIDE] * 3, out_specs=[WHOLE] * 3, out_sh...  4.76 us
    ppermute x2, waiting for transfers between devices, from_behind(): lax.ppermute(value, axis, [(i, (i + 1) % length) for i in range(length)])  4.23 us
  transfers between devices with their start and end apart: 3, of which 2 were waited for; matrix products, arithmetic and copies ran while one was open for 0% of the time, Pallas kernels for 0%

profile of v6, /device:TPU:8, one launch (start us, length us, event | category | flops | bytes accessed | tf_op | source)
XLA Modules:
  0.0 101.5 jit_solution(17363934427102008837)
XLA Ops:
  0.0 0.0 copy-start.1
  0.0 0.0 copy-start.2
  0.0 4.8 %shard_map.64 = (bf16[448,512]{1,0:T(8,128)(2,1)S(1)}, f32[8,128]{1,0:T(8,128)S(1)}, bf16[4,512,512]{2,1,0:T(8,128)(2,1)S(1)}) custom-call(bf16[14,14,2,512]{3,2,1,0:T(2,128)(2,1)} %bitcast.31, bf16[3,3,512,512]{3,2,1,0:T(8,128)(2,1)} %bitcast.28, bf16[3,3,512,512]{3,2,1,0:T(8,128)(2,1)} %bitcast.24), custom_call_target="tpu_custom_call" | custom-call | tf_op jit(solution)/shard_map/pallas_call | solution.py:208
  4.8 28.3 %all_to_all.20 = f16[64,8,128]{2,1,0:T(8,128)(2,1)S(1)} all-to-all(f16[64,8,128]{2,1,0:T(8,128)(2,1)S(1)} %broadcast_in_dim.19), channel_id=1, replica_groups=mesh['section'=8,'replica'=64] {'replica'}, dimensions={0} | all-to-all | bytes 262144 | tf_op jit(solution)/shard_map/all_to_all | solution.py:66
  33.1 0.0 copy-done.1
  33.1 0.0 copy-done.2
  33.1 0.0 copy-start
  33.2 3.1 %shard_map.65 = (bf16[448,512]{1,0:T(8,128)(2,1)S(1)}, f32[8,128]{1,0:T(8,128)S(1)}, bf16[3,512,512]{2,1,0:T(8,128)(2,1)S(1)}) custom-call(bf16[448,512]{1,0:T(8,128)(2,1)S(1)} %get-tuple-element.19.refs_0_, f32[64,8,128]{2,1,0:T(8,128)S(1)} %convert_element_type.28.refs_1_, f32[4,128]{1,0:T(4,128)S(1)} %bitcast.20, f32[4,128]{1,0:T(4,128)S(1)} %bitcast.22, ...), custom_call_target="tpu_custom_call" | custom-call | tf_op jit(solution)/shard_map/pallas_call | solution.py:152
  36.3 0.7 broadcast_in_dim.20
  37.0 5.3 %all-to-all-start.1 = ((f16[64,8,128]{2,1,0:T(8,128)(2,1)}), f16[64,8,128]{2,1,0:T(8,128)(2,1)S(1)}, u32[]{:S(2)}, u32[]{:S(2)}) async-start(f16[64,8,128]{2,1,0:T(8,128)(2,1)} %broadcast_in_dim.20), calls=%async_computation.1 | async-start | bytes 262144 | tf_op jit(solution)/shard_map/all_to_all | solution.py:66
  42.3 0.0 collective-permute-start
  42.4 12.0 %all-to-all-done.1 = f16[64,8,128]{2,1,0:T(8,128)(2,1)S(1)} async-done(((f16[64,8,128]{2,1,0:T(8,128)(2,1)}), f16[64,8,128]{2,1,0:T(8,128)(2,1)S(1)}, u32[]{:S(2)}, u32[]{:S(2)}) %all-to-all-start.1) | async-done | bytes 131104 | tf_op jit(solution)/shard_map/all_to_all | solution.py:66
  54.4 0.1 slice_reduce_fusion
  54.5 0.1 fusion.1
  54.6 0.0 collective-permute-start.1
  54.6 4.2 %collective-permute-done.1.refs_1_ = f32[8,128]{1,0:T(8,128)S(1)} collective-permute-done((f32[8,128]{1,0:T(8,128)S(1)}, f32[8,128]{1,0:T(8,128)S(1)}, u32[]{:S(2)}, u32[]{:S(2)}) %collective-permute-start.1) | collective-permute-done | bytes 4128 | tf_op jit(solution)/shard_map/ppermute | solution.py:293
  58.8 0.0 collective-permute-done.refs_0_
  58.8 0.0 copy-done
  58.8 4.1 %shard_map.66 = (bf16[448,512]{1,0:T(8,128)(2,1)S(1)}, f32[8,128]{1,0:T(8,128)S(1)}, bf16[4,512,512]{2,1,0:T(8,128)(2,1)S(1)}) custom-call(bf16[448,512]{1,0:T(8,128)(2,1)S(1)} %collective-permute-done.refs_0_, f32[8,128]{1,0:T(8,128)S(1)} %collective-permute-done.1.refs_1_, bf16[14,14,2,512]{3,2,1,0:T(2,128)(2,1)S(1)} %bitcast.15, ...), custom_call_target="tpu_custom_call" | custom-call | tf_op jit(solution)/shard_map/pallas_call | solution.py:152
  63.0 17.2 %all_to_all.21 = f16[64,8,128]{2,1,0:T(8,128)(2,1)S(1)} all-to-all(f16[64,8,128]{2,1,0:T(8,128)(2,1)S(1)} %broadcast_in_dim.22), channel_id=1, replica_groups=mesh['section'=8,'replica'=64] {'replica'}, dimensions={0} | all-to-all | bytes 262144 | tf_op jit(solution)/shard_map/all_to_all | solution.py:66
  80.2 3.1 %shard_map.67 = (bf16[448,512]{1,0:T(8,128)(2,1)S(1)}, f32[8,128]{1,0:T(8,128)S(1)}) custom-call(bf16[448,512]{1,0:T(8,128)(2,1)S(1)} %get-tuple-element.28.refs_0_, f32[64,8,128]{2,1,0:T(8,128)S(1)} %convert_element_type.33.refs_1_, f32[4,128]{1,0:T(4,128)S(1)} %bitcast.21, f32[4,128]{1,0:T(4,128)S(1)} %bitcast.23, ...), custom_call_target="tpu_custom_call" | custom-call | tf_op jit(solution)/shard_map/pallas_call | solution.py:152
  83.4 16.5 %all_to_all.22 = f16[64,8,128]{2,1,0:T(8,128)(2,1)S(1)} all-to-all(f16[64,8,128]{2,1,0:T(8,128)(2,1)S(1)} %broadcast_in_dim.23), channel_id=1, replica_groups=mesh['section'=8,'replica'=64] {'replica'}, dimensions={0} | all-to-all | bytes 262144 | tf_op jit(solution)/shard_map/all_to_all | solution.py:66
  99.9 1.6 %shard_map.68 = bf16[2,14,14,2,512]{4,3,2,1,0:T(2,128)(2,1)} custom-call(bf16[448,512]{1,0:T(8,128)(2,1)S(1)} %get-tuple-element.25.refs_0_, bf16[448,512]{1,0:T(8,128)(2,1)S(1)} %get-tuple-element.31.refs_1_, f32[8,128]{1,0:T(8,128)S(1)} %pad_maximum_fusion.refs_2_, f32[64,8,128]{2,1,0:T(8,128)S(1)} %convert_element_type.35.refs_3_, f32[4,128]{1,0:T(4,128)S(1)} %bitcast.17, ...), custom_call_target="tpu_custom_call" | custom-call | tf_op jit(solution)/shard_map/pallas_call | solution.py:281
  (16 shorter events, 0.2 us)
Async XLA Ops:
  0.0 33.1 %copy-start.1 = (f32[1,2,512]{2,1,0:T(2,128)S(1)}, f32[1,2,512]{2,1,0:T(2,128)}, u32[]{:S(2)}) copy-start(f32[1,2,512]{2,1,0:T(2,128)} %param.10) | copy-start | bytes 12292
  0.0 33.1 %copy-start.2 = (f32[1,2,512]{2,1,0:T(2,128)S(1)}, f32[1,2,512]{2,1,0:T(2,128)}, u32[]{:S(2)}) copy-start(f32[1,2,512]{2,1,0:T(2,128)} %param.11) | copy-start | bytes 12292
  33.1 25.7 %copy-start = (bf16[1,2,14,14,512]{4,1,3,2,0:T(2,128)(2,1)S(1)}, bf16[1,2,14,14,512]{4,1,3,2,0:T(2,128)(2,1)}, u32[]{:S(2)}) copy-start(bf16[1,2,14,14,512]{4,1,3,2,0:T(2,128)(2,1)} %param.7) | copy-start | bytes 1204228
  37.0 17.4 %all-to-all-start.1 = ((f16[64,8,128]{2,1,0:T(8,128)(2,1)}), f16[64,8,128]{2,1,0:T(8,128)(2,1)S(1)}, u32[]{:S(2)}, u32[]{:S(2)}) async-start(f16[64,8,128]{2,1,0:T(8,128)(2,1)} %broadcast_in_dim.20), calls=%async_computation.1 | async-start | bytes 262144 | tf_op jit(solution)/shard_map/all_to_all | solution.py:66
  42.3 16.5 %collective-permute-start = (bf16[448,512]{1,0:T(8,128)(2,1)S(1)}, bf16[448,512]{1,0:T(8,128)(2,1)S(1)}, u32[]{:S(2)}, u32[]{:S(2)}) collective-permute-start(bf16[448,512]{1,0:T(8,128)(2,1)S(1)} %get-tuple-element.25.refs_0_), channel_id=1, source_target_pairs={{0,64},{64,128},{128,192},{192,256},{256,320},{320,384},{384,448},... | collective-permute-start | bytes 1376264 | tf_op jit(solution)/shard_map/ppermute | solution.py:293
  54.6 4.3 %collective-permute-start.1 = (f32[8,128]{1,0:T(8,128)S(1)}, f32[8,128]{1,0:T(8,128)S(1)}, u32[]{:S(2)}, u32[]{:S(2)}) collective-permute-start(f32[8,128]{1,0:T(8,128)S(1)} %pad_maximum_fusion.refs_2_), channel_id=1, source_target_pairs={{0,64},{64,128},{128,192},{192,256},{256,320},{320,384},{384,448},... | collective-permute-start | bytes 12296 | tf_op jit(solution)/shard_map/ppermute | solution.py:293

commit v7 on v6

--- a/solution.py
+++ b/solution.py
@@ -39,7 +39,7 @@
 
 
 TAPS = [(0, 1), (1, 1), (2, 1), (0, 0), (1, 0), (2, 0), (0, 2), (1, 2), (2, 2)]
-OPENING_AHEAD = 3
+OPENING_AHEAD = 4
 CLOSING_AHEAD = 4
 
 

time: 102 us -> 102 us (level)
  transfers between devices with their start and end apart: 3 -> 3, of which waited for: 2 -> 2; matrix products, arithmetic and copies ran while one was open for 0% -> 1% of each run, Pallas kernels for 0% -> 0%
where the time goes in v7:
time: 102 us
  blocking collectives  61.4 us (60%)
  waiting for transfers between devices  16.1 us (16%)
  Pallas kernels  16 us (16%)
  starting transfers between devices  6.14 us (6%)
  other arithmetic  1.18 us (1%)
    all_to_all x3, blocking collectives, exchange(): return lax.all_to_all(copies, 'replica', 0, 0).astype(jnp.float32)  61.4 us
    all_to_all x1, waiting for transfers between devices, exchange(): return lax.all_to_all(copies, 'replica', 0, 0).astype(jnp.float32)  11.9 us
    pallas_call x3, Pallas kernels, conv_layer(): pl.pallas_call(run, in_specs=[WHOLE] * (len(operands) + 1) + [OUTSIDE] *...  9.65 us
    all_to_all x1, starting transfers between devices, exchange(): return lax.all_to_all(copies, 'replica', 0, 0).astype(jnp.float32)  6.1 us
    pallas_call x1, Pallas kernels, opening_layer(): pl.pallas_call(run, in_specs=[OUTSIDE] * 3, out_specs=[WHOLE] * 3, out_sh...  4.76 us
    ppermute x2, waiting for transfers between devices, from_behind(): lax.ppermute(value, axis, [(i, (i + 1) % length) for i in range(length)])  4.23 us
  transfers between devices with their start and end apart: 3, of which 2 were waited for; matrix products, arithmetic and copies ran while one was open for 1% of the time, Pallas kernels for 0%

profile of v7, /device:TPU:8, one launch (start us, length us, event | category | flops | bytes accessed | tf_op | source)
XLA Modules:
  0.0 101.7 jit_solution(5610144960475920382)
XLA Ops:
  0.0 0.0 copy-start.1
  0.0 0.0 copy-start.2
  0.0 4.8 %shard_map.64 = (bf16[448,512]{1,0:T(8,128)(2,1)S(1)}, f32[8,128]{1,0:T(8,128)S(1)}, bf16[4,512,512]{2,1,0:T(8,128)(2,1)S(1)}) custom-call(bf16[14,14,2,512]{3,2,1,0:T(2,128)(2,1)} %bitcast.31, bf16[3,3,512,512]{3,2,1,0:T(8,128)(2,1)} %bitcast.28, bf16[3,3,512,512]{3,2,1,0:T(8,128)(2,1)} %bitcast.24), custom_call_target="tpu_custom_call" | custom-call | tf_op jit(solution)/shard_map/pallas_call | solution.py:208
  4.8 28.3 %all_to_all.20 = f16[64,8,128]{2,1,0:T(8,128)(2,1)S(1)} all-to-all(f16[64,8,128]{2,1,0:T(8,128)(2,1)S(1)} %broadcast_in_dim.19), channel_id=1, replica_groups=mesh['section'=8,'replica'=64] {'replica'}, dimensions={0} | all-to-all | bytes 262144 | tf_op jit(solution)/shard_map/all_to_all | solution.py:66
  33.1 0.0 copy-done.1
  33.1 0.0 copy-done.2
  33.1 0.0 copy-start
  33.2 3.2 %shard_map.65 = (bf16[448,512]{1,0:T(8,128)(2,1)S(1)}, f32[8,128]{1,0:T(8,128)S(1)}, bf16[4,512,512]{2,1,0:T(8,128)(2,1)S(1)}) custom-call(bf16[448,512]{1,0:T(8,128)(2,1)S(1)} %get-tuple-element.19.refs_0_, f32[64,8,128]{2,1,0:T(8,128)S(1)} %convert_element_type.28.refs_1_, f32[4,128]{1,0:T(4,128)S(1)} %bitcast.20, f32[4,128]{1,0:T(4,128)S(1)} %bitcast.22, ...), custom_call_target="tpu_custom_call" | custom-call | tf_op jit(solution)/shard_map/pallas_call | solution.py:152
  36.3 0.7 broadcast_in_dim.20
  37.0 6.1 %all-to-all-start.1 = ((f16[64,8,128]{2,1,0:T(8,128)(2,1)}), f16[64,8,128]{2,1,0:T(8,128)(2,1)}, u32[]{:S(2)}, u32[]{:S(2)}) async-start(f16[64,8,128]{2,1,0:T(8,128)(2,1)} %broadcast_in_dim.20), calls=%async_computation.1 | async-start | bytes 262144 | tf_op jit(solution)/shard_map/all_to_all | solution.py:66
  43.1 0.0 collective-permute-start
  43.1 11.9 %all-to-all-done.1 = f16[64,8,128]{2,1,0:T(8,128)(2,1)} async-done(((f16[64,8,128]{2,1,0:T(8,128)(2,1)}), f16[64,8,128]{2,1,0:T(8,128)(2,1)}, u32[]{:S(2)}, u32[]{:S(2)}) %all-to-all-start.1) | async-done | bytes 131104 | tf_op jit(solution)/shard_map/all_to_all | solution.py:66
  55.1 0.9 convert_element_type.30
  56.0 0.1 slice_reduce_fusion
  56.1 0.1 fusion.1
  56.2 0.0 collective-permute-start.1
  56.2 4.2 %collective-permute-done.1.refs_1_ = f32[8,128]{1,0:T(8,128)S(1)} collective-permute-done((f32[8,128]{1,0:T(8,128)S(1)}, f32[8,128]{1,0:T(8,128)S(1)}, u32[]{:S(2)}, u32[]{:S(2)}) %collective-permute-start.1) | collective-permute-done | bytes 4128 | tf_op jit(solution)/shard_map/ppermute | solution.py:293
  60.4 0.0 collective-permute-done.refs_0_
  60.4 0.0 copy-done
  60.4 3.4 %shard_map.66 = (bf16[448,512]{1,0:T(8,128)(2,1)S(1)}, f32[8,128]{1,0:T(8,128)S(1)}, bf16[4,512,512]{2,1,0:T(8,128)(2,1)S(1)}) custom-call(bf16[448,512]{1,0:T(8,128)(2,1)S(1)} %collective-permute-done.refs_0_, f32[8,128]{1,0:T(8,128)S(1)} %collective-permute-done.1.refs_1_, bf16[14,14,2,512]{3,2,1,0:T(2,128)(2,1)S(1)} %bitcast.15, ...), custom_call_target="tpu_custom_call" | custom-call | tf_op jit(solution)/shard_map/pallas_call | solution.py:152
  63.9 16.5 %all_to_all.21 = f16[64,8,128]{2,1,0:T(8,128)(2,1)S(1)} all-to-all(f16[64,8,128]{2,1,0:T(8,128)(2,1)S(1)} %broadcast_in_dim.22), channel_id=1, replica_groups=mesh['section'=8,'replica'=64] {'replica'}, dimensions={0} | all-to-all | bytes 262144 | tf_op jit(solution)/shard_map/all_to_all | solution.py:66
  80.4 3.1 %shard_map.67 = (bf16[448,512]{1,0:T(8,128)(2,1)S(1)}, f32[8,128]{1,0:T(8,128)S(1)}) custom-call(bf16[448,512]{1,0:T(8,128)(2,1)S(1)} %get-tuple-element.28.refs_0_, f32[64,8,128]{2,1,0:T(8,128)S(1)} %convert_element_type.33.refs_1_, f32[4,128]{1,0:T(4,128)S(1)} %bitcast.21, f32[4,128]{1,0:T(4,128)S(1)} %bitcast.23, ...), custom_call_target="tpu_custom_call" | custom-call | tf_op jit(solution)/shard_map/pallas_call | solution.py:152
  83.6 16.6 %all_to_all.22 = f16[64,8,128]{2,1,0:T(8,128)(2,1)S(1)} all-to-all(f16[64,8,128]{2,1,0:T(8,128)(2,1)S(1)} %broadcast_in_dim.23), channel_id=1, replica_groups=mesh['section'=8,'replica'=64] {'replica'}, dimensions={0} | all-to-all | bytes 262144 | tf_op jit(solution)/shard_map/all_to_all | solution.py:66
  100.2 1.6 %shard_map.68 = bf16[2,14,14,2,512]{4,3,2,1,0:T(2,128)(2,1)} custom-call(bf16[448,512]{1,0:T(8,128)(2,1)S(1)} %get-tuple-element.25.refs_0_, bf16[448,512]{1,0:T(8,128)(2,1)S(1)} %get-tuple-element.31.refs_1_, f32[8,128]{1,0:T(8,128)S(1)} %pad_maximum_fusion.refs_2_, f32[64,8,128]{2,1,0:T(8,128)S(1)} %convert_element_type.35.refs_3_, f32[4,128]{1,0:T(4,128)S(1)} %bitcast.17, ...), custom_call_target="tpu_custom_call" | custom-call | tf_op jit(solution)/shard_map/pallas_call | solution.py:281
  (15 shorter events, 0.2 us)
Async XLA Ops:
  0.0 33.1 %copy-start.1 = (f32[1,2,512]{2,1,0:T(2,128)S(1)}, f32[1,2,512]{2,1,0:T(2,128)}, u32[]{:S(2)}) copy-start(f32[1,2,512]{2,1,0:T(2,128)} %param.10) | copy-start | bytes 12292
  0.0 33.1 %copy-start.2 = (f32[1,2,512]{2,1,0:T(2,128)S(1)}, f32[1,2,512]{2,1,0:T(2,128)}, u32[]{:S(2)}) copy-start(f32[1,2,512]{2,1,0:T(2,128)} %param.11) | copy-start | bytes 12292
  33.1 27.3 %copy-start = (bf16[1,2,14,14,512]{4,1,3,2,0:T(2,128)(2,1)S(1)}, bf16[1,2,14,14,512]{4,1,3,2,0:T(2,128)(2,1)}, u32[]{:S(2)}) copy-start(bf16[1,2,14,14,512]{4,1,3,2,0:T(2,128)(2,1)} %param.7) | copy-start | bytes 1204228
  37.0 18.0 %all-to-all-start.1 = ((f16[64,8,128]{2,1,0:T(8,128)(2,1)}), f16[64,8,128]{2,1,0:T(8,128)(2,1)}, u32[]{:S(2)}, u32[]{:S(2)}) async-start(f16[64,8,128]{2,1,0:T(8,128)(2,1)} %broadcast_in_dim.20), calls=%async_computation.1 | async-start | bytes 262144 | tf_op jit(solution)/shard_map/all_to_all | solution.py:66
  43.1 17.3 %collective-permute-start = (bf16[448,512]{1,0:T(8,128)(2,1)S(1)}, bf16[448,512]{1,0:T(8,128)(2,1)S(1)}, u32[]{:S(2)}, u32[]{:S(2)}) collective-permute-start(bf16[448,512]{1,0:T(8,128)(2,1)S(1)} %get-tuple-element.25.refs_0_), channel_id=1, source_target_pairs={{0,64},{64,128},{128,192},{192,256},{256,320},{320,384},{384,448},... | collective-permute-start | bytes 1376264 | tf_op jit(solution)/shard_map/ppermute | solution.py:293
  56.2 4.3 %collective-permute-start.1 = (f32[8,128]{1,0:T(8,128)S(1)}, f32[8,128]{1,0:T(8,128)S(1)}, u32[]{:S(2)}, u32[]{:S(2)}) collective-permute-start(f32[8,128]{1,0:T(8,128)S(1)} %pad_maximum_fusion.refs_2_), channel_id=1, source_target_pairs={{0,64},{64,128},{128,192},{192,256},{256,320},{320,384},{384,448},... | collective-permute-start | bytes 12296 | tf_op jit(solution)/shard_map/ppermute | solution.py:293

commit v8 on v7

--- a/solution.py
+++ b/solution.py
@@ -39,15 +39,31 @@
 
 
 TAPS = [(0, 1), (1, 1), (2, 1), (0, 0), (1, 0), (2, 0), (0, 2), (1, 2), (2, 2)]
-OPENING_AHEAD = 4
+OPENING_AHEAD = 3.5
 CLOSING_AHEAD = 4
 
 
-def convolve_and_measure(plan, padded, tap, stored_ref, packed_ref):
+def early_and_late(channels, count):
+    early, late = [], []
+    for place, (kh, kw) in enumerate(TAPS):
+        split = int(channels * min(max(count - place, 0), 1))
+        if split > 0:
+            early.append((kh, kw, 0, split))
+        if split < channels:
+            late.append((kh, kw, split, channels - split))
+    return early, late
+
+
+def row_of(taps, place):
+    return sum(size for _, _, _, size in taps[:place])
+
+
+def convolve_and_measure(plan, padded, taps, filters_of, stored_ref, packed_ref):
     conv_out = None
-    for kh, kw in TAPS:
-        shifted = padded[kw, pl.ds(kh * plan.line, plan.rows), :]
-        part = jnp.dot(shifted, tap(kh, kw), preferred_element_type=jnp.float32)
+    for tap in taps:
+        kh, kw, channel, size = tap
+        shifted = padded[kw, pl.ds(kh * plan.line, plan.rows), channel : channel + size]
+        part = jnp.dot(shifted, filters_of(tap), preferred_element_type=jnp.float32)
         conv_out = part if conv_out is None else conv_out + part
     stored_ref[...] = conv_out.astype(jnp.bfloat16)
     real = plan.real_rows()
@@ -92,10 +108,12 @@
     return pltpu.with_memory_space_constraint(value, pltpu.HBM)
 
 
-def fetch_taps(kernel_hbm, taps, place, sems):
-    return [
-        pltpu.make_async_copy(kernel_hbm.at[kh, kw], place(i), sems.at[i]) for i, (kh, kw) in enumerate(taps)
-    ]
+def fetch_taps(kernel_hbm, taps, target, sems):
+    copies = []
+    for place, (kh, kw, channel, size) in enumerate(taps):
+        source = kernel_hbm.at[kh, kw, pl.ds(channel, size)]
+        copies.append(pltpu.make_async_copy(source, target.at[pl.ds(row_of(taps, place), size)], sems.at[place]))
+    return copies
 
 
 def layer_outputs(plan):
@@ -106,7 +124,7 @@
 
 
 def filters_in_vmem(taps, kernel):
-    return pltpu.VMEM((len(taps),) + kernel.shape[2:], kernel.dtype)
+    return pltpu.VMEM((row_of(taps, len(taps)), kernel.shape[3]), kernel.dtype)
 
 
 def padded_scratch(plan):
@@ -120,7 +138,8 @@
 
 def conv_layer(plan, body, operands, early, kernel, following, count):
     ahead = [] if following is None else [following]
-    first, late, upcoming = TAPS[: early.shape[0]], TAPS[early.shape[0] :], TAPS[:count]
+    first, late = early_and_late(plan.channels, early.shape[0] / plan.channels)
+    upcoming, _ = early_and_late(plan.channels, count)
 
     def run(*refs):
         ins, refs = refs[: len(operands)], refs[len(operands) :]
@@ -129,23 +148,23 @@
         stored_ref, packed_ref, refs = refs[0], refs[1], refs[2:]
         next_early, refs = refs[: len(ahead)], refs[len(ahead) :]
         padded, sides, sems, next_sems = refs
-        copies = fetch_taps(kernel_hbm, late, lambda i: sides.at[i], sems)
+        copies = fetch_taps(kernel_hbm, late, sides, sems)
         for source, target in zip(next_hbm, next_early):
-            copies += fetch_taps(source, upcoming, lambda i: target.at[i], next_sems)
+            copies += fetch_taps(source, upcoming, target, next_sems)
         for copy in copies:
             copy.start()
         zero_borders(plan, padded)
         body(padded, *ins)
         fill_shifted(plan, padded)
 
-        def tap(kh, kw):
-            if (kh, kw) in first:
-                return early_ref[first.index((kh, kw))]
-            place = late.index((kh, kw))
+        def filters_of(tap):
+            if tap in first:
+                return early_ref[pl.ds(row_of(first, first.index(tap)), tap[3]), :]
+            place = late.index(tap)
             copies[place].wait()
-            return sides[place]
-
-        convolve_and_measure(plan, padded, tap, stored_ref, packed_ref)
+            return sides[pl.ds(row_of(late, place), tap[3]), :]
+
+        convolve_and_measure(plan, padded, first + late, filters_of, stored_ref, packed_ref)
         for copy in copies[len(late) :]:
             copy.wait()
 
@@ -158,7 +177,7 @@
             padded_scratch(plan),
             filters_in_vmem(late, kernel),
             pltpu.SemaphoreType.DMA((len(late),)),
-            pltpu.SemaphoreType.DMA((max(count, 1),)),
+            pltpu.SemaphoreType.DMA((max(len(upcoming), 1),)),
         ],
         compiler_params=PARAMS,
     )(*operands, in_vmem(early), in_hbm(kernel), *map(in_hbm, ahead))
@@ -177,12 +196,15 @@
 
 
 def opening_layer(plan, maps, kernel, following, count):
+    _, taps = early_and_late(plan.channels, 0)
+    upcoming, _ = early_and_late(plan.channels, count)
+
     def run(maps_hbm, kernel_hbm, next_hbm, stored_ref, packed_ref, next_early, *scratch):
         maps_vmem, map_sem, padded, filters, sems, next_sems = scratch
         fetch = pltpu.make_async_copy(maps_hbm, maps_vmem, map_sem)
         fetch.start()
-        copies = fetch_taps(kernel_hbm, TAPS, lambda i: filters.at[i], sems)
-        ahead = fetch_taps(next_hbm, TAPS[:count], lambda i: next_early.at[i], next_sems)
+        copies = fetch_taps(kernel_hbm, taps, filters, sems)
+        ahead = fetch_taps(next_hbm, upcoming, next_early, next_sems)
         for copy in copies[:3]:
             copy.start()
         zero_borders(plan, padded)
@@ -196,12 +218,12 @@
         spread_lines(plan, maps_vmem, write)
         fill_shifted(plan, padded)
 
-        def tap(kh, kw):
-            place = TAPS.index((kh, kw))
+        def filters_of(tap):
+            place = taps.index(tap)
             copies[place].wait()
-            return filters[place]
-
-        convolve_and_measure(plan, padded, tap, stored_ref, packed_ref)
+            return filters[pl.ds(row_of(taps, place), tap[3]), :]
+
+        convolve_and_measure(plan, padded, taps, filters_of, stored_ref, packed_ref)
         for copy in ahead:
             copy.wait()
 
@@ -209,14 +231,14 @@
         run,
         in_specs=[OUTSIDE] * 3,
         out_specs=[WHOLE] * 3,
-        out_shape=layer_outputs(plan) + [filters_in_vmem(TAPS[:count], following)],
+        out_shape=layer_outputs(plan) + [filters_in_vmem(upcoming, following)],
         scratch_shapes=[
             pltpu.VMEM(maps.shape, maps.dtype),
             pltpu.SemaphoreType.DMA(()),
             padded_scratch(plan),
-            filters_in_vmem(TAPS, kernel),
-            pltpu.SemaphoreType.DMA((len(TAPS),)),
-            pltpu.SemaphoreType.DMA((count,)),
+            filters_in_vmem(taps, kernel),
+            pltpu.SemaphoreType.DMA((len(taps),)),
+            pltpu.SemaphoreType.DMA((len(upcoming),)),
         ],
         compiler_params=PARAMS,
     )(in_hbm(maps), in_hbm(kernel), in_hbm(following))

time: 102 us -> 101 us (level)
  transfers between devices with their start and end apart: 3 -> 3, of which waited for: 2 -> 2; matrix products, arithmetic and copies ran while one was open for 1% -> 0% of each run, Pallas kernels for 0% -> 0%
where the time goes in v8:
time: 101 us
  blocking collectives  62 us (61%)
  waiting for transfers between devices  16.2 us (16%)
  Pallas kernels  15.8 us (16%)
  starting transfers between devices  5.36 us (5%)
    all_to_all x3, blocking collectives, exchange(): return lax.all_to_all(copies, 'replica', 0, 0).astype(jnp.float32)  62 us
    all_to_all x1, waiting for transfers between devices, exchange(): return lax.all_to_all(copies, 'replica', 0, 0).astype(jnp.float32)  12 us
    pallas_call x3, Pallas kernels, conv_layer(): pl.pallas_call(run, in_specs=[WHOLE] * (len(operands) + 1) + [OUTSIDE] *...  9.5 us
    all_to_all x1, starting transfers between devices, exchange(): return lax.all_to_all(copies, 'replica', 0, 0).astype(jnp.float32)  5.33 us
    pallas_call x1, Pallas kernels, opening_layer(): pl.pallas_call(run, in_specs=[OUTSIDE] * 3, out_specs=[WHOLE] * 3, out_sh...  4.76 us
    ppermute x2, waiting for transfers between devices, from_behind(): lax.ppermute(value, axis, [(i, (i + 1) % length) for i in range(length)])  4.23 us
  transfers between devices with their start and end apart: 3, of which 2 were waited for; matrix products, arithmetic and copies ran while one was open for 0% of the time, Pallas kernels for 0%

profile of v8, /device:TPU:8, one launch (start us, length us, event | category | flops | bytes accessed | tf_op | source)
XLA Modules:
  0.0 100.6 jit_solution(2763943712527717534)
XLA Ops:
  0.0 0.0 copy-start.1
  0.0 0.0 copy-start.2
  0.0 4.8 %shard_map.64 = (bf16[448,512]{1,0:T(8,128)(2,1)S(1)}, f32[8,128]{1,0:T(8,128)S(1)}, bf16[2048,512]{1,0:T(8,128)(2,1)S(1)}) custom-call(bf16[14,14,2,512]{3,2,1,0:T(2,128)(2,1)} %bitcast.31, bf16[3,3,512,512]{3,2,1,0:T(8,128)(2,1)} %bitcast.28, bf16[3,3,512,512]{3,2,1,0:T(8,128)(2,1)} %bitcast.24), custom_call_target="tpu_custom_call" | custom-call | tf_op jit(solution)/shard_map/pallas_call | solution.py:230
  4.8 28.3 %all_to_all.20 = f16[64,8,128]{2,1,0:T(8,128)(2,1)S(1)} all-to-all(f16[64,8,128]{2,1,0:T(8,128)(2,1)S(1)} %broadcast_in_dim.19), channel_id=1, replica_groups=mesh['section'=8,'replica'=64] {'replica'}, dimensions={0} | all-to-all | bytes 262144 | tf_op jit(solution)/shard_map/all_to_all | solution.py:82
  33.1 0.0 copy-done.1
  33.1 0.0 copy-done.2
  33.1 0.0 copy-start
  33.2 3.2 %shard_map.65 = (bf16[448,512]{1,0:T(8,128)(2,1)S(1)}, f32[8,128]{1,0:T(8,128)S(1)}, bf16[1792,512]{1,0:T(8,128)(2,1)S(1)}) custom-call(bf16[448,512]{1,0:T(8,128)(2,1)S(1)} %get-tuple-element.19.refs_0_, f32[64,8,128]{2,1,0:T(8,128)S(1)} %convert_element_type.28.refs_1_, f32[4,128]{1,0:T(4,128)S(1)} %bitcast.20, f32[4,128]{1,0:T(4,128)S(1)} %bitcast.22, ...), custom_call_target="tpu_custom_call" | custom-call | tf_op jit(solution)/shard_map/pallas_call | solution.py:171
  36.3 0.7 broadcast_in_dim.20
  37.0 5.3 %all-to-all-start.1 = ((f16[64,8,128]{2,1,0:T(8,128)(2,1)}), f16[64,8,128]{2,1,0:T(8,128)(2,1)S(1)}, u32[]{:S(2)}, u32[]{:S(2)}) async-start(f16[64,8,128]{2,1,0:T(8,128)(2,1)} %broadcast_in_dim.20), calls=%async_computation.1 | async-start | bytes 262144 | tf_op jit(solution)/shard_map/all_to_all | solution.py:82
  42.3 0.0 collective-permute-start
  42.4 12.0 %all-to-all-done.1 = f16[64,8,128]{2,1,0:T(8,128)(2,1)S(1)} async-done(((f16[64,8,128]{2,1,0:T(8,128)(2,1)}), f16[64,8,128]{2,1,0:T(8,128)(2,1)S(1)}, u32[]{:S(2)}, u32[]{:S(2)}) %all-to-all-start.1) | async-done | bytes 131104 | tf_op jit(solution)/shard_map/all_to_all | solution.py:82
  54.4 0.1 slice_reduce_fusion
  54.5 0.1 fusion.1
  54.6 0.0 collective-permute-start.1
  54.6 4.2 %collective-permute-done.1.refs_1_ = f32[8,128]{1,0:T(8,128)S(1)} collective-permute-done((f32[8,128]{1,0:T(8,128)S(1)}, f32[8,128]{1,0:T(8,128)S(1)}, u32[]{:S(2)}, u32[]{:S(2)}) %collective-permute-start.1) | collective-permute-done | bytes 4128 | tf_op jit(solution)/shard_map/ppermute | solution.py:315
  58.8 0.0 collective-permute-done.refs_0_
  58.8 0.0 copy-done
  58.8 3.2 %shard_map.66 = (bf16[448,512]{1,0:T(8,128)(2,1)S(1)}, f32[8,128]{1,0:T(8,128)S(1)}, bf16[2048,512]{1,0:T(8,128)(2,1)S(1)}) custom-call(bf16[448,512]{1,0:T(8,128)(2,1)S(1)} %collective-permute-done.refs_0_, f32[8,128]{1,0:T(8,128)S(1)} %collective-permute-done.1.refs_1_, bf16[14,14,2,512]{3,2,1,0:T(2,128)(2,1)S(1)} %bitcast.15, ...), custom_call_target="tpu_custom_call" | custom-call | tf_op jit(solution)/shard_map/pallas_call | solution.py:171
  62.1 17.2 %all_to_all.21 = f16[64,8,128]{2,1,0:T(8,128)(2,1)S(1)} all-to-all(f16[64,8,128]{2,1,0:T(8,128)(2,1)S(1)} %broadcast_in_dim.22), channel_id=1, replica_groups=mesh['section'=8,'replica'=64] {'replica'}, dimensions={0} | all-to-all | bytes 262144 | tf_op jit(solution)/shard_map/all_to_all | solution.py:82
  79.3 3.1 %shard_map.67 = (bf16[448,512]{1,0:T(8,128)(2,1)S(1)}, f32[8,128]{1,0:T(8,128)S(1)}) custom-call(bf16[448,512]{1,0:T(8,128)(2,1)S(1)} %get-tuple-element.28.refs_0_, f32[64,8,128]{2,1,0:T(8,128)S(1)} %convert_element_type.33.refs_1_, f32[4,128]{1,0:T(4,128)S(1)} %bitcast.21, f32[4,128]{1,0:T(4,128)S(1)} %bitcast.23, ...), custom_call_target="tpu_custom_call" | custom-call | tf_op jit(solution)/shard_map/pallas_call | solution.py:171
  82.5 16.5 %all_to_all.22 = f16[64,8,128]{2,1,0:T(8,128)(2,1)S(1)} all-to-all(f16[64,8,128]{2,1,0:T(8,128)(2,1)S(1)} %broadcast_in_dim.23), channel_id=1, replica_groups=mesh['section'=8,'replica'=64] {'replica'}, dimensions={0} | all-to-all | bytes 262144 | tf_op jit(solution)/shard_map/all_to_all | solution.py:82
  99.0 1.6 %shard_map.68 = bf16[2,14,14,2,512]{4,3,2,1,0:T(2,128)(2,1)} custom-call(bf16[448,512]{1,0:T(8,128)(2,1)S(1)} %get-tuple-element.25.refs_0_, bf16[448,512]{1,0:T(8,128)(2,1)S(1)} %get-tuple-element.31.refs_1_, f32[8,128]{1,0:T(8,128)S(1)} %pad_maximum_fusion.refs_2_, f32[64,8,128]{2,1,0:T(8,128)S(1)} %convert_element_type.35.refs_3_, f32[4,128]{1,0:T(4,128)S(1)} %bitcast.17, ...), custom_call_target="tpu_custom_call" | custom-call | tf_op jit(solution)/shard_map/pallas_call | solution.py:303
  (16 shorter events, 0.2 us)
Async XLA Ops:
  0.0 33.1 %copy-start.1 = (f32[1,2,512]{2,1,0:T(2,128)S(1)}, f32[1,2,512]{2,1,0:T(2,128)}, u32[]{:S(2)}) copy-start(f32[1,2,512]{2,1,0:T(2,128)} %param.10) | copy-start | bytes 12292
  0.0 33.1 %copy-start.2 = (f32[1,2,512]{2,1,0:T(2,128)S(1)}, f32[1,2,512]{2,1,0:T(2,128)}, u32[]{:S(2)}) copy-start(f32[1,2,512]{2,1,0:T(2,128)} %param.11) | copy-start | bytes 12292
  33.1 25.7 %copy-start = (bf16[1,2,14,14,512]{4,1,3,2,0:T(2,128)(2,1)S(1)}, bf16[1,2,14,14,512]{4,1,3,2,0:T(2,128)(2,1)}, u32[]{:S(2)}) copy-start(bf16[1,2,14,14,512]{4,1,3,2,0:T(2,128)(2,1)} %param.7) | copy-start | bytes 1204228
  37.0 17.4 %all-to-all-start.1 = ((f16[64,8,128]{2,1,0:T(8,128)(2,1)}), f16[64,8,128]{2,1,0:T(8,128)(2,1)S(1)}, u32[]{:S(2)}, u32[]{:S(2)}) async-start(f16[64,8,128]{2,1,0:T(8,128)(2,1)} %broadcast_in_dim.20), calls=%async_computation.1 | async-start | bytes 262144 | tf_op jit(solution)/shard_map/all_to_all | solution.py:82
  42.3 16.5 %collective-permute-start = (bf16[448,512]{1,0:T(8,128)(2,1)S(1)}, bf16[448,512]{1,0:T(8,128)(2,1)S(1)}, u32[]{:S(2)}, u32[]{:S(2)}) collective-permute-start(bf16[448,512]{1,0:T(8,128)(2,1)S(1)} %get-tuple-element.25.refs_0_), channel_id=1, source_target_pairs={{0,64},{64,128},{128,192},{192,256},{256,320},{320,384},{384,448},... | collective-permute-start | bytes 1376264 | tf_op jit(solution)/shard_map/ppermute | solution.py:315
  54.6 4.3 %collective-permute-start.1 = (f32[8,128]{1,0:T(8,128)S(1)}, f32[8,128]{1,0:T(8,128)S(1)}, u32[]{:S(2)}, u32[]{:S(2)}) collective-permute-start(f32[8,128]{1,0:T(8,128)S(1)} %pad_maximum_fusion.refs_2_), channel_id=1, source_target_pairs={{0,64},{64,128},{128,192},{192,256},{256,320},{320,384},{384,448},... | collective-permute-start | bytes 12296 | tf_op jit(solution)/shard_map/ppermute | solution.py:315

commit v9 on v8

--- a/solution.py
+++ b/solution.py
@@ -136,8 +136,10 @@
 PARAMS = pltpu.CompilerParams(vmem_limit_bytes=32 << 20)
 
 
-def conv_layer(plan, body, operands, early, kernel, following, count):
+def conv_layer(plan, body, operands, early, kernel, following, count, earlier=None):
     ahead = [] if following is None else [following]
+    done = [] if earlier is None else [in_vmem(earlier[0]), earlier[1]]
+    shape = result_shape(plan)
     first, late = early_and_late(plan.channels, early.shape[0] / plan.channels)
     upcoming, _ = early_and_late(plan.channels, count)
 
@@ -145,14 +147,21 @@
         ins, refs = refs[: len(operands)], refs[len(operands) :]
         early_ref, kernel_hbm, refs = refs[0], refs[1], refs[2:]
         next_hbm, refs = refs[: len(ahead)], refs[len(ahead) :]
+        done_refs, refs = refs[: len(done)], refs[len(done) :]
         stored_ref, packed_ref, refs = refs[0], refs[1], refs[2:]
         next_early, refs = refs[: len(ahead)], refs[len(ahead) :]
+        if done:
+            result_hbm, *refs, result_vmem, result_sem = refs
+            written = pltpu.make_async_copy(result_vmem, result_hbm.at[0], result_sem)
         padded, sides, sems, next_sems = refs
         copies = fetch_taps(kernel_hbm, late, sides, sems)
-        for source, target in zip(next_hbm, next_early):
-            copies += fetch_taps(source, upcoming, target, next_sems)
         for copy in copies:
             copy.start()
+        for source, target in zip(next_hbm, next_early):
+            ahead_copies = fetch_taps(source, upcoming, target, next_sems)
+            for copy in ahead_copies:
+                copy.start(priority=1)
+            copies += ahead_copies
         zero_borders(plan, padded)
         body(padded, *ins)
         fill_shifted(plan, padded)
@@ -161,26 +170,48 @@
             if tap in first:
                 return early_ref[pl.ds(row_of(first, first.index(tap)), tap[3]), :]
             place = late.index(tap)
+            if done and place == 0:
+                terms = done_refs[1][...]
+                write = map_writer(plan, result_vmem)
+                normalize_into(plan, done_refs[0], terms[: plan.groups], terms[plan.groups :], write)
+                written.start()
             copies[place].wait()
             return sides[pl.ds(row_of(late, place), tap[3]), :]
 
         convolve_and_measure(plan, padded, first + late, filters_of, stored_ref, packed_ref)
         for copy in copies[len(late) :]:
             copy.wait()
+        if done:
+            written.wait()
 
     return pl.pallas_call(
         run,
-        in_specs=[WHOLE] * (len(operands) + 1) + [OUTSIDE] * (1 + len(ahead)),
-        out_specs=[WHOLE] * (2 + len(ahead)),
-        out_shape=layer_outputs(plan) + [filters_in_vmem(upcoming, kernel) for kernel in ahead],
+        in_specs=[WHOLE] * (len(operands) + 1) + [OUTSIDE] * (1 + len(ahead)) + [WHOLE] * len(done),
+        out_specs=[WHOLE] * (2 + len(ahead)) + ([OUTSIDE] if done else []),
+        out_shape=layer_outputs(plan) + [filters_in_vmem(upcoming, kernel) for kernel in ahead]
+        + ([pltpu.HBM(shape, jnp.bfloat16)] if done else []),
         scratch_shapes=[
             padded_scratch(plan),
             filters_in_vmem(late, kernel),
             pltpu.SemaphoreType.DMA((len(late),)),
             pltpu.SemaphoreType.DMA((max(len(upcoming), 1),)),
-        ],
+        ]
+        + ([pltpu.VMEM(shape[1:], jnp.bfloat16), pltpu.SemaphoreType.DMA(())] if done else []),
         compiler_params=PARAMS,
-    )(*operands, in_vmem(early), in_hbm(kernel), *map(in_hbm, ahead))
+    )(*operands, in_vmem(early), in_hbm(kernel), *map(in_hbm, ahead), *done)
+
+
+def result_shape(plan):
+    return (TICKS, plan.height, plan.width, plan.images, plan.channels)
+
+
+def map_writer(plan, out_ref):
+    def write(lanes, values):
+        for row in range(plan.height):
+            line = values[row * plan.line : row * plan.line + plan.width * plan.images]
+            out_ref[row, :, :, lanes] = line.reshape(plan.width, plan.images, LANES)
+
+    return write
 
 
 def inner(plan):
@@ -206,7 +237,7 @@
         copies = fetch_taps(kernel_hbm, taps, filters, sems)
         ahead = fetch_taps(next_hbm, upcoming, next_early, next_sems)
         for copy in copies[:3]:
-            copy.start()
+            copy.start(priority=1)
         zero_borders(plan, padded)
         fetch.wait()
         for copy in copies[3:] + ahead:
@@ -244,7 +275,7 @@
     )(in_hbm(maps), in_hbm(kernel), in_hbm(following))
 
 
-def layer_of_stored(plan, stored, gathered, gain, bias, early, kernel, following, count):
+def layer_of_stored(plan, stored, gathered, gain, bias, early, kernel, following, count, earlier=None):
     def body(padded, stored_ref, gathered_ref, gain_ref, bias_ref):
         scale, offset = join(plan, gathered_ref[...], gain_ref[...], bias_ref[...])
 
@@ -253,7 +284,7 @@
 
         normalize_into(plan, stored_ref, scale, offset, write)
 
-    return conv_layer(plan, body, [in_vmem(stored), gathered, gain, bias], early, kernel, following, count)
+    return conv_layer(plan, body, [in_vmem(stored), gathered, gain, bias], early, kernel, following, count, earlier)
 
 
 def layer_of_moved(plan, stored, terms, maps, is_first, early, kernel, following, count):
@@ -275,39 +306,23 @@
     return conv_layer(plan, body, operands, early, kernel, following, count)
 
 
-def finish(plan, stored, terms, gathered, gain, bias):
-    shape = (TICKS, plan.height, plan.width, plan.images, plan.channels)
-
-    def run(*refs):
-        *refs, out_hbm, out_ref, sems = refs
-        copies = []
-        for tick in range(TICKS):
-
-            def write(lanes, values, tick=tick):
-                for row in range(plan.height):
-                    line = values[row * plan.line : row * plan.line + plan.width * plan.images]
-                    out_ref[tick, row, :, :, lanes] = line.reshape(plan.width, plan.images, LANES)
-
-            if tick + 1 < TICKS:
-                known = refs[TICKS + tick][...]
-                scale, offset = known[: plan.groups], known[plan.groups :]
-            else:
-                scale, offset = join(plan, *(ref[...] for ref in refs[2 * TICKS - 1 :]))
-            normalize_into(plan, refs[tick], scale, offset, write)
-            copies.append(pltpu.make_async_copy(out_ref.at[tick], out_hbm.at[tick], sems.at[tick]))
-            copies[-1].start()
-        for copy in copies:
-            copy.wait()
-
-    operands = [in_vmem(value) for value in stored] + terms + [gathered, gain, bias]
+def finish(plan, stored, gathered, gain, bias, result):
+    def run(stored_ref, gathered_ref, gain_ref, bias_ref, _, out_hbm, out_vmem, sem):
+        scale, offset = join(plan, gathered_ref[...], gain_ref[...], bias_ref[...])
+        normalize_into(plan, stored_ref, scale, offset, map_writer(plan, out_vmem))
+        copy = pltpu.make_async_copy(out_vmem, out_hbm.at[TICKS - 1], sem)
+        copy.start()
+        copy.wait()
+
     return pl.pallas_call(
         run,
-        in_specs=[WHOLE] * len(operands),
+        in_specs=[WHOLE] * 4 + [OUTSIDE],
         out_specs=OUTSIDE,
-        out_shape=pltpu.HBM(shape, jnp.bfloat16),
-        scratch_shapes=[pltpu.VMEM(shape, jnp.bfloat16), pltpu.SemaphoreType.DMA((TICKS,))],
+        out_shape=pltpu.HBM(result.shape, result.dtype),
+        input_output_aliases={4: 0},
+        scratch_shapes=[pltpu.VMEM(result.shape[1:], result.dtype), pltpu.SemaphoreType.DMA(())],
         compiler_params=PARAMS,
-    )(*operands)
+    )(in_vmem(stored), gathered, gain, bias, result)
 
 
 def from_behind(value, axis):
@@ -331,7 +346,7 @@
     order = (1, 2, 0, 3)
     maps = jnp.transpose(pending_section_entries[0], order)
     stored, packed, early = opening_layer(plan, maps, first_kernel, second_kernel, CLOSING_AHEAD)
-    kept, kept_terms = [], []
+    earlier = None
     for tick in range(TICKS):
         gathered = exchange(plan, packed)
         if tick == 0:
@@ -340,22 +355,21 @@
             bias = biases[0].reshape(2, plan.groups, LANES)
         last = tick + 1 == TICKS
         ahead = (None, 0) if last else (first_kernel, OPENING_AHEAD)
-        stored, packed, *early = layer_of_stored(
-            plan, stored, gathered, gain[0], bias[0], early, second_kernel, *ahead
+        stored, packed, *rest = layer_of_stored(
+            plan, stored, gathered, gain[0], bias[0], early, second_kernel, *ahead, earlier
         )
-        kept.append(stored)
         if last:
             break
         moved = from_behind(stored, "section")
         terms = jnp.concatenate(join(plan, exchange(plan, packed), gain[1], bias[1]), axis=0)
-        kept_terms.append(terms)
+        earlier = (stored, terms)
         terms = from_behind(terms, "section")
         arriving = jnp.transpose(arriving_microsets[tick], order)
         ahead = (second_kernel, CLOSING_AHEAD)
         stored, packed, early = layer_of_moved(
-            plan, moved, terms, arriving, is_first, early[0], first_kernel, *ahead
+            plan, moved, terms, arriving, is_first, rest[0], first_kernel, *ahead
         )
-    result = finish(plan, kept, kept_terms, exchange(plan, packed), gain[1], bias[1])
+    result = finish(plan, stored, exchange(plan, packed), gain[1], bias[1], rest[0])
     return jnp.transpose(result, (0, 3, 1, 2, 4))[None]
 
 

time: 101 us -> 101 us (level)
  no operation moved by 1% of the time
where the time goes in v9:
time: 101 us; the launch traced here: 100 us
  blocking collectives  62 us (61%)
  waiting for transfers between devices  16.2 us (16%)
  Pallas kernels  15.5 us (15%)
  starting transfers between devices  5.35 us (5%)
    all_to_all x3, blocking collectives, exchange(): return lax.all_to_all(copies, 'replica', 0, 0).astype(jnp.float32)  62 us
    all_to_all x1, waiting for transfers between devices, exchange(): return lax.all_to_all(copies, 'replica', 0, 0).astype(jnp.float32)  12 us
    pallas_call x3, Pallas kernels, conv_layer(): pl.pallas_call(run, in_specs=[WHOLE] * (len(operands) + 1) + [OUTSIDE] *...  9.77 us
    all_to_all x1, starting transfers between devices, exchange(): return lax.all_to_all(copies, 'replica', 0, 0).astype(jnp.float32)  5.32 us
    pallas_call x1, Pallas kernels, opening_layer(): pl.pallas_call(run, in_specs=[OUTSIDE] * 3, out_specs=[WHOLE] * 3, out_sh...  4.51 us
    ppermute x2, waiting for transfers between devices, from_behind(): lax.ppermute(value, axis, [(i, (i + 1) % length) for i in range(length)])  4.23 us
  transfers between devices with their start and end apart: 3, of which 2 were waited for; matrix products, arithmetic and copies ran while one was open for 0% of the time, Pallas kernels for 0%

profile of v9, /device:TPU:8, one launch (start us, length us, event | category | flops | bytes accessed | tf_op | source)
XLA Modules:
  0.0 100.3 jit_solution(7244429090815973653)
XLA Ops:
  0.0 0.0 copy-start.1
  0.0 0.0 copy-start.2
  0.0 4.5 %shard_map.64 = (bf16[448,512]{1,0:T(8,128)(2,1)S(1)}, f32[8,128]{1,0:T(8,128)S(1)}, bf16[2048,512]{1,0:T(8,128)(2,1)S(1)}) custom-call(bf16[14,14,2,512]{3,2,1,0:T(2,128)(2,1)} %bitcast.31, bf16[3,3,512,512]{3,2,1,0:T(8,128)(2,1)} %bitcast.28, bf16[3,3,512,512]{3,2,1,0:T(8,128)(2,1)} %bitcast.24), custom_call_target="tpu_custom_call" | custom-call | tf_op jit(solution)/shard_map/pallas_call | solution.py:261
  4.6 28.3 %all_to_all.20 = f16[64,8,128]{2,1,0:T(8,128)(2,1)S(1)} all-to-all(f16[64,8,128]{2,1,0:T(8,128)(2,1)S(1)} %broadcast_in_dim.19), channel_id=1, replica_groups=mesh['section'=8,'replica'=64] {'replica'}, dimensions={0} | all-to-all | bytes 262144 | tf_op jit(solution)/shard_map/all_to_all | solution.py:82
  32.9 0.0 copy-done.1
  32.9 0.0 copy-done.2
  32.9 0.0 copy-start
  32.9 3.2 %shard_map.65 = (bf16[448,512]{1,0:T(8,128)(2,1)S(1)}, f32[8,128]{1,0:T(8,128)S(1)}, bf16[1792,512]{1,0:T(8,128)(2,1)S(1)}) custom-call(bf16[448,512]{1,0:T(8,128)(2,1)S(1)} %get-tuple-element.20.refs_0_, f32[64,8,128]{2,1,0:T(8,128)S(1)} %convert_element_type.28.refs_1_, f32[4,128]{1,0:T(4,128)S(1)} %bitcast.20, f32[4,128]{1,0:T(4,128)S(1)} %bitcast.22, ...), custom_call_target="tpu_custom_call" | custom-call | tf_op jit(solution)/shard_map/pallas_call | solution.py:187
  36.1 0.7 broadcast_in_dim.20
  36.8 5.3 %all-to-all-start.1 = ((f16[64,8,128]{2,1,0:T(8,128)(2,1)}), f16[64,8,128]{2,1,0:T(8,128)(2,1)S(1)}, u32[]{:S(2)}, u32[]{:S(2)}) async-start(f16[64,8,128]{2,1,0:T(8,128)(2,1)} %broadcast_in_dim.20), calls=%async_computation.1 | async-start | bytes 262144 | tf_op jit(solution)/shard_map/all_to_all | solution.py:82
  42.1 0.0 collective-permute-start
  42.1 12.0 %all-to-all-done.1 = f16[64,8,128]{2,1,0:T(8,128)(2,1)S(1)} async-done(((f16[64,8,128]{2,1,0:T(8,128)(2,1)}), f16[64,8,128]{2,1,0:T(8,128)(2,1)S(1)}, u32[]{:S(2)}, u32[]{:S(2)}) %all-to-all-start.1) | async-done | bytes 131104 | tf_op jit(solution)/shard_map/all_to_all | solution.py:82
  54.1 0.1 slice_reduce_fusion
  54.2 0.1 fusion.1
  54.3 0.0 collective-permute-start.1
  54.4 4.2 %collective-permute-done.1.refs_1_ = f32[8,128]{1,0:T(8,128)S(1)} collective-permute-done((f32[8,128]{1,0:T(8,128)S(1)}, f32[8,128]{1,0:T(8,128)S(1)}, u32[]{:S(2)}, u32[]{:S(2)}) %collective-permute-start.1) | collective-permute-done | bytes 4128 | tf_op jit(solution)/shard_map/ppermute | solution.py:330
  58.6 0.0 collective-permute-done.refs_0_
  58.6 0.0 copy-done
  58.6 3.2 %shard_map.66 = (bf16[448,512]{1,0:T(8,128)(2,1)S(1)}, f32[8,128]{1,0:T(8,128)S(1)}, bf16[2048,512]{1,0:T(8,128)(2,1)S(1)}) custom-call(bf16[448,512]{1,0:T(8,128)(2,1)S(1)} %collective-permute-done.refs_0_, f32[8,128]{1,0:T(8,128)S(1)} %collective-permute-done.1.refs_1_, bf16[14,14,2,512]{3,2,1,0:T(2,128)(2,1)S(1)} %bitcast.15, ...), custom_call_target="tpu_custom_call" | custom-call | tf_op jit(solution)/shard_map/pallas_call | solution.py:187
  61.9 17.2 %all_to_all.21 = f16[64,8,128]{2,1,0:T(8,128)(2,1)S(1)} all-to-all(f16[64,8,128]{2,1,0:T(8,128)(2,1)S(1)} %broadcast_in_dim.22), channel_id=1, replica_groups=mesh['section'=8,'replica'=64] {'replica'}, dimensions={0} | all-to-all | bytes 262144 | tf_op jit(solution)/shard_map/all_to_all | solution.py:82
  79.1 3.4 %shard_map.67 = (bf16[448,512]{1,0:T(8,128)(2,1)S(1)}, f32[8,128]{1,0:T(8,128)S(1)}, bf16[2,14,14,2,512]{4,3,2,1,0:T(2,128)(2,1)}) custom-call(bf16[448,512]{1,0:T(8,128)(2,1)S(1)} %get-tuple-element.29.refs_0_, f32[64,8,128]{2,1,0:T(8,128)S(1)} %convert_element_type.33.refs_1_, f32[4,128]{1,0:T(4,128)S(1)} %bitcast.21, f32[4,128]{1,0:T(4,128)S(1)} %bitcast.23, ...), custom_call_target="tpu_custom_call" | custom-call | tf_op jit(solution)/shard_map/pallas_call | solution.py:187
  82.5 16.5 %all_to_all.22 = f16[64,8,128]{2,1,0:T(8,128)(2,1)S(1)} all-to-all(f16[64,8,128]{2,1,0:T(8,128)(2,1)S(1)} %broadcast_in_dim.23), channel_id=1, replica_groups=mesh['section'=8,'replica'=64] {'replica'}, dimensions={0} | all-to-all | bytes 262144 | tf_op jit(solution)/shard_map/all_to_all | solution.py:82
  99.1 1.2 %shard_map.68 = bf16[2,14,14,2,512]{4,3,2,1,0:T(2,128)(2,1)} custom-call(bf16[448,512]{1,0:T(8,128)(2,1)S(1)} %get-tuple-element.32.stored_ref, f32[64,8,128]{2,1,0:T(8,128)S(1)} %convert_element_type.35.gathered_ref, f32[4,128]{1,0:T(4,128)S(1)} %bitcast.17, f32[4,128]{1,0:T(4,128)S(1)} %bitcast.19, ...), custom_call_target="tpu_custom_call", output_to_operand_aliasing={{}: (4, {})} | custom-call | tf_op jit(solution)/shard_map/pallas_call | solution.py:317
  (16 shorter events, 0.2 us)
Async XLA Ops:
  0.0 32.9 %copy-start.1 = (f32[1,2,512]{2,1,0:T(2,128)S(1)}, f32[1,2,512]{2,1,0:T(2,128)}, u32[]{:S(2)}) copy-start(f32[1,2,512]{2,1,0:T(2,128)} %param.10) | copy-start | bytes 12292
  0.0 32.9 %copy-start.2 = (f32[1,2,512]{2,1,0:T(2,128)S(1)}, f32[1,2,512]{2,1,0:T(2,128)}, u32[]{:S(2)}) copy-start(f32[1,2,512]{2,1,0:T(2,128)} %param.11) | copy-start | bytes 12292
  32.9 25.7 %copy-start = (bf16[1,2,14,14,512]{4,1,3,2,0:T(2,128)(2,1)S(1)}, bf16[1,2,14,14,512]{4,1,3,2,0:T(2,128)(2,1)}, u32[]{:S(2)}) copy-start(bf16[1,2,14,14,512]{4,1,3,2,0:T(2,128)(2,1)} %param.7) | copy-start | bytes 1204228
  36.8 17.3 %all-to-all-start.1 = ((f16[64,8,128]{2,1,0:T(8,128)(2,1)}), f16[64,8,128]{2,1,0:T(8,128)(2,1)S(1)}, u32[]{:S(2)}, u32[]{:S(2)}) async-start(f16[64,8,128]{2,1,0:T(8,128)(2,1)} %broadcast_in_dim.20), calls=%async_computation.1 | async-start | bytes 262144 | tf_op jit(solution)/shard_map/all_to_all | solution.py:82
  42.1 16.5 %collective-permute-start = (bf16[448,512]{1,0:T(8,128)(2,1)S(1)}, bf16[448,512]{1,0:T(8,128)(2,1)S(1)}, u32[]{:S(2)}, u32[]{:S(2)}) collective-permute-start(bf16[448,512]{1,0:T(8,128)(2,1)S(1)} %get-tuple-element.26.refs_6_), channel_id=1, source_target_pairs={{0,64},{64,128},{128,192},{192,256},{256,320},{320,384},{384,448},... | collective-permute-start | bytes 1376264 | tf_op jit(solution)/shard_map/ppermute | solution.py:330
  54.3 4.3 %collective-permute-start.1 = (f32[8,128]{1,0:T(8,128)S(1)}, f32[8,128]{1,0:T(8,128)S(1)}, u32[]{:S(2)}, u32[]{:S(2)}) collective-permute-start(f32[8,128]{1,0:T(8,128)S(1)} %pad_maximum_fusion.refs_7_), channel_id=1, source_target_pairs={{0,64},{64,128},{128,192},{192,256},{256,320},{320,384},{384,448},... | collective-permute-start | bytes 12296 | tf_op jit(solution)/shard_map/ppermute | solution.py:330

commit v10 on v9

--- a/solution.py
+++ b/solution.py
@@ -41,6 +41,7 @@
 TAPS = [(0, 1), (1, 1), (2, 1), (0, 0), (1, 0), (2, 0), (0, 2), (1, 2), (2, 2)]
 OPENING_AHEAD = 3.5
 CLOSING_AHEAD = 4
+FIRST_AHEAD = 5
 
 
 def early_and_late(channels, count):
@@ -201,6 +202,20 @@
     )(*operands, in_vmem(early), in_hbm(kernel), *map(in_hbm, ahead), *done)
 
 
+def joined(plan, gathered, gain, bias):
+    def run(gathered_ref, gain_ref, bias_ref, terms_ref):
+        scale, offset = join(plan, gathered_ref[...], gain_ref[...], bias_ref[...])
+        terms_ref[...] = jnp.concatenate([scale, offset], axis=0)
+
+    return pl.pallas_call(
+        run,
+        in_specs=[WHOLE] * 3,
+        out_specs=WHOLE,
+        out_shape=pltpu.VMEM((2 * plan.groups, LANES), jnp.float32),
+        compiler_params=PARAMS,
+    )(gathered, gain, bias)
+
+
 def result_shape(plan):
     return (TICKS, plan.height, plan.width, plan.images, plan.channels)
 
@@ -345,7 +360,7 @@
     is_first = jnp.broadcast_to((lax.axis_index("section") == 0).astype(jnp.float32), (1, LANES))
     order = (1, 2, 0, 3)
     maps = jnp.transpose(pending_section_entries[0], order)
-    stored, packed, early = opening_layer(plan, maps, first_kernel, second_kernel, CLOSING_AHEAD)
+    stored, packed, early = opening_layer(plan, maps, first_kernel, second_kernel, FIRST_AHEAD)
     earlier = None
     for tick in range(TICKS):
         gathered = exchange(plan, packed)
@@ -361,7 +376,7 @@
         if last:
             break
         moved = from_behind(stored, "section")
-        terms = jnp.concatenate(join(plan, exchange(plan, packed), gain[1], bias[1]), axis=0)
+        terms = joined(plan, exchange(plan, packed), gain[1], bias[1])
         earlier = (stored, terms)
         terms = from_behind(terms, "section")
         arriving = jnp.transpose(arriving_microsets[tick], order)

time: 101 us -> 99 us (0.980)
  blocking collectives: 62 us -> 78.4 us
  waiting for transfers between devices: 16.2 us -> 3.63 us
  starting transfers between devices: 5.35 us -> 0.63 us
    all_to_all x3 -> x4, blocking collectives: 62 us -> 78.4 us  [exchange(): return lax.all_to_all(copies, 'replica', 0, 0).astype(jnp.float32)]
    all_to_all x1 -> x0, waiting for transfers between devices: 12 us -> none  [exchange(): return lax.all_to_all(copies, 'replica', 0, 0).astype(jnp.float32)]
    all_to_all x1 -> x0, starting transfers between devices: 5.32 us -> none  [exchange(): return lax.all_to_all(copies, 'replica', 0, 0).astype(jnp.float32)]
  transfers between devices with their start and end apart: 3 -> 2, of which waited for: 2 -> 1; matrix products, arithmetic and copies ran while one was open for 0% -> 0% of each run, Pallas kernels for 0% -> 0%
where the time goes in v10:
time: 99 us; the launch traced here: 98.7 us
  blocking collectives  78.4 us (79%)
  Pallas kernels  15.6 us (16%)
  waiting for transfers between devices  3.63 us (4%)
    all_to_all x4, blocking collectives, exchange(): return lax.all_to_all(copies, 'replica', 0, 0).astype(jnp.float32)  78.4 us
    pallas_call x3, Pallas kernels, conv_layer(): pl.pallas_call(run, in_specs=[WHOLE] * (len(operands) + 1) + [OUTSIDE] *...  9.72 us
    pallas_call x1, Pallas kernels, opening_layer(): pl.pallas_call(run, in_specs=[OUTSIDE] * 3, out_specs=[WHOLE] * 3, out_sh...  4.52 us
    ppermute x2, waiting for transfers between devices, from_behind(): lax.ppermute(value, axis, [(i, (i + 1) % length) for i in range(length)])  3.63 us
  transfers between devices with their start and end apart: 2, of which 1 were waited for; matrix products, arithmetic and copies ran while one was open for 0% of the time, Pallas kernels for 0%

profile of v10, /device:TPU:8, one launch (start us, length us, event | category | flops | bytes accessed | tf_op | source)
XLA Modules:
  0.0 98.7 jit_solution(2601929938366412032)
XLA Ops:
  0.0 0.0 copy-start.1
  0.0 0.0 copy-start.2
  0.0 4.5 %shard_map.64 = (bf16[448,512]{1,0:T(8,128)(2,1)S(1)}, f32[8,128]{1,0:T(8,128)S(1)}, bf16[2560,512]{1,0:T(8,128)(2,1)S(1)}) custom-call(bf16[14,14,2,512]{3,2,1,0:T(2,128)(2,1)} %bitcast.31, bf16[3,3,512,512]{3,2,1,0:T(8,128)(2,1)} %bitcast.28, bf16[3,3,512,512]{3,2,1,0:T(8,128)(2,1)} %bitcast.24), custom_call_target="tpu_custom_call" | custom-call | tf_op jit(solution)/shard_map/pallas_call | solution.py:276
  4.6 28.3 %all_to_all.20 = f16[64,8,128]{2,1,0:T(8,128)(2,1)S(1)} all-to-all(f16[64,8,128]{2,1,0:T(8,128)(2,1)S(1)} %broadcast_in_dim.18), channel_id=1, replica_groups=mesh['section'=8,'replica'=64] {'replica'}, dimensions={0} | all-to-all | bytes 262144 | tf_op jit(solution)/shard_map/all_to_all | solution.py:83
  32.9 0.0 copy-done.1
  32.9 0.0 copy-done.2
  32.9 0.0 copy-start
  32.9 3.1 %shard_map.65 = (bf16[448,512]{1,0:T(8,128)(2,1)S(1)}, f32[8,128]{1,0:T(8,128)S(1)}, bf16[1792,512]{1,0:T(8,128)(2,1)S(1)}) custom-call(bf16[448,512]{1,0:T(8,128)(2,1)S(1)} %get-tuple-element.20.refs_0_, f32[64,8,128]{2,1,0:T(8,128)S(1)} %convert_element_type.28.refs_1_, f32[4,128]{1,0:T(4,128)S(1)} %bitcast.22, f32[4,128]{1,0:T(4,128)S(1)} %bitcast.20, ...), custom_call_target="tpu_custom_call" | custom-call | tf_op jit(solution)/shard_map/pallas_call | solution.py:188
  36.0 0.0 collective-permute-start
  36.1 17.2 %all_to_all.21 = f16[64,8,128]{2,1,0:T(8,128)(2,1)S(1)} all-to-all(f16[64,8,128]{2,1,0:T(8,128)(2,1)S(1)} %broadcast_in_dim.19), channel_id=1, replica_groups=mesh['section'=8,'replica'=64] {'replica'}, dimensions={0} | all-to-all | bytes 262144 | tf_op jit(solution)/shard_map/all_to_all | solution.py:83
  53.3 0.2 shard_map.66.refs_7_
  53.4 0.6 collective-permute-start.1
  54.0 3.6 %collective-permute-done.1.refs_1_ = f32[8,128]{1,0:T(8,128)S(1)} collective-permute-done((f32[8,128]{1,0:T(8,128)S(1)}, f32[8,128]{1,0:T(8,128)S(1)}, u32[]{:S(2)}, u32[]{:S(2)}) %collective-permute-start.1) | collective-permute-done | bytes 4128 | tf_op jit(solution)/shard_map/ppermute | solution.py:345
  57.7 0.0 collective-permute-done.refs_0_
  57.7 0.0 copy-done
  57.7 3.2 %shard_map.67 = (bf16[448,512]{1,0:T(8,128)(2,1)S(1)}, f32[8,128]{1,0:T(8,128)S(1)}, bf16[2048,512]{1,0:T(8,128)(2,1)S(1)}) custom-call(bf16[448,512]{1,0:T(8,128)(2,1)S(1)} %collective-permute-done.refs_0_, f32[8,128]{1,0:T(8,128)S(1)} %collective-permute-done.1.refs_1_, bf16[14,14,2,512]{3,2,1,0:T(2,128)(2,1)S(1)} %bitcast.15, ...), custom_call_target="tpu_custom_call" | custom-call | tf_op jit(solution)/shard_map/pallas_call | solution.py:188
  60.9 16.5 %all_to_all.22 = f16[64,8,128]{2,1,0:T(8,128)(2,1)S(1)} all-to-all(f16[64,8,128]{2,1,0:T(8,128)(2,1)S(1)} %broadcast_in_dim.21), channel_id=1, replica_groups=mesh['section'=8,'replica'=64] {'replica'}, dimensions={0} | all-to-all | bytes 262144 | tf_op jit(solution)/shard_map/all_to_all | solution.py:83
  77.4 3.4 %shard_map.68 = (bf16[448,512]{1,0:T(8,128)(2,1)S(1)}, f32[8,128]{1,0:T(8,128)S(1)}, bf16[2,14,14,2,512]{4,3,2,1,0:T(2,128)(2,1)}) custom-call(bf16[448,512]{1,0:T(8,128)(2,1)S(1)} %get-tuple-element.29.refs_0_, f32[64,8,128]{2,1,0:T(8,128)S(1)} %convert_element_type.33.refs_1_, f32[4,128]{1,0:T(4,128)S(1)} %bitcast.23, f32[4,128]{1,0:T(4,128)S(1)} %bitcast.21, ...), custom_call_target="tpu_custom_call" | custom-call | tf_op jit(solution)/shard_map/pallas_call | solution.py:188
  80.9 16.6 %all_to_all.23 = f16[64,8,128]{2,1,0:T(8,128)(2,1)S(1)} all-to-all(f16[64,8,128]{2,1,0:T(8,128)(2,1)S(1)} %broadcast_in_dim.22), channel_id=1, replica_groups=mesh['section'=8,'replica'=64] {'replica'}, dimensions={0} | all-to-all | bytes 262144 | tf_op jit(solution)/shard_map/all_to_all | solution.py:83
  97.5 1.2 %shard_map.69 = bf16[2,14,14,2,512]{4,3,2,1,0:T(2,128)(2,1)} custom-call(bf16[448,512]{1,0:T(8,128)(2,1)S(1)} %get-tuple-element.32.stored_ref, f32[64,8,128]{2,1,0:T(8,128)S(1)} %convert_element_type.35.gathered_ref, f32[4,128]{1,0:T(4,128)S(1)} %bitcast.19, f32[4,128]{1,0:T(4,128)S(1)} %bitcast.17, ...), custom_call_target="tpu_custom_call", output_to_operand_aliasing={{}: (4, {})} | custom-call | tf_op jit(solution)/shard_map/pallas_call | solution.py:332
  (14 shorter events, 0.2 us)
Async XLA Ops:
  0.0 32.9 %copy-start.1 = (f32[1,2,512]{2,1,0:T(2,128)S(1)}, f32[1,2,512]{2,1,0:T(2,128)}, u32[]{:S(2)}) copy-start(f32[1,2,512]{2,1,0:T(2,128)} %param.11) | copy-start | bytes 12292
  0.0 32.9 %copy-start.2 = (f32[1,2,512]{2,1,0:T(2,128)S(1)}, f32[1,2,512]{2,1,0:T(2,128)}, u32[]{:S(2)}) copy-start(f32[1,2,512]{2,1,0:T(2,128)} %param.10) | copy-start | bytes 12292
  32.9 24.7 %copy-start = (bf16[1,2,14,14,512]{4,1,3,2,0:T(2,128)(2,1)S(1)}, bf16[1,2,14,14,512]{4,1,3,2,0:T(2,128)(2,1)}, u32[]{:S(2)}) copy-start(bf16[1,2,14,14,512]{4,1,3,2,0:T(2,128)(2,1)} %param.7) | copy-start | bytes 1204228
  36.0 21.6 %collective-permute-start = (bf16[448,512]{1,0:T(8,128)(2,1)S(1)}, bf16[448,512]{1,0:T(8,128)(2,1)S(1)}, u32[]{:S(2)}, u32[]{:S(2)}) collective-permute-start(bf16[448,512]{1,0:T(8,128)(2,1)S(1)} %get-tuple-element.26.refs_6_), channel_id=1, source_target_pairs={{0,64},{64,128},{128,192},{192,256},{256,320},{320,384},{384,448},... | collective-permute-start | bytes 1376264 | tf_op jit(solution)/shard_map/ppermute | solution.py:345
  53.4 4.2 %collective-permute-start.1 = (f32[8,128]{1,0:T(8,128)S(1)}, f32[8,128]{1,0:T(8,128)S(1)}, u32[]{:S(2)}, u32[]{:S(2)}) collective-permute-start(f32[8,128]{1,0:T(8,128)S(1)} %shard_map.66.refs_7_), channel_id=1, source_target_pairs={{0,64},{64,128},{128,192},{192,256},{256,320},{320,384},{384,448},... | collective-permute-start | bytes 12296 | tf_op jit(solution)/shard_map/ppermute | solution.py:345
